TPU v7x, 256 devices: a whole 4x4x8 slice. The times are simulated.
256 devices in a mesh: grp: 2 (over x_hi), ep: 64 (over x_lo, y, z), dp: 2 (over core).
Axes of the slice: x: 4 (x_hi: 2, x_lo: 2; x = x_hi * 2 + x_lo), y: 4, z: 8, core: 2. Of those that a mesh axis runs over, the one named last changes fastest.
Arguments:
- rows_in: bfloat16 [2, 2048, 4096], P('grp', ('ep', 'dp')), may hold values from -6 to 6
- cotangent: bfloat16 [2048, 4096], P(('ep', 'dp')), may hold values from -6 to 6
- lengths: int32 [4], replicated, may hold values from 1 to 1024, 2048 in all
- train_experts: int32 [2048, 8], P(('ep', 'dp')), may hold values from 0 to 63, all different within a row; in each aligned block of 16 rows (0 to 15, 16 to 31, ...) at most 2 rows name the same one
- train_gates: float32 [2048, 8], P(('ep', 'dp')), may hold values from 0.02 to 0.3
- decode_experts: int32 [2, 2048, 8], P(None, ('ep', 'dp')), may hold values from 0 to 63, all different within a row; in each aligned block of 16 rows (0 to 15, 16 to 31, ..., all dimensions but the last counted through in order) at most 2 rows name the same one
- decode_gates: float32 [2, 2048, 8], P(None, ('ep', 'dp')), may hold values from 0.02 to 0.3
- gate_up: bfloat16 [2, 64, 4096, 2, 768], P('grp', 'ep', None, None, 'dp'), may hold values from -0.09375 to 0.09375
- down: bfloat16 [2, 64, 768, 4096], P('grp', 'ep', 'dp'), may hold values from -0.21875 to 0.21875
Outputs:
- result: bfloat16 [2, 2048, 4096], P('grp', ('ep', 'dp'))
Inputs may be any that keep to these rules, and one draw needn't show every extreme that they name: `train_experts`: in every aligned block of 16 rows (the rows of one device), the 8 ids of a row differ and no id is named by more than 2 rows of the block; some block reaches 2. `decode_experts`: for each step, in every aligned block of 16 rows (the rows of one device), the 8 ids of a row differ and no id is named by more than 2 rows of the block; some block reaches 2. The lengths sum to 2048 and the longest is exactly 1024.
All inputs are finite; a program needn't handle non-finite values.
Results may differ from a plain program's by a relative error of at most 0.008.
Values may be sent and summed in bfloat16 or wider, within the bound.
A program may use at most 192 MiB of HBM per device.

v0:
```python
import jax
import jax.numpy as jnp
from jax import lax
from jax.sharding import PartitionSpec as P

EPSILON = 1e-06


def passed_along(block, axis, distance):
    devices = range(lax.axis_size(axis))
    route = [(i - distance, i) for i in devices if i - distance in devices]
    return lax.ppermute(block, axis, route)


def routing_tables(expert_ids, gate_values, capacity, expert_count):
    row_count, top_count = expert_ids.shape
    flat_ids = expert_ids.reshape(row_count * top_count)
    onehot = (flat_ids[:, None] == jnp.arange(expert_count, dtype=jnp.int32)[None, :]).astype(
        jnp.int32
    )
    earlier = jnp.cumsum(onehot, axis=0) - onehot
    ranks = jnp.sum(earlier * onehot, axis=1)
    slots = flat_ids * capacity + ranks
    hits = (slots[:, None] == jnp.arange(expert_count * capacity, dtype=jnp.int32)[None, :]).astype(
        jnp.float32
    )
    hits = hits.reshape(row_count, top_count, expert_count * capacity)
    picker = jnp.sum(hits, axis=1)
    weigher = jnp.sum(hits * gate_values[:, :, None], axis=1)
    return (picker, weigher)


def replica_sum(per_replica):
    total = jnp.zeros(per_replica.shape[1:], jnp.float32)
    for replica in range(per_replica.shape[0]):
        total = total + lax.optimization_barrier(per_replica[replica].astype(jnp.bfloat16)).astype(
            jnp.float32
        )
    return total


def renew(weights, grads, axis_number, rate):
    scale = jnp.sqrt(jnp.mean(grads * grads, axis=axis_number, keepdims=True) + EPSILON)
    return (weights.astype(jnp.float32) - rate * grads / scale).astype(jnp.bfloat16)


def forward_core(rows_four, weights_gu, weights_dn, part_count):
    ep_count, rep_count, capacity, model_width = rows_four.shape
    hidden_count = weights_gu.shape[2]
    slot_count = ep_count * rep_count * capacity
    both = jnp.dot(
        rows_four.reshape(slot_count, model_width),
        weights_gu.reshape(model_width, 2 * hidden_count),
        preferred_element_type=jnp.float32,
    ).reshape(slot_count, 2, hidden_count)
    active = both[:, 0]
    upward = both[:, 1]
    hidden = (active * jax.nn.sigmoid(active) * upward).astype(jnp.bfloat16)
    piece = jnp.dot(hidden, weights_dn, preferred_element_type=jnp.float32)
    pieces = piece.astype(jnp.bfloat16).reshape(ep_count, rep_count, 1, capacity, model_width)
    return pieces.reshape(ep_count, rep_count * part_count, capacity, model_width)


def learn_core(rows_four, grads_four, weights_gu, weights_dn, part_count):
    ep_count, rep_count, capacity, model_width = rows_four.shape
    hidden_count = weights_gu.shape[2]
    slot_count = ep_count * rep_count * capacity
    flat_grads = grads_four.reshape(slot_count, model_width)
    both = jnp.dot(
        rows_four.reshape(slot_count, model_width),
        weights_gu.reshape(model_width, 2 * hidden_count),
        preferred_element_type=jnp.float32,
    ).reshape(slot_count, 2, hidden_count)
    active = both[:, 0]
    upward = both[:, 1]
    sigma = jax.nn.sigmoid(active)
    swish = active * sigma
    hidden = (swish * upward).astype(jnp.bfloat16)
    back = lax.dot_general(
        flat_grads, weights_dn, (((1,), (1,)), ((), ())), preferred_element_type=jnp.float32
    )
    d_active = back * upward * sigma * (1.0 + active * (1.0 - sigma))
    d_upward = back * swish
    d_both = jnp.stack([d_active, d_upward], axis=1).astype(jnp.bfloat16)
    grad_dn = jnp.einsum(
        "epch,epcd->phd",
        hidden.reshape(ep_count, rep_count, capacity, hidden_count),
        grads_four,
        preferred_element_type=jnp.float32,
    )
    grad_gu = jnp.einsum(
        "epcd,epcgh->pdgh",
        rows_four,
        d_both.reshape(ep_count, rep_count, capacity, 2, hidden_count),
        preferred_element_type=jnp.float32,
    )
    piece = jnp.einsum("mgh,dgh->md", d_both, weights_gu, preferred_element_type=jnp.float32)
    pieces = piece.astype(jnp.bfloat16).reshape(ep_count, rep_count, 1, capacity, model_width)
    ahead = jnp.dot(hidden, weights_dn, preferred_element_type=jnp.float32)
    forward_pieces = ahead.astype(jnp.bfloat16).reshape(
        ep_count, rep_count, 1, capacity, model_width
    )
    slot_dx = pieces.reshape(ep_count, rep_count * part_count, capacity, model_width)
    slot_fw = forward_pieces.reshape(ep_count, rep_count * part_count, capacity, model_width)
    return (grad_gu, grad_dn, slot_dx, slot_fw)


def per_device(
    rows_in,
    cotangent,
    lengths,
    train_experts,
    train_gates,
    decode_experts,
    decode_gates,
    gate_up,
    down,
):
    ep_count = lax.axis_size("ep")
    dp_count = lax.axis_size("dp")
    row_count, model_width = cotangent.shape
    top_count = train_experts.shape[1]
    capacity = min(row_count, max(2, 4 * row_count * top_count // (3 * ep_count)))
    is_learner = lax.axis_index("grp") == 0
    own_gu = gate_up[0, 0]
    own_dn = down[0, 0]
    hidden_all = own_gu.shape[2] * dp_count

    def spread(stacked):
        arrived = lax.all_to_all(stacked, "ep", split_axis=1, concat_axis=1, tiled=True)
        return lax.all_gather(arrived, "dp", axis=2)

    def weights_for(weights_gu, weights_dn):
        return (weights_gu, weights_dn, 1)

    def bring_back(slot_out):
        mine = lax.axis_index("dp")
        keep = lax.dynamic_index_in_dim(slot_out, mine, axis=1, keepdims=False)
        give = lax.dynamic_index_in_dim(slot_out, 1 - mine, axis=1, keepdims=False)
        got = lax.ppermute(give, "dp", [(0, 1), (1, 0)])
        summed = (keep.astype(jnp.float32) + got.astype(jnp.float32)).astype(jnp.bfloat16)
        return lax.all_to_all(summed, "ep", split_axis=0, concat_axis=0, tiled=True)

    def combine(mixing, returned):
        total = returned.astype(jnp.float32).reshape(ep_count * capacity, model_width)
        return jnp.einsum("rs,sd->rd", mixing, total, precision=lax.Precision.HIGHEST)

    def dispatch(picker, values):
        buffer = jnp.einsum(
            "rs,rd->sd", picker.astype(jnp.bfloat16), values, preferred_element_type=jnp.float32
        )
        return buffer.astype(jnp.bfloat16)

    tokens = rows_in[0]
    total_rows = row_count * ep_count * dp_count
    longest = 2 * total_rows // lengths.shape[0]
    first_row = (lax.axis_index("ep") * dp_count + lax.axis_index("dp")) * row_count
    places = first_row + jnp.arange(row_count, dtype=jnp.int32)
    ends = jnp.cumsum(lengths)
    starts = ends - lengths
    inside = (places[:, None] >= starts[None, :]) & (places[:, None] < ends[None, :])
    seq_len = jnp.sum(jnp.where(inside, lengths[None, :], 0), axis=1).astype(jnp.float32)
    weight = 2.0 * longest / (seq_len + longest)
    route_ids = jnp.where(is_learner, train_experts, decode_experts[0])
    route_gates = jnp.where(is_learner, train_gates, decode_gates[0])
    picker, weigher = routing_tables(route_ids, route_gates, capacity, ep_count)
    row_buffer = dispatch(picker, tokens)
    cot_wide = cotangent.astype(jnp.float32)
    grad_buffer = jnp.einsum(
        "rs,rd->sd", weigher * weight[:, None], cot_wide, precision=lax.Precision.HIGHEST
    ).astype(jnp.bfloat16)
    stacked = jnp.stack([row_buffer, grad_buffer], axis=0).reshape(
        2, ep_count, capacity, model_width
    )
    arrived = spread(stacked)
    use_gu, use_dn, part_count = weights_for(own_gu, own_dn)
    per_gu, per_dn, slot_dx, slot_fw = learn_core(
        arrived[0], arrived[1], use_gu, use_dn, part_count
    )
    grad_gu = replica_sum(per_gu)
    grad_dn = replica_sum(per_dn)
    returned = bring_back(jnp.where(is_learner, slot_dx, slot_fw))
    mixing = jnp.where(is_learner, picker, weigher)
    base = jnp.where(is_learner, weight[:, None] * cot_wide, tokens.astype(jnp.float32))
    carried = (base + combine(mixing, returned)).astype(jnp.bfloat16)
    sent_gu = renew(own_gu, grad_gu, 0, 0.5 / model_width**0.5)
    sent_dn = renew(own_dn, grad_dn, 1, 0.5 / hidden_all**0.5)
    fresh_gu, fresh_dn = sent_gu, sent_dn
    current = passed_along(carried, "grp", -1)
    picker, weigher = routing_tables(decode_experts[1], decode_gates[1], capacity, ep_count)
    stacked = dispatch(picker, current).reshape(1, ep_count, capacity, model_width)
    arrived = spread(stacked)
    use_gu, use_dn, part_count = weights_for(fresh_gu, fresh_dn)
    slot_out = forward_core(arrived[0], use_gu, use_dn, part_count)
    returned = bring_back(slot_out)
    current = (current.astype(jnp.float32) + combine(weigher, returned)).astype(jnp.bfloat16)
    final_rows = jnp.where(is_learner, carried, passed_along(current, "grp", 1))
    return final_rows[None]


def solution(mesh):
    placed = (
        P("grp", ("ep", "dp"), None),
        P(("ep", "dp"), None),
        P(),
        P(("ep", "dp"), None),
        P(("ep", "dp"), None),
        P(None, ("ep", "dp"), None),
        P(None, ("ep", "dp"), None),
        P("grp", "ep", None, None, "dp"),
        P("grp", "ep", "dp", None),
    )
    return jax.shard_map(
        per_device,
        mesh=mesh,
        in_specs=placed,
        out_specs=P("grp", ("ep", "dp"), None),
        check_vma=False,
    )
```

profile of v0, /device:TPU:4, one launch (start us, length us, event | category | flops | bytes accessed | tf_op | source)
XLA Modules:
  0.0 338.0 jit_solution(17910174214038131874)
XLA Ops:
  6.5 0.7 slice.52
  8.0 0.7 bitcast_add_fusion
  9.6 0.7 bitcast_select_fusion
  10.4 0.8 reduce-window.8
  11.2 0.7 bitcast_subtract_fusion
  11.9 0.7 select_reduce_fusion.4
  12.8 2.0 convolution_convert_fusion.3
  14.8 0.7 stack.28
  15.5 0.5 convolution_convert_fusion.4
  15.9 0.7 stack.27
  16.7 2.7 pad_maximum_fusion
  19.4 64.1 %all_to_all.20 = bf16[2,64,2,4096]{3,2,0,1:T(2,128)(2,1)S(1)} all-to-all(bf16[2,64,2,4096]{3,2,0,1:T(2,128)(2,1)S(1)} %pad_maximum_fusion), channel_id=1, replica_groups=mesh['grp'=2,'ep'=64,'dp'=2] {'ep'}, dimensions={1} | all-to-all | bytes 4194304 | tf_op jit(solution)/shard_map/all_to_all | solution.py:130
  83.5 2.6 copy.98
  86.1 6.5 %copy.119 = bf16[512,8,2,384]{3,1,2,0:T(8,128)(2,1)} copy(bf16[512,8,2,384]{3,2,1,0:T(2,128)(2,1)} %bitcast.148) | data formatting | bytes 12582912
  92.7 9.1 %copy.101 = bf16[768,4096]{1,0:T(8,128)(2,1)} copy(bf16[768,4096]{0,1:T(8,128)(2,1)} %bitcast.147) | data formatting | bytes 12582912 | tf_op jit(solution)/shard_map/dot_general | solution.py:69
  102.4 3.9 %fusion.58 = (bf16[1,64,4,4096]{3,1,0,2:T(8,128)(2,1)S(1)}, bf16[1,64,4,4096]{3,1,0,2:T(8,128)(2,1)}) fusion(bf16[2,64,4,4096]{3,1,0,2:T(8,128)(2,1)} %all-gather.5.cloned.1.call-done), kind=kLoop, calls=%fused_computation.106 | loop fusion | bytes 8388608 | tf_op jit(solution)/shard_map/slice | solution.py:178
  106.3 3.0 copy.100
  109.3 4.0 %reshape.151 = bf16[256,4096,1]{1,0,2:T(8,128)(2,1)} reshape(bf16[1,64,4,4096]{3,2,1,0:T(4,128)(2,1)} %copy.100) | data formatting | bytes 4194304 | tf_op jit(solution)/shard_map/reshape;squeeze | solution.py:70
  113.3 4.5 %copy.99 = bf16[1,64,4,4096]{3,2,1,0:T(4,128)(2,1)} copy(bf16[1,64,4,4096]{3,1,0,2:T(8,128)(2,1)} %get-tuple-element.14) | data formatting | bytes 4194304 | tf_op jit(solution)/shard_map/slice | solution.py:178
  117.8 4.1 %reshape_squeeze.13 = bf16[256,4096]{1,0:T(8,128)(2,1)} reshape(bf16[1,64,4,4096]{3,2,1,0:T(4,128)(2,1)} %copy.99) | data formatting | bytes 4194304 | tf_op jit(solution)/shard_map/reshape;squeeze | solution.py:68
  122.0 5.4 %fusion.60 = f32[256,2,384]{2,0,1:T(8,128)S(1)} fusion(bf16[256,4096,1]{1,0,2:T(8,128)(2,1)} %reshape.151, bf16[2,384,4096]{2,1,0:T(8,128)(2,1)} %bitcast.151), kind=kOutput, calls=%fused_computation.108 | convolution fusion | flops 1610612736 | bytes 9175040 | tf_op jit(solution)/shard_map/dot_general | solution.py:69
  127.4 2.0 fusion.31
  129.4 0.7 copy-done.14
  130.2 1.0 stack.34
  131.2 5.0 %fusion.8 = bf16[256,4096]{1,0:T(8,128)(2,1)S(1)} fusion(bf16[1,1,4096,2,384]{4,3,2,1,0:T(2,128)(2,1)} %param.16, bf16[256,1,384]{2,0,1:T(8,128)(2,1)} %bitcast.155, bf16[256,1,384]{2,0,1:T(8,128)(2,1)} %bitcast.154), kind=kOutput, calls=%fused_computation.18 | convolution fusion | flops 1611857920 | bytes 8781824 | tf_op jit(solution)/shard_map/mgh,dgh->md/dot_general | solution.py:97
  136.2 2.6 fusion.11
  138.8 4.4 %select_n.70 = bf16[64,2,2,4096]{3,2,1,0:T(2,128)(2,1)} reshape(bf16[256,4096]{1,0:T(8,128)(2,1)} %fusion.11) | data formatting | bytes 4194304 | tf_op jit(solution)/shard_map/jit(_where)/select_n | solution.py:182
  143.2 2.1 dynamic-slice_bitcast_fusion.1
  145.7 6.4 %bitcast_convert_fusion = bf16[2,4096,2,384]{3,1,2,0:T(8,128)(2,1)} fusion(bf16[64,2,2,4096,1]{3,0,2,4,1:T(8,128)(2,1)S(1)} %bitcast.149, bf16[64,2,2,1,384]{4,0,2,3,1:T(8,128)(2,1)S(1)} %copy.111, bf16[64,2,2,1,384]{4,0,2,3,1:T(8,128)(2,1)S(1)} %copy.110), kind=kOutput, calls=%fused_computation | convolution fusion | flops 1617690624 | bytes 15073280 | tf_op jit(solution)/shard_map/epcd,epcgh->pdgh/dot_general | solution.py:91
  152.1 2.8 fusion.17
  154.9 11.3 %all-to-all-start.1 = ((bf16[64,2,4096]{2,1,0:T(2,128)(2,1)}), bf16[64,2,4096]{2,1,0:T(2,128)(2,1)S(1)}, u32[]{:S(2)}, u32[]{:S(2)}) async-start(bf16[64,2,4096]{2,1,0:T(2,128)(2,1)} %fusion.17), calls=%async_computation.1 | async-start | bytes 2097152 | tf_op jit(solution)/shard_map/all_to_all | solution.py:142
  166.2 6.0 %slice_bitcast_fusion.1 = (bf16[4096,2,384]{2,0,1:T(8,128)(2,1)S(1)}, bf16[4096,2,384]{2,0,1:T(8,128)(2,1)S(1)}) fusion(bf16[2,4096,2,384]{3,1,2,0:T(8,128)(2,1)} %bitcast_convert_fusion), kind=kLoop, calls=%fused_computation.6 | loop fusion | bytes 25165824 | tf_op jit(solution)/shard_map/convert_element_type | solution.py:36
  172.3 2.6 copy-done
  174.8 1.9 copy-done.1
  176.8 2.0 multiply_reduce_fusion
  178.8 17.0 %all-to-all-done.1 = bf16[64,2,4096]{2,1,0:T(2,128)(2,1)S(1)} async-done(((bf16[64,2,4096]{2,1,0:T(2,128)(2,1)}), bf16[64,2,4096]{2,1,0:T(2,128)(2,1)S(1)}, u32[]{:S(2)}, u32[]{:S(2)}) %all-to-all-start.1) | async-done | bytes 1048608 | tf_op jit(solution)/shard_map/all_to_all | solution.py:142
  196.3 0.5 fusion.12
  196.8 2.8 collective-permute-start.1
  199.9 1.0 squeeze.62
  200.8 1.2 collective-permute-done.1
  202.1 0.5 convolution_convert_fusion.2
  202.5 1.5 reshape.137
  204.0 6.1 %all-to-all-start.2 = ((bf16[1,64,2,4096]{3,2,0,1:T(2,128)(2,1)}), bf16[1,64,2,4096]{3,2,0,1:T(2,128)(2,1)S(1)}, u32[]{:S(2)}, u32[]{:S(2)}) async-start(bf16[1,64,2,4096]{3,2,0,1:T(2,128)(2,1)} %bitcast.21), calls=%async_computation.2 | async-start | bytes 2097152 | tf_op jit(solution)/shard_map/all_to_all | solution.py:130
  210.5 10.9 %subtract_convert_fusion = bf16[4096,2,384]{2,0,1:T(8,128)(2,1)} fusion(bf16[4096,2,384]{2,0,1:T(8,128)(2,1)} %copy-done.1, bf16[4096,2,384]{2,0,1:T(8,128)(2,1)} %copy-done, f32[2,384]{1,0:T(2,128)S(1)} %add_sqrt_fusion, bf16[1,1,4096,2,384]{4,3,2,1,0:T(2,128)(2,1)} %param.16), kind=kLoop, calls=%fused_computation.2 | loop fusion | flops 25165824 | bytes 25168896 | tf_op jit(solution)/shard_map/convert_element_type | solution.py:44
  221.4 16.6 %all-to-all-done.2 = bf16[1,64,2,4096]{3,2,0,1:T(2,128)(2,1)S(1)} async-done(((bf16[1,64,2,4096]{3,2,0,1:T(2,128)(2,1)}), bf16[1,64,2,4096]{3,2,0,1:T(2,128)(2,1)S(1)}, u32[]{:S(2)}, u32[]{:S(2)}) %all-to-all-start.2) | async-done | bytes 1048608 | tf_op jit(solution)/shard_map/all_to_all | solution.py:130
  238.0 1.6 copy.108
  239.7 5.4 %bitcast_convert_fusion.1 = bf16[2,384,4096]{2,1,0:T(8,128)(2,1)} fusion(bf16[64,2,2,4096]{3,0,2,1:T(8,128)(2,1)S(1)} %bitcast.150, f32[64,2,2,384]{3,2,1,0:T(2,128)} %squeeze.62, f32[64,2,2,384]{3,2,1,0:T(2,128)S(1)} %squeeze.61), kind=kOutput, calls=%fused_computation.1 | convolution fusion | flops 809041920 | bytes 9175040 | tf_op jit(solution)/shard_map/epch,epcd->phd/dot_general | solution.py:85
  245.1 8.6 %copy.112 = bf16[4096,2,384]{0,2,1:T(8,128)(2,1)} copy(bf16[4096,2,384]{2,0,1:T(8,128)(2,1)} %subtract_convert_fusion) | data formatting | bytes 12582912 | tf_op jit(solution)/shard_map/convert_element_type | solution.py:44
  253.7 3.3 slice_bitcast_fusion.3
  257.0 1.1 multiply_reduce_fusion.1
  258.1 0.5 copy-done.3
  258.6 4.6 %copy.109 = bf16[1,64,4,4096]{3,2,1,0:T(4,128)(2,1)} copy(bf16[1,64,4,4096]{3,1,0,2:T(8,128)(2,1)} %all-gather.7.cloned.1.call-done) | data formatting | bytes 4194304 | tf_op jit(solution)/shard_map/all_gather | solution.py:131
  263.2 4.0 %reshape.155 = bf16[256,4096,1]{1,0,2:T(8,128)(2,1)} reshape(bf16[1,64,4,4096]{3,2,1,0:T(4,128)(2,1)} %copy.109) | data formatting | bytes 4194304 | tf_op jit(solution)/shard_map/reshape;squeeze | solution.py:52
  267.2 5.4 %fusion = f32[256,2,384]{2,0,1:T(8,128)S(1)} fusion(bf16[256,4096,1]{1,0,2:T(8,128)(2,1)} %reshape.155, bf16[4096,2,384]{0,2,1:T(8,128)(2,1)} %copy.112), kind=kOutput, calls=%fused_computation.7 | convolution fusion | flops 1610612736 | bytes 9175040 | tf_op jit(solution)/shard_map/dot_general | solution.py:51
  272.6 3.5 %convolution_convert_fusion = bf16[256,4096]{1,0:T(8,128)(2,1)} fusion(bf16[384,4096]{1,0:T(8,128)(2,1)S(1)} %copy-done.4, bf16[384,4096]{1,0:T(8,128)(2,1)S(1)} %get-tuple-element.11, bf16[1,1,384,4096]{3,2,1,0:T(8,128)(2,1)S(1)} %copy-done.18, f32[384]{0:T(512)S(1)} %add_sqrt_fusion.1, f32[256,2,384]{2,0,1:T(8,128)S(1)} %fusion), kind=kOutput, calls=%fused_computation.16 | convolution fusion | flops 819527680 | bytes 12322304 | tf_op jit(solution)/shard_map/dot_general | solution.py:59
  276.1 3.5 %reshape_reshape.2 = bf16[64,2,2,4096]{3,2,1,0:T(2,128)(2,1)S(1)} reshape(bf16[256,4096]{1,0:T(8,128)(2,1)} %convolution_convert_fusion) | data formatting | bytes 4194304 | tf_op jit(solution)/shard_map/reshape;reshape | solution.py:61
  279.6 0.9 dynamic-slice_bitcast_fusion
  280.6 2.6 collective-permute-done.2
  283.2 1.8 fusion.16
  285.1 35.6 %all_to_all.21 = bf16[64,2,4096]{2,1,0:T(2,128)(2,1)S(1)} all-to-all(bf16[64,2,4096]{2,1,0:T(2,128)(2,1)S(1)} %fusion.16), channel_id=1, replica_groups=mesh['grp'=2,'ep'=64,'dp'=2] {'ep'}, dimensions={0} | all-to-all | bytes 2097152 | tf_op jit(solution)/shard_map/all_to_all | solution.py:142
  321.1 0.5 add_convert_fusion
  321.7 1.3 collective-permute-start.3
  323.0 7.1 %collective-permute-done.3 = bf16[16,4096]{1,0:T(8,128)(2,1)S(1)} collective-permute-done((bf16[16,4096]{1,0:T(8,128)(2,1)S(1)}, bf16[16,4096]{1,0:T(8,128)(2,1)S(1)}, u32[]{:S(2)}, u32[]{:S(2)}) %collective-permute-start.3) | collective-permute-done | bytes 131104 | tf_op jit(solution)/shard_map/ppermute | solution.py:12
  330.0 0.7 select_bitcast_fusion
  (76 shorter events, 4.5 us)
Async XLA Ops:
  6.5 8.9 %copy-start.8 = (bf16[1,16,4096]{2,1,0:T(8,128)(2,1)S(1)}, bf16[1,16,4096]{2,1,0:T(8,128)(2,1)}, u32[]{:S(2)}) copy-start(bf16[1,16,4096]{2,1,0:T(8,128)(2,1)} %param.9) | copy-start | bytes 393220
  6.5 95.9 %all-gather.5.cloned.1.call-start = ((), (), s32[]{:S(2)}) async-start(), calls=%async_computation.4 | async-start | bytes 6291456 | tf_op jit(solution)/shard_map/all_gather | solution.py:131
  92.7 9.2 %copy-start.15 = (f32[2,16,8]{1,2,0:T(8,128)S(1)}, f32[2,16,8]{1,2,0:T(8,128)}, u32[]{:S(2)}) copy-start(f32[2,16,8]{1,2,0:T(8,128)} %param.15) | copy-start | bytes 3076
  121.9 5.4 %copy-start.6 = (bf16[256,4096]{1,0:T(8,128)(2,1)S(1)}, bf16[256,4096]{1,0:T(8,128)(2,1)}, u32[]{:S(2)}) copy-start(bf16[256,4096]{1,0:T(8,128)(2,1)} %reshape_squeeze.13) | copy-start | bytes 6291460
  122.0 5.4 %copy-start.16 = (bf16[1,1,384,4096]{3,2,1,0:T(8,128)(2,1)S(1)}, bf16[1,1,384,4096]{3,2,1,0:T(8,128)(2,1)}, u32[]{:S(2)}) copy-start(bf16[1,1,384,4096]{3,2,1,0:T(8,128)(2,1)} %param.17) | copy-start | bytes 9437188
  129.4 0.7 copy-start.14
  131.2 5.0 %copy-start.17 = (bf16[1,1,384,4096]{3,2,1,0:T(8,128)(2,1)S(1)}, bf16[1,1,384,4096]{3,2,1,0:T(8,128)(2,1)}, u32[]{:S(2)}) copy-start(bf16[1,1,384,4096]{3,2,1,0:T(8,128)(2,1)} %param.17) | copy-start | bytes 9437188
  145.3 6.8 %collective-permute-start = (bf16[64,2,4096]{2,1,0:T(2,128)(2,1)S(1)}, bf16[64,2,4096]{2,1,0:T(2,128)(2,1)S(1)}, u32[]{:S(2)}, u32[]{:S(2)}) collective-permute-start(bf16[64,2,4096]{2,1,0:T(2,128)(2,1)S(1)} %dynamic-slice_bitcast_fusion.1), channel_id=1, source_target_pairs={{0,1},{1,0},{2,3},{3,2},{4,5},{5,4},{6,7},{7,6},{8,9},{9,8},{10,11... | collective-permute-start | bytes 3145736 | tf_op jit(solution)/shard_map/ppermute | solution.py:140
  145.7 6.4 %copy-start.5 = (bf16[64,2,2,4096]{3,2,1,0:T(2,128)(2,1)S(1)}, bf16[64,2,2,4096]{3,2,1,0:T(2,128)(2,1)}, u32[]{:S(2)}) copy-start(bf16[64,2,2,4096]{3,2,1,0:T(2,128)(2,1)} %select_n.70) | copy-start | bytes 6291460
  154.9 40.9 %all-to-all-start.1 = ((bf16[64,2,4096]{2,1,0:T(2,128)(2,1)}), bf16[64,2,4096]{2,1,0:T(2,128)(2,1)S(1)}, u32[]{:S(2)}, u32[]{:S(2)}) async-start(bf16[64,2,4096]{2,1,0:T(2,128)(2,1)} %fusion.17), calls=%async_computation.1 | async-start | bytes 2097152 | tf_op jit(solution)/shard_map/all_to_all | solution.py:142
  172.3 2.6 copy-start
  172.3 4.5 %copy-start.1 = (bf16[4096,2,384]{2,0,1:T(8,128)(2,1)}, bf16[4096,2,384]{2,0,1:T(8,128)(2,1)S(1)}, u32[]{:S(2)}) copy-start(bf16[4096,2,384]{2,0,1:T(8,128)(2,1)S(1)} %get-tuple-element.10) | copy-start | bytes 18874372
  176.8 19.5 %copy-start.7 = (bf16[16,4096]{1,0:T(8,128)(2,1)S(1)}, bf16[16,4096]{1,0:T(8,128)(2,1)}, u32[]{:S(2)}) copy-start(bf16[16,4096]{1,0:T(8,128)(2,1)} %param.10) | copy-start | bytes 393220
  176.8 19.5 %copy-start.9 = (bf16[1,16,4096]{2,1,0:T(8,128)(2,1)S(1)}, bf16[1,16,4096]{2,1,0:T(8,128)(2,1)}, u32[]{:S(2)}) copy-start(bf16[1,16,4096]{2,1,0:T(8,128)(2,1)} %param.9) | copy-start | bytes 393220
  196.8 7.2 %copy-start.12 = (bf16[16,4096]{1,0:T(8,128)(2,1)}, bf16[16,4096]{1,0:T(8,128)(2,1)S(1)}, u32[]{:S(2)}) copy-start(bf16[16,4096]{1,0:T(8,128)(2,1)S(1)} %fusion.12) | copy-start | bytes 393220
  196.8 5.3 %collective-permute-start.1 = (bf16[16,4096]{1,0:T(8,128)(2,1)S(1)}, bf16[16,4096]{1,0:T(8,128)(2,1)S(1)}, u32[]{:S(2)}, u32[]{:S(2)}) collective-permute-start(bf16[16,4096]{1,0:T(8,128)(2,1)S(1)} %fusion.12), channel_id=1, source_target_pairs={{128,0},{129,1},{130,2},{131,3},{132,4},{133,5},{134,6},{135,7},{1... | collective-permute-start | bytes 393224 | tf_op jit(solution)/shard_map/ppermute | solution.py:12
  202.1 8.4 %copy-start.10 = (bf16[16,4096]{1,0:T(8,128)(2,1)}, bf16[16,4096]{1,0:T(8,128)(2,1)S(1)}, u32[]{:S(2)}) copy-start(bf16[16,4096]{1,0:T(8,128)(2,1)S(1)} %collective-permute-done.1) | copy-start | bytes 393220
  204.0 34.0 %all-to-all-start.2 = ((bf16[1,64,2,4096]{3,2,0,1:T(2,128)(2,1)}), bf16[1,64,2,4096]{3,2,0,1:T(2,128)(2,1)S(1)}, u32[]{:S(2)}, u32[]{:S(2)}) async-start(bf16[1,64,2,4096]{3,2,0,1:T(2,128)(2,1)} %bitcast.21), calls=%async_computation.2 | async-start | bytes 2097152 | tf_op jit(solution)/shard_map/all_to_all | solution.py:130
  210.2 48.5 %all-gather.7.cloned.1.call-start = ((), (), s32[]{:S(2)}) async-start(), calls=%async_computation.5 | async-start | bytes 3145728 | tf_op jit(solution)/shard_map/all_gather | solution.py:131
  221.4 18.2 %copy-start.2 = (bf16[1,64,4,4096]{3,1,0,2:T(8,128)(2,1)S(1)}, bf16[1,64,4,4096]{3,1,0,2:T(8,128)(2,1)}, u32[]{:S(2)}) copy-start(bf16[1,64,4,4096]{3,1,0,2:T(8,128)(2,1)} %get-tuple-element.14) | copy-start | bytes 6291460
  257.0 1.7 copy-start.3
  267.2 5.4 %copy-start.4 = (bf16[384,4096]{1,0:T(8,128)(2,1)S(1)}, bf16[384,4096]{1,0:T(8,128)(2,1)}, u32[]{:S(2)}) copy-start(bf16[384,4096]{1,0:T(8,128)(2,1)} %copy-done.3) | copy-start | bytes 9437188
  267.2 5.4 %copy-start.18 = (bf16[1,1,384,4096]{3,2,1,0:T(8,128)(2,1)S(1)}, bf16[1,1,384,4096]{3,2,1,0:T(8,128)(2,1)}, u32[]{:S(2)}) copy-start(bf16[1,1,384,4096]{3,2,1,0:T(8,128)(2,1)} %param.17) | copy-start | bytes 9437188
  280.5 40.7 %copy-start.11 = (bf16[16,4096]{1,0:T(8,128)(2,1)S(1)}, bf16[16,4096]{1,0:T(8,128)(2,1)}, u32[]{:S(2)}) copy-start(bf16[16,4096]{1,0:T(8,128)(2,1)} %copy-done.10) | copy-start | bytes 393220
  280.5 2.7 collective-permute-start.2
  285.1 45.0 %copy-start.13 = (bf16[16,4096]{1,0:T(8,128)(2,1)S(1)}, bf16[16,4096]{1,0:T(8,128)(2,1)}, u32[]{:S(2)}) copy-start(bf16[16,4096]{1,0:T(8,128)(2,1)} %copy-done.12) | copy-start | bytes 393220
  321.7 8.4 %collective-permute-start.3 = (bf16[16,4096]{1,0:T(8,128)(2,1)S(1)}, bf16[16,4096]{1,0:T(8,128)(2,1)S(1)}, u32[]{:S(2)}, u32[]{:S(2)}) collective-permute-start(bf16[16,4096]{1,0:T(8,128)(2,1)S(1)} %add_convert_fusion), channel_id=1, source_target_pairs={{0,128},{1,129},{2,130},{3,131},{4,132},{5,133},{6,134},{7,135},{8... | collective-permute-start | bytes 393224 | tf_op jit(solution)/shard_map/ppermute | solution.py:12
Sparse Core Ops, SparseCore 0:
  86.2 16.0 all-gather.4
  239.8 12.2 all-gather.6
where the time goes:
time: 345 us; the launch traced here: 338 us
  blocking collectives  99.7 us (29%)
  local copies, waits for them, and re-layouts  90.3 us (26%)
  waiting for transfers between devices  45 us (13%)
  matrix products  39.6 us (11%)
  other arithmetic  26.8 us (8%)
  starting transfers between devices  22.2 us (6%)
  between operations  14.4 us (4%)
    all_to_all x1, blocking collectives, spread(): lax.all_to_all(stacked, 'ep', split_axis=1, concat_axis=1, tiled=True)  64.1 us
    all_to_all x1, blocking collectives, bring_back(): return lax.all_to_all(summed, 'ep', split_axis=0, concat_axis=0, tiled=True)  35.6 us
    all_to_all x1, waiting for transfers between devices, bring_back(): return lax.all_to_all(summed, 'ep', split_axis=0, concat_axis=0, tiled=True)  17 us
    all_to_all x1, waiting for transfers between devices, spread(): lax.all_to_all(stacked, 'ep', split_axis=1, concat_axis=1, tiled=True)  16.6 us
    unnamed x39, local copies, waits for them, and re-layouts  12.3 us
    all_to_all x1, starting transfers between devices, bring_back(): return lax.all_to_all(summed, 'ep', split_axis=0, concat_axis=0, tiled=True)  11.3 us
    convert_element_type x1, other arithmetic, renew(): (weights.astype(jnp.float32) - rate * grads / scale).astype(jnp.bfloat16)  10.9 us
    convert_element_type x2, local copies, waits for them, and re-layouts, replica_sum(): per_replica[replica].astype(jnp.bfloat16)  9.31 us
  transfers between devices with their start and end apart: 8, of which 6 were waited for; matrix products, arithmetic and copies ran while one was open for 18% of the time, Pallas kernels for 0%

commit v1 on v0

--- a/solution.py
+++ b/solution.py
@@ -1,7 +1,87 @@
 import jax
 import jax.numpy as jnp
 from jax import lax
+from jax.experimental import pallas as pl
+from jax.experimental.pallas import tpu as pltpu
 from jax.sharding import PartitionSpec as P
+import functools
+
+MESH = pl.DeviceIdType.MESH
+
+
+def exchange_kernel(count, x_ref, y_ref, send_sem, recv_sem, own_sem):
+    me = lax.axis_index("ep")
+    barrier = pltpu.get_barrier_semaphore()
+
+    def greet(k, carry):
+        other = lax.rem(me + k, count)
+        pl.semaphore_signal(barrier, inc=1, device_id={"ep": other}, device_id_type=MESH)
+        return carry
+
+    lax.fori_loop(1, count, greet, 0)
+    pl.semaphore_wait(barrier, count - 1)
+    own = pltpu.make_async_copy(x_ref.at[me], y_ref.at[me], own_sem)
+    own.start()
+
+    def outgoing(k):
+        other = lax.rem(me + k, count)
+        return pltpu.make_async_remote_copy(
+            src_ref=x_ref.at[other],
+            dst_ref=y_ref.at[me],
+            send_sem=send_sem.at[other],
+            recv_sem=recv_sem.at[me],
+            device_id={"ep": other},
+            device_id_type=MESH,
+        )
+
+    def incoming(k):
+        other = lax.rem(me + count - k, count)
+        return pltpu.make_async_remote_copy(
+            src_ref=x_ref.at[other],
+            dst_ref=y_ref.at[other],
+            send_sem=send_sem.at[other],
+            recv_sem=recv_sem.at[other],
+            device_id={"ep": other},
+            device_id_type=MESH,
+        )
+
+    def launch(k, carry):
+        outgoing(k).start()
+        return carry
+
+    lax.fori_loop(1, count, launch, 0)
+
+    def settle(k, carry):
+        outgoing(k).wait_send()
+        return carry
+
+    lax.fori_loop(1, count, settle, 0)
+
+    def land(k, carry):
+        incoming(k).wait_recv()
+        return carry
+
+    lax.fori_loop(1, count, land, 0)
+    own.wait()
+
+
+def exchange(x, tag):
+    count = x.shape[0]
+    size = x.size * x.dtype.itemsize
+    return pl.pallas_call(
+        functools.partial(exchange_kernel, count),
+        out_shape=jax.ShapeDtypeStruct(x.shape, x.dtype),
+        in_specs=[pl.BlockSpec(memory_space=pl.ANY)],
+        out_specs=pl.BlockSpec(memory_space=pl.ANY),
+        scratch_shapes=[
+            pltpu.SemaphoreType.DMA((count,)),
+            pltpu.SemaphoreType.DMA((count,)),
+            pltpu.SemaphoreType.DMA(()),
+        ],
+        compiler_params=pltpu.CompilerParams(collective_id=tag, has_side_effects=True),
+        cost_estimate=pl.CostEstimate(flops=0, transcendentals=0, bytes_accessed=2 * size),
+    )(x)
+
 
 EPSILON = 1e-06
 
@@ -126,20 +206,20 @@
     own_dn = down[0, 0]
     hidden_all = own_gu.shape[2] * dp_count
 
-    def spread(stacked):
-        arrived = lax.all_to_all(stacked, "ep", split_axis=1, concat_axis=1, tiled=True)
+    def spread(stacked, tag):
+        arrived = jnp.moveaxis(exchange(jnp.moveaxis(stacked, 1, 0), tag), 0, 1)
         return lax.all_gather(arrived, "dp", axis=2)
 
     def weights_for(weights_gu, weights_dn):
         return (weights_gu, weights_dn, 1)
 
-    def bring_back(slot_out):
+    def bring_back(slot_out, tag):
         mine = lax.axis_index("dp")
         keep = lax.dynamic_index_in_dim(slot_out, mine, axis=1, keepdims=False)
         give = lax.dynamic_index_in_dim(slot_out, 1 - mine, axis=1, keepdims=False)
         got = lax.ppermute(give, "dp", [(0, 1), (1, 0)])
         summed = (keep.astype(jnp.float32) + got.astype(jnp.float32)).astype(jnp.bfloat16)
-        return lax.all_to_all(summed, "ep", split_axis=0, concat_axis=0, tiled=True)
+        return exchange(summed, tag)
 
     def combine(mixing, returned):
         total = returned.astype(jnp.float32).reshape(ep_count * capacity, model_width)
@@ -172,14 +252,14 @@
     stacked = jnp.stack([row_buffer, grad_buffer], axis=0).reshape(
         2, ep_count, capacity, model_width
     )
-    arrived = spread(stacked)
+    arrived = spread(stacked, 0)
     use_gu, use_dn, part_count = weights_for(own_gu, own_dn)
     per_gu, per_dn, slot_dx, slot_fw = learn_core(
         arrived[0], arrived[1], use_gu, use_dn, part_count
     )
     grad_gu = replica_sum(per_gu)
     grad_dn = replica_sum(per_dn)
-    returned = bring_back(jnp.where(is_learner, slot_dx, slot_fw))
+    returned = bring_back(jnp.where(is_learner, slot_dx, slot_fw), 1)
     mixing = jnp.where(is_learner, picker, weigher)
     base = jnp.where(is_learner, weight[:, None] * cot_wide, tokens.astype(jnp.float32))
     carried = (base + combine(mixing, returned)).astype(jnp.bfloat16)
@@ -189,10 +269,10 @@
     current = passed_along(carried, "grp", -1)
     picker, weigher = routing_tables(decode_experts[1], decode_gates[1], capacity, ep_count)
     stacked = dispatch(picker, current).reshape(1, ep_count, capacity, model_width)
-    arrived = spread(stacked)
+    arrived = spread(stacked, 2)
     use_gu, use_dn, part_count = weights_for(fresh_gu, fresh_dn)
     slot_out = forward_core(arrived[0], use_gu, use_dn, part_count)
-    returned = bring_back(slot_out)
+    returned = bring_back(slot_out, 3)
     current = (current.astype(jnp.float32) + combine(weigher, returned)).astype(jnp.bfloat16)
     final_rows = jnp.where(is_learner, carried, passed_along(current, "grp", 1))
     return final_rows[None]

time: 345 us -> 349 us (1.012)
  Pallas kernels: 0 us -> 158 us
  blocking collectives: 99.7 us -> 0 us
  waiting for transfers between devices: 45 us -> 14.3 us
  starting transfers between devices: 22.2 us -> 5.34 us
  local copies, waits for them, and re-layouts: 90.3 us -> 82.6 us
  other arithmetic: 26.8 us -> 32.1 us
  matrix products: 39.6 us -> 35.9 us
    pallas_call x0 -> x4, Pallas kernels: none -> 158 us  [exchange(): pl.pallas_call(functools.partial(exchange_kernel, count), out_shape=jax.S...]
    all_to_all x2 -> x0, blocking collectives: 99.7 us -> none  [the longest x1 64.1 us: spread(): lax.all_to_all(stacked, 'ep', split_axis=1, concat_axis=1, tiled=True)]
    all_to_all x2 -> x0, waiting for transfers between devices: 33.6 us -> none  [the longest x1 17 us: bring_back(): return lax.all_to_all(summed, 'ep', split_axis=0, concat_axis=0, tiled=True)]
    all_to_all x2 -> x0, starting transfers between devices: 17.4 us -> none  [the longest x1 11.3 us: bring_back(): return lax.all_to_all(summed, 'ep', split_axis=0, concat_axis=0, tiled=True)]
    all_gather x1 -> x0, local copies, waits for them, and re-layouts: 4.56 us -> none  [spread(): return lax.all_gather(arrived, 'dp', axis=2)]
    transpose x0 -> x1, local copies, waits for them, and re-layouts: none -> 4.25 us  [spread(): arrived = jnp.moveaxis(exchange(jnp.moveaxis(stacked, 1, 0), tag), 0, 1)]
    all_to_all x2 -> x0, local copies, waits for them, and re-layouts: 4.2 us -> none  [spread(): lax.all_to_all(stacked, 'ep', split_axis=1, concat_axis=1, tiled=True)]
    transpose x0 -> x1, other arithmetic: none -> 4.02 us  [spread(): arrived = jnp.moveaxis(exchange(jnp.moveaxis(stacked, 1, 0), tag), 0, 1)]
  transfers between devices with their start and end apart: 8 -> 6, of which waited for: 6 -> 4; matrix products, arithmetic and copies ran while one was open for 18% -> 14% of each run, Pallas kernels for 0% -> 0%
where the time goes in v1:
time: 349 us; the launch traced here: 343 us
  Pallas kernels  158 us (45%)
  local copies, waits for them, and re-layouts  82.6 us (24%)
  matrix products  35.9 us (10%)
  other arithmetic  32.1 us (9%)
  waiting for transfers between devices  14.3 us (4%)
  between operations  14.2 us (4%)
  starting transfers between devices  5.34 us (2%)
    pallas_call x4, Pallas kernels, exchange(): pl.pallas_call(functools.partial(exchange_kernel, count), out_shape=jax.S...  158 us
    convert_element_type x1, other arithmetic, renew(): (weights.astype(jnp.float32) - rate * grads / scale).astype(jnp.bfloat16)  10.9 us
    convert_element_type x2, local copies, waits for them, and re-layouts, replica_sum(): per_replica[replica].astype(jnp.bfloat16)  10.1 us
    unnamed x55, local copies, waits for them, and re-layouts  9.76 us
    dot_general x1, local copies, waits for them, and re-layouts, learn_core(): jnp.dot(rows_four.reshape(slot_count, model_width), weights_gu.reshape(mo...  8.85 us
    convert_element_type x1, local copies, waits for them, and re-layouts, renew(): (weights.astype(jnp.float32) - rate * grads / scale).astype(jnp.bfloat16)  8.66 us
    ppermute x2, waiting for transfers between devices, passed_along(): return lax.ppermute(block, axis, route)  8.35 us
  transfers between devices with their start and end apart: 6, of which 4 were waited for; matrix products, arithmetic and copies ran while one was open for 14% of the time, Pallas kernels for 0%

profile of v1, /device:TPU:4, one launch (start us, length us, event | category | flops | bytes accessed | tf_op | source)
XLA Modules:
  0.0 342.7 jit_solution(10104709288732948119)
XLA Ops:
  6.5 0.7 slice.52
  8.0 0.7 bitcast_add_fusion
  9.6 0.7 bitcast_select_fusion
  10.4 0.8 reduce-window.8
  11.2 0.7 bitcast_subtract_fusion
  11.9 0.7 select_reduce_fusion.4
  12.8 2.0 convolution_convert_fusion.3
  14.8 0.7 stack.28
  15.5 0.4 convolution_convert_fusion.4
  15.9 0.7 stack.27
  16.7 4.0 %maximum_bitcast_fusion.x_ref = bf16[64,2,2,4096]{3,2,1,0:T(2,128)(2,1)} fusion(bf16[1,64,2,4096]{3,2,0,1:T(2,128)(2,1)S(1)} %stack.28, bf16[1,64,2,4096]{3,2,0,1:T(2,128)(2,1)S(1)} %stack.27), kind=kLoop, calls=%fused_computation.30 | loop fusion | flops 1048576 | bytes 4194304 | tf_op jit(solution)/shard_map/transpose | solution.py:210
  20.7 58.3 %shard_map.91 = bf16[64,2,2,4096]{3,2,1,0:T(2,128)(2,1)} custom-call(bf16[64,2,2,4096]{3,2,1,0:T(2,128)(2,1)} %maximum_bitcast_fusion.x_ref), custom_call_target="tpu_custom_call" | custom-call | bytes 4194304 | tf_op jit(solution)/shard_map/pallas_call | solution.py:71
  79.0 4.2 %copy.92 = bf16[2,64,2,4096]{3,1,0,2:T(8,128)(2,1)} copy(bf16[2,64,2,4096]{3,2,0,1:T(2,128)(2,1)} %bitcast.157) | data formatting | bytes 4194304 | tf_op jit(solution)/shard_map/transpose | solution.py:210
  83.3 0.6 all-gather.7.cloned.1.call-start
  83.8 6.5 %copy.114 = bf16[512,8,2,384]{3,1,2,0:T(8,128)(2,1)} copy(bf16[512,8,2,384]{3,2,1,0:T(2,128)(2,1)} %bitcast.152) | data formatting | bytes 12582912
  90.4 8.9 %copy.95 = bf16[768,4096]{1,0:T(8,128)(2,1)} copy(bf16[768,4096]{0,1:T(8,128)(2,1)} %bitcast.151) | data formatting | bytes 12582912 | tf_op jit(solution)/shard_map/dot_general | solution.py:149
  99.4 0.7 convert_reduce_fusion
  100.1 3.3 all-gather.5.cloned.1.call-done
  103.4 3.9 %fusion.58 = (bf16[1,64,4,4096]{3,1,0,2:T(8,128)(2,1)S(1)}, bf16[1,64,4,4096]{3,1,0,2:T(8,128)(2,1)}) fusion(bf16[2,64,4,4096]{3,1,0,2:T(8,128)(2,1)} %all-gather.5.cloned.1.call-done), kind=kLoop, calls=%fused_computation.106 | loop fusion | bytes 8388608 | tf_op jit(solution)/shard_map/slice | solution.py:258
  107.3 3.0 copy.94
  110.3 4.0 %reshape.147 = bf16[256,4096,1]{1,0,2:T(8,128)(2,1)} reshape(bf16[1,64,4,4096]{3,2,1,0:T(4,128)(2,1)} %copy.94) | data formatting | bytes 4194304 | tf_op jit(solution)/shard_map/reshape;squeeze | solution.py:150
  114.3 4.5 %copy.93 = bf16[1,64,4,4096]{3,2,1,0:T(4,128)(2,1)} copy(bf16[1,64,4,4096]{3,1,0,2:T(8,128)(2,1)} %get-tuple-element.14) | data formatting | bytes 4194304 | tf_op jit(solution)/shard_map/slice | solution.py:258
  118.8 4.0 %reshape_squeeze.13 = bf16[256,4096]{1,0:T(8,128)(2,1)} reshape(bf16[1,64,4,4096]{3,2,1,0:T(4,128)(2,1)} %copy.93) | data formatting | bytes 4194304 | tf_op jit(solution)/shard_map/reshape;squeeze | solution.py:148
  122.8 5.4 %fusion.60 = f32[256,2,384]{2,0,1:T(8,128)S(1)} fusion(bf16[256,4096,1]{1,0,2:T(8,128)(2,1)} %reshape.147, bf16[2,384,4096]{2,1,0:T(8,128)(2,1)} %bitcast.158), kind=kOutput, calls=%fused_computation.108 | convolution fusion | flops 1610612736 | bytes 9175040 | tf_op jit(solution)/shard_map/dot_general | solution.py:149
  128.3 1.3 fusion.31
  130.3 6.4 %bitcast_convert_fusion = bf16[2,4096,2,384]{3,1,2,0:T(8,128)(2,1)} fusion(bf16[64,2,2,4096,1]{3,0,2,4,1:T(8,128)(2,1)S(1)} %bitcast.155, bf16[64,2,2,1,384]{4,0,2,3,1:T(8,128)(2,1)S(1)} %copy.103, bf16[64,2,2,1,384]{4,0,2,3,1:T(8,128)(2,1)S(1)} %copy.102), kind=kOutput, calls=%fused_computation | convolution fusion | flops 1617690624 | bytes 15073280 | tf_op jit(solution)/shard_map/epcd,epcgh->pdgh/dot_general | solution.py:171
  136.6 6.4 %slice_bitcast_fusion.1 = (bf16[4096,2,384]{2,0,1:T(8,128)(2,1)S(1)}, bf16[4096,2,384]{2,0,1:T(8,128)(2,1)S(1)}) fusion(bf16[2,4096,2,384]{3,1,2,0:T(8,128)(2,1)} %bitcast_convert_fusion), kind=kLoop, calls=%fused_computation.6 | loop fusion | bytes 25165824 | tf_op jit(solution)/shard_map/convert_element_type | solution.py:116
  143.0 3.2 multiply_reduce_fusion
  146.3 1.3 copy-done.1
  147.6 1.3 add_sqrt_fusion
  148.9 1.9 fusion.8
  151.0 2.6 fusion.11
  153.6 3.2 select_n.70
  156.8 0.9 dynamic-slice_bitcast_fusion.1
  158.1 10.9 %subtract_convert_fusion = bf16[4096,2,384]{2,0,1:T(8,128)(2,1)} fusion(bf16[4096,2,384]{2,0,1:T(8,128)(2,1)} %copy-done.1, bf16[4096,2,384]{2,0,1:T(8,128)(2,1)} %copy-done, f32[2,384]{1,0:T(2,128)S(1)} %copy-done.18, bf16[1,1,4096,2,384]{4,3,2,1,0:T(2,128)(2,1)} %param.16), kind=kLoop, calls=%fused_computation.2 | loop fusion | flops 25165824 | bytes 25168896 | tf_op jit(solution)/shard_map/convert_element_type | solution.py:124
  169.0 2.8 fusion.17.x_ref
  171.9 34.2 %shard_map.92 = bf16[64,2,4096]{2,1,0:T(2,128)(2,1)} custom-call(bf16[64,2,4096]{2,1,0:T(2,128)(2,1)} %fusion.17.x_ref), custom_call_target="tpu_custom_call" | custom-call | bytes 2097152 | tf_op jit(solution)/shard_map/pallas_call | solution.py:71
  206.1 1.5 reshape.133
  207.6 0.5 fusion.12
  208.1 2.7 collective-permute-start.1
  211.2 1.0 squeeze.62
  212.1 1.3 collective-permute-done.1
  213.4 0.6 copy-done.12
  214.1 1.5 convolution_convert_fusion.2
  215.6 1.7 transpose_reshape.3.x_ref
  217.3 32.2 %shard_map.93 = bf16[64,1,2,4096]{3,2,1,0:T(2,128)(2,1)} custom-call(bf16[64,1,2,4096]{3,2,1,0:T(2,128)(2,1)} %transpose_reshape.3.x_ref), custom_call_target="tpu_custom_call" | custom-call | bytes 2097152 | tf_op jit(solution)/shard_map/pallas_call | solution.py:71
  249.6 4.4 %bitcast_convert_fusion.1 = bf16[2,384,4096]{2,1,0:T(8,128)(2,1)} fusion(bf16[64,2,2,4096]{3,0,2,1:T(8,128)(2,1)S(1)} %bitcast.156, f32[64,2,2,384]{3,2,1,0:T(2,128)S(1)} %copy-done.6, f32[64,2,2,384]{3,2,1,0:T(2,128)S(1)} %squeeze.61), kind=kOutput, calls=%fused_computation.1 | convolution fusion | flops 809041920 | bytes 9175040 | tf_op jit(solution)/shard_map/epch,epcd->phd/dot_general | solution.py:165
  254.0 8.7 %copy.104 = bf16[4096,2,384]{0,2,1:T(8,128)(2,1)} copy(bf16[4096,2,384]{2,0,1:T(8,128)(2,1)} %subtract_convert_fusion) | data formatting | bytes 12582912 | tf_op jit(solution)/shard_map/convert_element_type | solution.py:124
  262.7 3.8 %slice_bitcast_fusion.3 = (bf16[384,4096]{1,0:T(8,128)(2,1)S(1)}, bf16[384,4096]{1,0:T(8,128)(2,1)S(1)}) fusion(bf16[2,384,4096]{2,1,0:T(8,128)(2,1)} %bitcast_convert_fusion.1), kind=kLoop, calls=%fused_computation.26 | loop fusion | bytes 12582912 | tf_op jit(solution)/shard_map/convert_element_type | solution.py:116
  266.5 1.1 multiply_reduce_fusion.1
  267.6 0.5 copy-done.3
  268.1 4.1 %reshape.151 = bf16[256,4096,1]{1,0,2:T(8,128)(2,1)} reshape(bf16[64,2,2,4096]{3,2,1,0:T(2,128)(2,1)} %all-gather.7.cloned.1.call-done) | data formatting | bytes 4194304 | tf_op jit(solution)/shard_map/reshape;squeeze | solution.py:132
  272.2 5.4 %fusion = f32[256,2,384]{2,0,1:T(8,128)S(1)} fusion(bf16[256,4096,1]{1,0,2:T(8,128)(2,1)} %reshape.151, bf16[4096,2,384]{0,2,1:T(8,128)(2,1)} %copy.104), kind=kOutput, calls=%fused_computation.7 | convolution fusion | flops 1610612736 | bytes 9175040 | tf_op jit(solution)/shard_map/dot_general | solution.py:131
  277.6 3.5 %convolution_convert_fusion = bf16[256,4096]{1,0:T(8,128)(2,1)} fusion(bf16[384,4096]{1,0:T(8,128)(2,1)S(1)} %copy-done.4, bf16[384,4096]{1,0:T(8,128)(2,1)S(1)} %get-tuple-element.11, bf16[1,1,384,4096]{3,2,1,0:T(8,128)(2,1)S(1)} %copy-done.24, f32[384]{0:T(512)S(1)} %add_sqrt_fusion.1, f32[256,2,384]{2,0,1:T(8,128)S(1)} %fusion), kind=kOutput, calls=%fused_computation.16 | convolution fusion | flops 819527680 | bytes 12322304 | tf_op jit(solution)/shard_map/dot_general | solution.py:139
  281.2 3.2 reshape_reshape.2
  284.3 0.9 dynamic-slice_bitcast_fusion
  285.6 2.6 collective-permute-done.2
  288.2 2.8 fusion.16.x_ref
  291.0 33.5 %shard_map.94 = bf16[64,2,4096]{2,1,0:T(2,128)(2,1)} custom-call(bf16[64,2,4096]{2,1,0:T(2,128)(2,1)} %fusion.16.x_ref), custom_call_target="tpu_custom_call" | custom-call | bytes 2097152 | tf_op jit(solution)/shard_map/pallas_call | solution.py:71
  324.5 1.5 reshape.135
  326.0 0.5 add_convert_fusion
  326.5 1.3 collective-permute-start.3
  327.8 7.1 %collective-permute-done.3 = bf16[16,4096]{1,0:T(8,128)(2,1)S(1)} collective-permute-done((bf16[16,4096]{1,0:T(8,128)(2,1)S(1)}, bf16[16,4096]{1,0:T(8,128)(2,1)S(1)}, u32[]{:S(2)}, u32[]{:S(2)}) %collective-permute-start.3) | collective-permute-done | bytes 131104 | tf_op jit(solution)/shard_map/ppermute | solution.py:92
  334.9 0.7 select_bitcast_fusion
  (89 shorter events, 3.9 us)
Async XLA Ops:
  6.5 8.9 %copy-start.11 = (bf16[1,16,4096]{2,1,0:T(8,128)(2,1)S(1)}, bf16[1,16,4096]{2,1,0:T(8,128)(2,1)}, u32[]{:S(2)}) copy-start(bf16[1,16,4096]{2,1,0:T(8,128)(2,1)} %param.9) | copy-start | bytes 393220
  6.5 96.8 %all-gather.5.cloned.1.call-start = ((), (), s32[]{:S(2)}) async-start(), calls=%async_computation | async-start | bytes 6291456 | tf_op jit(solution)/shard_map/all_gather | solution.py:211
  12.6 4.0 %copy-start.20 = (f32[16]{0:T(128)}, f32[16]{0:T(128)S(1)}, u32[]{:S(2)}) copy-start(f32[16]{0:T(128)S(1)} %add_divide_fusion) | copy-start | bytes 196
  83.3 184.8 %all-gather.7.cloned.1.call-start = ((), (), s32[]{:S(2)}) async-start(), calls=%async_computation.1 | async-start | bytes 3145728 | tf_op jit(solution)/shard_map/all_gather | solution.py:211
  90.4 8.9 %copy-start.19 = (f32[2,16,8]{1,2,0:T(8,128)S(1)}, f32[2,16,8]{1,2,0:T(8,128)}, u32[]{:S(2)}) copy-start(f32[2,16,8]{1,2,0:T(8,128)} %param.15) | copy-start | bytes 3076
  122.8 5.4 %copy-start.5 = (bf16[256,4096]{1,0:T(8,128)(2,1)S(1)}, bf16[256,4096]{1,0:T(8,128)(2,1)}, u32[]{:S(2)}) copy-start(bf16[256,4096]{1,0:T(8,128)(2,1)} %reshape_squeeze.13) | copy-start | bytes 6291460
  122.8 5.4 %copy-start.22 = (bf16[1,1,384,4096]{3,2,1,0:T(8,128)(2,1)S(1)}, bf16[1,1,384,4096]{3,2,1,0:T(8,128)(2,1)}, u32[]{:S(2)}) copy-start(bf16[1,1,384,4096]{3,2,1,0:T(8,128)(2,1)} %param.17) | copy-start | bytes 9437188
  128.2 1.3 copy-start.7
  129.6 0.7 copy-start.16
  130.3 18.6 %slice-start = ((s8[6291456]{0:T(1024)(128)(4,1)}), s8[4194304]{0:T(1024)(128)(4,1)S(1)}, s32[]{:S(2)}) async-start(s8[6291456]{0:T(1024)(128)(4,1)} %bitcast.153), calls=%async_computation.2 | async-start | bytes 8388608
  136.6 12.2 %slice-start.1 = ((s8[6291456]{0:T(1024)(128)(4,1)}), s8[2097152]{0:T(1024)(128)(4,1)S(1)}, s32[]{:S(2)}) async-start(s8[6291456]{0:T(1024)(128)(4,1)} %bitcast.153), calls=%async_computation.3 | async-start | bytes 4194304
  143.0 3.2 copy-start
  143.0 4.6 %copy-start.1 = (bf16[4096,2,384]{2,0,1:T(8,128)(2,1)}, bf16[4096,2,384]{2,0,1:T(8,128)(2,1)S(1)}, u32[]{:S(2)}) copy-start(bf16[4096,2,384]{2,0,1:T(8,128)(2,1)S(1)} %get-tuple-element.10) | copy-start | bytes 18874372
  143.0 5.9 %copy-start.17 = (bf16[256,384]{1,0:T(8,128)(2,1)S(1)}, bf16[256,384]{1,0:T(8,128)(2,1)}, u32[]{:S(2)}) copy-start(bf16[256,384]{1,0:T(8,128)(2,1)} %copy-done.16) | copy-start | bytes 589828
  148.9 1.9 copy-start.8
  148.9 2.1 copy-start.23
  153.6 4.5 %copy-start.18 = (f32[2,384]{1,0:T(2,128)S(1)}, f32[2,384]{1,0:T(2,128)}, u32[]{:S(2)}) copy-start(f32[2,384]{1,0:T(2,128)} %add_sqrt_fusion) | copy-start | bytes 9220
  157.7 11.3 %collective-permute-start = (bf16[64,2,4096]{2,1,0:T(2,128)(2,1)S(1)}, bf16[64,2,4096]{2,1,0:T(2,128)(2,1)S(1)}, u32[]{:S(2)}, u32[]{:S(2)}) collective-permute-start(bf16[64,2,4096]{2,1,0:T(2,128)(2,1)S(1)} %dynamic-slice_bitcast_fusion.1), channel_id=1, source_target_pairs={{0,1},{1,0},{2,3},{3,2},{4,5},{5,4},{6,7},{7,6},{8,9},{9,8},{10,11... | collective-permute-start | bytes 3145736 | tf_op jit(solution)/shard_map/ppermute | solution.py:220
  169.0 38.5 %copy-start.10 = (bf16[16,4096]{1,0:T(8,128)(2,1)S(1)}, bf16[16,4096]{1,0:T(8,128)(2,1)}, u32[]{:S(2)}) copy-start(bf16[16,4096]{1,0:T(8,128)(2,1)} %param.10) | copy-start | bytes 393220
  169.0 38.5 %copy-start.21 = (f32[16]{0:T(128)S(1)}, f32[16]{0:T(128)}, u32[]{:S(2)}) copy-start(f32[16]{0:T(128)} %copy-done.20) | copy-start | bytes 196
  171.9 39.0 %copy-start.9 = (f32[256,2,384]{2,0,1:T(8,128)S(1)}, f32[256,2,384]{2,0,1:T(8,128)}, u32[]{:S(2)}) copy-start(f32[256,2,384]{2,0,1:T(8,128)} %copy-done.7) | copy-start | bytes 2359300
  208.1 5.3 %copy-start.14 = (bf16[16,4096]{1,0:T(8,128)(2,1)}, bf16[16,4096]{1,0:T(8,128)(2,1)S(1)}, u32[]{:S(2)}) copy-start(bf16[16,4096]{1,0:T(8,128)(2,1)S(1)} %fusion.12) | copy-start | bytes 393220
  208.1 5.3 %collective-permute-start.1 = (bf16[16,4096]{1,0:T(8,128)(2,1)S(1)}, bf16[16,4096]{1,0:T(8,128)(2,1)S(1)}, u32[]{:S(2)}, u32[]{:S(2)}) collective-permute-start(bf16[16,4096]{1,0:T(8,128)(2,1)S(1)} %fusion.12), channel_id=1, source_target_pairs={{128,0},{129,1},{130,2},{131,3},{132,4},{133,5},{134,6},{135,7},{1... | collective-permute-start | bytes 393224 | tf_op jit(solution)/shard_map/ppermute | solution.py:92
  213.4 0.6 copy-start.12
  214.1 35.5 %copy-start.2 = (bf16[1,64,4,4096]{3,1,0,2:T(8,128)(2,1)S(1)}, bf16[1,64,4,4096]{3,1,0,2:T(8,128)(2,1)}, u32[]{:S(2)}) copy-start(bf16[1,64,4,4096]{3,1,0,2:T(8,128)(2,1)} %get-tuple-element.14) | copy-start | bytes 6291460
  217.3 32.3 %copy-start.6 = (f32[64,2,2,384]{3,2,1,0:T(2,128)S(1)}, f32[64,2,2,384]{3,2,1,0:T(2,128)}, u32[]{:S(2)}) copy-start(f32[64,2,2,384]{3,2,1,0:T(2,128)} %squeeze.62) | copy-start | bytes 1179652
  266.4 1.6 copy-start.3
  272.2 5.4 %copy-start.4 = (bf16[384,4096]{1,0:T(8,128)(2,1)S(1)}, bf16[384,4096]{1,0:T(8,128)(2,1)}, u32[]{:S(2)}) copy-start(bf16[384,4096]{1,0:T(8,128)(2,1)} %copy-done.3) | copy-start | bytes 9437188
  272.2 5.4 %copy-start.24 = (bf16[1,1,384,4096]{3,2,1,0:T(8,128)(2,1)S(1)}, bf16[1,1,384,4096]{3,2,1,0:T(8,128)(2,1)}, u32[]{:S(2)}) copy-start(bf16[1,1,384,4096]{3,2,1,0:T(8,128)(2,1)} %param.17) | copy-start | bytes 9437188
  285.2 40.8 %copy-start.13 = (bf16[16,4096]{1,0:T(8,128)(2,1)S(1)}, bf16[16,4096]{1,0:T(8,128)(2,1)}, u32[]{:S(2)}) copy-start(bf16[16,4096]{1,0:T(8,128)(2,1)} %copy-done.12) | copy-start | bytes 393220
  285.2 3.0 collective-permute-start.2
  291.0 43.9 %copy-start.15 = (bf16[16,4096]{1,0:T(8,128)(2,1)S(1)}, bf16[16,4096]{1,0:T(8,128)(2,1)}, u32[]{:S(2)}) copy-start(bf16[16,4096]{1,0:T(8,128)(2,1)} %copy-done.14) | copy-start | bytes 393220
  326.5 8.4 %collective-permute-start.3 = (bf16[16,4096]{1,0:T(8,128)(2,1)S(1)}, bf16[16,4096]{1,0:T(8,128)(2,1)S(1)}, u32[]{:S(2)}, u32[]{:S(2)}) collective-permute-start(bf16[16,4096]{1,0:T(8,128)(2,1)S(1)} %add_convert_fusion), channel_id=1, source_target_pairs={{0,128},{1,129},{2,130},{3,131},{4,132},{5,133},{6,134},{7,135},{8... | collective-permute-start | bytes 393224 | tf_op jit(solution)/shard_map/ppermute | solution.py:92
Sparse Core Ops, SparseCore 0:
  83.4 19.9 all-gather.4
  249.7 16.3 all-gather.6

commit v2 on v1

v2 whole, which is shorter than its diff:
```python
import jax
import jax.numpy as jnp
from jax import lax
from jax.experimental import pallas as pl
from jax.experimental.pallas import tpu as pltpu
from jax.sharding import PartitionSpec as P
import functools

MESH = pl.DeviceIdType.MESH


def exchange_kernel(count, width, *refs):
    parts = len(refs) // 2 - 1
    sources, targets = refs[:parts], refs[parts:2 * parts]
    send_sem, recv_sem, own_sem = refs[2 * parts:]
    me = lax.axis_index("ep")
    barrier = pltpu.get_barrier_semaphore()

    def greet(k, carry):
        other = lax.rem(me + k, count)
        pl.semaphore_signal(barrier, inc=1, device_id={"ep": other}, device_id_type=MESH)
        return carry

    lax.fori_loop(1, count, greet, 0)
    pl.semaphore_wait(barrier, count - 1)
    owns = []
    for part in range(parts):
        here = pl.ds(pl.multiple_of(me * width, width), width)
        own = pltpu.make_async_copy(sources[part].at[here], targets[part].at[here], own_sem.at[part])
        own.start()
        owns.append(own)

    def outgoing(part, k):
        other = lax.rem(me + k, count)
        return pltpu.make_async_remote_copy(
            src_ref=sources[part].at[pl.ds(pl.multiple_of(other * width, width), width)],
            dst_ref=targets[part].at[pl.ds(pl.multiple_of(me * width, width), width)],
            send_sem=send_sem.at[part, other],
            recv_sem=recv_sem.at[part, me],
            device_id={"ep": other},
            device_id_type=MESH,
        )

    def incoming(part, k):
        other = lax.rem(me + count - k, count)
        there = pl.ds(pl.multiple_of(other * width, width), width)
        return pltpu.make_async_remote_copy(
            src_ref=sources[part].at[there],
            dst_ref=targets[part].at[there],
            send_sem=send_sem.at[part, other],
            recv_sem=recv_sem.at[part, other],
            device_id={"ep": other},
            device_id_type=MESH,
        )

    def launch(k, carry):
        for part in range(parts):
            outgoing(part, k).start()
        return carry

    lax.fori_loop(1, count, launch, 0)

    def settle(k, carry):
        for part in range(parts):
            outgoing(part, k).wait_send()
        return carry

    lax.fori_loop(1, count, settle, 0)

    def land(k, carry):
        for part in range(parts):
            incoming(part, k).wait_recv()
        return carry

    lax.fori_loop(1, count, land, 0)
    for own in owns:
        own.wait()


def exchange(blocks, count, tag):
    parts = len(blocks)
    width = blocks[0].shape[0] // count
    size = sum(block.size * block.dtype.itemsize for block in blocks)
    return pl.pallas_call(
        functools.partial(exchange_kernel, count, width),
        out_shape=[jax.ShapeDtypeStruct(block.shape, block.dtype) for block in blocks],
        in_specs=[pl.BlockSpec(memory_space=pl.ANY)] * parts,
        out_specs=[pl.BlockSpec(memory_space=pl.ANY)] * parts,
        scratch_shapes=[
            pltpu.SemaphoreType.DMA((parts, count)),
            pltpu.SemaphoreType.DMA((parts, count)),
            pltpu.SemaphoreType.DMA((parts,)),
        ],
        compiler_params=pltpu.CompilerParams(collective_id=tag, has_side_effects=True),
        cost_estimate=pl.CostEstimate(flops=0, transcendentals=0, bytes_accessed=2 * size),
    )(*blocks)


EPSILON = 1e-06


def passed_along(block, axis, distance):
    devices = range(lax.axis_size(axis))
    route = [(i - distance, i) for i in devices if i - distance in devices]
    return lax.ppermute(block, axis, route)


def routing_tables(expert_ids, gate_values, capacity, expert_count):
    row_count, top_count = expert_ids.shape
    flat_ids = expert_ids.reshape(row_count * top_count)
    onehot = (flat_ids[:, None] == jnp.arange(expert_count, dtype=jnp.int32)[None, :]).astype(
        jnp.int32
    )
    earlier = jnp.cumsum(onehot, axis=0) - onehot
    ranks = jnp.sum(earlier * onehot, axis=1)
    slots = flat_ids * capacity + ranks
    hits = (slots[:, None] == jnp.arange(expert_count * capacity, dtype=jnp.int32)[None, :]).astype(
        jnp.float32
    )
    hits = hits.reshape(row_count, top_count, expert_count * capacity)
    picker = jnp.sum(hits, axis=1)
    weigher = jnp.sum(hits * gate_values[:, :, None], axis=1)
    return (picker, weigher)


def replica_sum(per_replica):
    total = jnp.zeros(per_replica.shape[1:], jnp.float32)
    for replica in range(per_replica.shape[0]):
        total = total + lax.optimization_barrier(per_replica[replica].astype(jnp.bfloat16)).astype(
            jnp.float32
        )
    return total


def renew(weights, grads, axis_number, rate):
    scale = jnp.sqrt(jnp.mean(grads * grads, axis=axis_number, keepdims=True) + EPSILON)
    return (weights.astype(jnp.float32) - rate * grads / scale).astype(jnp.bfloat16)


def forward_core(slot_rows, weights_gu, weights_dn):
    hidden_count = weights_gu.shape[2]
    both = jnp.dot(
        slot_rows,
        weights_gu.reshape(slot_rows.shape[1], 2 * hidden_count),
        preferred_element_type=jnp.float32,
    ).reshape(-1, 2, hidden_count)
    active = both[:, 0]
    upward = both[:, 1]
    hidden = (active * jax.nn.sigmoid(active) * upward).astype(jnp.bfloat16)
    return jnp.dot(hidden, weights_dn, preferred_element_type=jnp.float32).astype(jnp.bfloat16)


def learn_core(slot_rows, slot_grads, weights_gu, weights_dn, rep_count):
    slot_count, model_width = slot_rows.shape
    hidden_count = weights_gu.shape[2]
    both = jnp.dot(
        slot_rows,
        weights_gu.reshape(model_width, 2 * hidden_count),
        preferred_element_type=jnp.float32,
    ).reshape(slot_count, 2, hidden_count)
    active = both[:, 0]
    upward = both[:, 1]
    sigma = jax.nn.sigmoid(active)
    swish = active * sigma
    hidden = (swish * upward).astype(jnp.bfloat16)
    back = lax.dot_general(
        slot_grads, weights_dn, (((1,), (1,)), ((), ())), preferred_element_type=jnp.float32
    )
    d_active = back * upward * sigma * (1.0 + active * (1.0 - sigma))
    d_upward = back * swish
    d_both = jnp.stack([d_active, d_upward], axis=1).astype(jnp.bfloat16)
    grad_dn = jnp.einsum(
        "pch,pcd->phd",
        hidden.reshape(rep_count, -1, hidden_count),
        slot_grads.reshape(rep_count, -1, model_width),
        preferred_element_type=jnp.float32,
    )
    grad_gu = jnp.einsum(
        "pcd,pcgh->pdgh",
        slot_rows.reshape(rep_count, -1, model_width),
        d_both.reshape(rep_count, -1, 2, hidden_count),
        preferred_element_type=jnp.float32,
    )
    slot_dx = jnp.einsum("mgh,dgh->md", d_both, weights_gu, preferred_element_type=jnp.float32)
    slot_fw = jnp.dot(hidden, weights_dn, preferred_element_type=jnp.float32)
    return (grad_gu, grad_dn, slot_dx.astype(jnp.bfloat16), slot_fw.astype(jnp.bfloat16))


def per_device(
    rows_in,
    cotangent,
    lengths,
    train_experts,
    train_gates,
    decode_experts,
    decode_gates,
    gate_up,
    down,
):
    ep_count = lax.axis_size("ep")
    dp_count = lax.axis_size("dp")
    row_count, model_width = cotangent.shape
    top_count = train_experts.shape[1]
    capacity = min(row_count, max(2, 4 * row_count * top_count // (3 * ep_count)))
    is_learner = lax.axis_index("grp") == 0
    own_gu = gate_up[0, 0]
    own_dn = down[0, 0]
    hidden_all = own_gu.shape[2] * dp_count

    def spread(buffers, tag):
        arrived = exchange(buffers, ep_count, tag)
        return [lax.all_gather(block, "dp", axis=0, tiled=True) for block in arrived]

    def bring_back(pieces, tag):
        half = pieces.shape[0] // dp_count
        mine = lax.axis_index("dp")
        keep = lax.dynamic_slice_in_dim(pieces, mine * half, half)
        give = lax.dynamic_slice_in_dim(pieces, (1 - mine) * half, half)
        got = lax.ppermute(give, "dp", [(0, 1), (1, 0)])
        summed = (keep.astype(jnp.float32) + got.astype(jnp.float32)).astype(jnp.bfloat16)
        return exchange([summed], ep_count, tag)[0]

    def combine(mixing, returned):
        total = returned.astype(jnp.float32)
        return jnp.einsum("rs,sd->rd", mixing, total, precision=lax.Precision.HIGHEST)

    def dispatch(picker, values):
        buffer = jnp.einsum(
            "rs,rd->sd", picker.astype(jnp.bfloat16), values, preferred_element_type=jnp.float32
        )
        return buffer.astype(jnp.bfloat16)

    tokens = rows_in[0]
    total_rows = row_count * ep_count * dp_count
    longest = 2 * total_rows // lengths.shape[0]
    first_row = (lax.axis_index("ep") * dp_count + lax.axis_index("dp")) * row_count
    places = first_row + jnp.arange(row_count, dtype=jnp.int32)
    ends = jnp.cumsum(lengths)
    starts = ends - lengths
    inside = (places[:, None] >= starts[None, :]) & (places[:, None] < ends[None, :])
    seq_len = jnp.sum(jnp.where(inside, lengths[None, :], 0), axis=1).astype(jnp.float32)
    weight = 2.0 * longest / (seq_len + longest)
    route_ids = jnp.where(is_learner, train_experts, decode_experts[0])
    route_gates = jnp.where(is_learner, train_gates, decode_gates[0])
    picker, weigher = routing_tables(route_ids, route_gates, capacity, ep_count)
    row_buffer = dispatch(picker, tokens)
    cot_wide = cotangent.astype(jnp.float32)
    grad_buffer = jnp.einsum(
        "rs,rd->sd", weigher * weight[:, None], cot_wide, precision=lax.Precision.HIGHEST
    ).astype(jnp.bfloat16)
    rows_got, grads_got = spread([row_buffer, grad_buffer], 0)
    per_gu, per_dn, slot_dx, slot_fw = learn_core(rows_got, grads_got, own_gu, own_dn, dp_count)
    grad_gu = replica_sum(per_gu)
    grad_dn = replica_sum(per_dn)
    returned = bring_back(jnp.where(is_learner, slot_dx, slot_fw), 1)
    mixing = jnp.where(is_learner, picker, weigher)
    base = jnp.where(is_learner, weight[:, None] * cot_wide, tokens.astype(jnp.float32))
    carried = (base + combine(mixing, returned)).astype(jnp.bfloat16)
    fresh_gu = renew(own_gu, grad_gu, 0, 0.5 / model_width**0.5)
    fresh_dn = renew(own_dn, grad_dn, 1, 0.5 / hidden_all**0.5)
    current = passed_along(carried, "grp", -1)
    picker, weigher = routing_tables(decode_experts[1], decode_gates[1], capacity, ep_count)
    (rows_got,) = spread([dispatch(picker, current)], 2)
    slot_out = forward_core(rows_got, fresh_gu, fresh_dn)
    returned = bring_back(slot_out, 3)
    current = (current.astype(jnp.float32) + combine(weigher, returned)).astype(jnp.bfloat16)
    final_rows = jnp.where(is_learner, carried, passed_along(current, "grp", 1))
    return final_rows[None]


def solution(mesh):
    placed = (
        P("grp", ("ep", "dp"), None),
        P(("ep", "dp"), None),
        P(),
        P(("ep", "dp"), None),
        P(("ep", "dp"), None),
        P(None, ("ep", "dp"), None),
        P(None, ("ep", "dp"), None),
        P("grp", "ep", None, None, "dp"),
        P("grp", "ep", "dp", None),
    )
    return jax.shard_map(
        per_device,
        mesh=mesh,
        in_specs=placed,
        out_specs=P("grp", ("ep", "dp"), None),
        check_vma=False,
    )
```

time: 349 us -> 312 us (0.89); the launches traced: 343 us -> 311 us
  local copies, waits for them, and re-layouts: 82.6 us -> 38.8 us
  waiting for transfers between devices: 14.3 us -> 36.3 us
  other arithmetic: 32.1 us -> 18 us
    all_gather x2 -> x3, waiting for transfers between devices: 3.31 us -> 24.9 us  [spread(): lax.all_gather(block, 'dp', axis=0, tiled=True)]
    another operation x11 -> x0, local copies, waits for them, and re-layouts: 18.6 us -> none  [the longest x1 4.13 us: forward_core(): rows_four.reshape(slot_count, model_width)]
    slice x3 -> x0, local copies, waits for them, and re-layouts: 11.4 us -> none  [the longest x2 6.91 us: per_device(): arrived[0]]
    convert_element_type x1, other arithmetic: 10.9 us -> 5.1 us  [renew(): (weights.astype(jnp.float32) - rate * grads / scale).astype(jnp.bfloat16)]
    transpose x1 -> x0, local copies, waits for them, and re-layouts: 4.25 us -> none  [spread(): arrived = jnp.moveaxis(exchange(jnp.moveaxis(stacked, 1, 0), tag), 0, 1)]
    transpose x1 -> x0, other arithmetic: 4.02 us -> none  [spread(): arrived = jnp.moveaxis(exchange(jnp.moveaxis(stacked, 1, 0), tag), 0, 1)]
    unnamed x55 -> x35, local copies, waits for them, and re-layouts: 9.76 us -> 9.76 us
  transfers between devices with their start and end apart: 6 -> 7, of which waited for: 4 -> 6; matrix products, arithmetic and copies ran while one was open for 14% -> 13% of each run, Pallas kernels for 0% -> 0%
where the time goes in v2:
time: 312 us; the launch traced here: 311 us
  Pallas kernels  160 us (51%)
  matrix products  39.2 us (13%)
  local copies, waits for them, and re-layouts  38.8 us (12%)
  waiting for transfers between devices  36.3 us (12%)
  other arithmetic  18 us (6%)
  between operations  13.5 us (4%)
  starting transfers between devices  4.81 us (2%)
    pallas_call x4, Pallas kernels, exchange(): pl.pallas_call(functools.partial(exchange_kernel, count, width), out_shap...  160 us
    all_gather x3, waiting for transfers between devices, spread(): lax.all_gather(block, 'dp', axis=0, tiled=True)  24.9 us
    unnamed x35, local copies, waits for them, and re-layouts  9.76 us
    convert_element_type x1, local copies, waits for them, and re-layouts, renew(): (weights.astype(jnp.float32) - rate * grads / scale).astype(jnp.bfloat16)  8.91 us
    dot_general x1, local copies, waits for them, and re-layouts, learn_core(): jnp.dot(slot_rows, weights_gu.reshape(model_width, 2 * hidden_count), pre...  8.86 us
    ppermute x2, waiting for transfers between devices, passed_along(): return lax.ppermute(block, axis, route)  8.29 us
    convert_element_type x2, local copies, waits for them, and re-layouts, replica_sum(): per_replica[replica].astype(jnp.bfloat16)  6.97 us
    dot_general x1, matrix products, learn_core(): jnp.einsum('pcd,pcgh->pdgh', slot_rows.reshape(rep_count, -1, model_width...  6.41 us
  transfers between devices with their start and end apart: 7, of which 6 were waited for; matrix products, arithmetic and copies ran while one was open for 13% of the time, Pallas kernels for 0%

profile of v2, /device:TPU:4, one launch (start us, length us, event | category | flops | bytes accessed | tf_op | source)
XLA Modules:
  0.0 310.7 jit_solution(6597335662577633)
XLA Ops:
  6.5 0.7 slice.44
  7.3 0.1 eq.69
  7.4 0.1 fusion.41
  7.5 0.2 reduce_window_sum.25
  7.7 0.2 select_reduce_fusion.1
  7.9 0.1 copy.50
  8.0 0.7 bitcast_add_fusion
  8.8 0.1 eq.62
  8.9 0.1 fusion.42
  9.0 0.2 reduce_window_sum.24
  9.2 0.2 select_reduce_fusion.3
  9.6 0.7 bitcast_select_fusion
  10.4 0.8 reduce-window.8
  11.2 0.7 bitcast_subtract_fusion
  11.8 0.7 select_reduce_fusion.4
  12.6 0.1 select_reduce_fusion.2
  12.7 2.3 convolution_convert_fusion.6.refs_0_
  15.0 3.0 convolution_convert_fusion.5.refs_1_
  18.0 59.5 %shard_map.91 = (bf16[128,4096]{1,0:T(8,128)(2,1)}, bf16[128,4096]{1,0:T(8,128)(2,1)}) custom-call(bf16[128,4096]{1,0:T(8,128)(2,1)} %convolution_convert_fusion.6.refs_0_, bf16[128,4096]{1,0:T(8,128)(2,1)} %convolution_convert_fusion.5.refs_1_), custom_call_target="tpu_custom_call" | custom-call | bytes 4194304 | tf_op jit(solution)/shard_map/pallas_call | solution.py:84
  77.6 0.7 all-gather.4.cloned.1.call-update
  78.3 6.5 %copy.63 = bf16[512,8,2,384]{3,1,2,0:T(8,128)(2,1)} copy(bf16[512,8,2,384]{3,2,1,0:T(2,128)(2,1)} %bitcast.137) | data formatting | bytes 12582912
  84.9 8.9 %copy.47 = bf16[768,4096]{1,0:T(8,128)(2,1)} copy(bf16[768,4096]{0,1:T(8,128)(2,1)} %bitcast.136) | data formatting | bytes 12582912 | tf_op jit(solution)/shard_map/dot_general | solution.py:156
  93.9 0.7 convert_reduce_fusion
  94.6 0.1 all-gather.6.cloned.1.call-done
  94.7 5.2 %fusion.17 = f32[256,2,384]{2,0,1:T(8,128)S(1)} fusion(bf16[2,384,4096]{2,1,0:T(8,128)(2,1)} %bitcast.140, bf16[256,4096]{1,0:T(8,128)(2,1)} %all-gather.6.cloned.1.call-done), kind=kOutput, calls=%fused_computation.31 | convolution fusion | flops 1610612736 | bytes 9175040 | tf_op jit(solution)/shard_map/dot_general | solution.py:156
  99.9 13.8 %all-gather.4.cloned.1.call-done = bf16[256,4096]{1,0:T(8,128)(2,1)} async-done(((bf16[128,4096]{1,0:T(8,128)(2,1)}), bf16[256,4096]{1,0:T(8,128)(2,1)}) %all-gather.4.cloned.1.call-update) | async-done | bytes 2097168 | tf_op jit(solution)/shard_map/all_gather | solution.py:212
  113.7 3.8 %fusion.32 = (bf16[256,384]{1,0:T(8,128)(2,1)S(1)}, bf16[256,384]{1,0:T(8,128)(2,1)S(1)}) fusion(f32[256,2,384]{2,0,1:T(8,128)S(1)} %fusion.17, bf16[256,4096]{1,0:T(8,128)(2,1)} %all-gather.4.cloned.1.call-done, bf16[1,1,384,4096]{3,2,1,0:T(8,128)(2,1)} %param.17), kind=kOutput, calls=%fused_computation.53 | convolution fusion | flops 806584320 | bytes 6422528 | tf_op jit(solution)/shard_map/dot_general | solution.py:166
  117.6 6.4 %convolution_convert_fusion = bf16[2,4096,2,384]{3,1,2,0:T(8,128)(2,1)} fusion(bf16[2,128,4096,1]{2,1,3,0:T(8,128)(2,1)S(1)} %bitcast.141, bf16[2,128,1,384]{3,1,2,0:T(8,128)(2,1)S(1)} %bitcast.147, bf16[2,128,1,384]{3,1,2,0:T(8,128)(2,1)S(1)} %bitcast.145), kind=kOutput, calls=%fused_computation.3 | convolution fusion | flops 1617690624 | bytes 15073280 | tf_op jit(solution)/shard_map/pcd,pcgh->pdgh/dot_general | solution.py:178
  124.0 6.2 %slice_bitcast_fusion.1 = (bf16[4096,2,384]{2,0,1:T(8,128)(2,1)S(1)}, bf16[4096,2,384]{2,0,1:T(8,128)(2,1)S(1)}) fusion(bf16[2,4096,2,384]{3,1,2,0:T(8,128)(2,1)} %convolution_convert_fusion), kind=kLoop, calls=%fused_computation.6 | loop fusion | bytes 25165824 | tf_op jit(solution)/shard_map/convert_element_type | solution.py:129
  130.2 2.0 multiply_reduce_fusion
  132.3 1.9 fusion.8
  134.2 0.2 copy-done.13
  134.4 1.3 fusion.11
  135.7 1.3 copy-done.3
  137.0 1.1 constant_dynamic-slice_fusion
  138.1 0.3 collective-permute-start
  138.4 5.1 %subtract_convert_fusion = bf16[4096,2,384]{2,0,1:T(8,128)(2,1)} fusion(bf16[4096,2,384]{2,0,1:T(8,128)(2,1)S(1)} %get-tuple-element.14, bf16[4096,2,384]{2,0,1:T(8,128)(2,1)S(1)} %get-tuple-element.13, f32[2,384]{1,0:T(2,128)S(1)} %add_sqrt_fusion, bf16[1,1,4096,2,384]{4,3,2,1,0:T(2,128)(2,1)S(1)} %bitcast.139), kind=kLoop, calls=%fused_computation | loop fusion | flops 25165824 | bytes 25168896 | tf_op jit(solution)/shard_map/convert_element_type | solution.py:137
  143.5 8.9 %copy.56 = bf16[4096,2,384]{0,2,1:T(8,128)(2,1)} copy(bf16[4096,2,384]{2,0,1:T(8,128)(2,1)} %subtract_convert_fusion) | data formatting | bytes 12582912 | tf_op jit(solution)/shard_map/convert_element_type | solution.py:137
  152.4 2.5 add_convert_fusion.1.refs_0_
  154.9 34.2 %shard_map.92 = bf16[128,4096]{1,0:T(8,128)(2,1)} custom-call(bf16[128,4096]{1,0:T(8,128)(2,1)} %add_convert_fusion.1.refs_0_), custom_call_target="tpu_custom_call" | custom-call | bytes 2097152 | tf_op jit(solution)/shard_map/pallas_call | solution.py:84
  189.2 1.9 fusion.12
  191.1 2.8 collective-permute-start.1
  193.8 1.2 fusion.57
  195.0 0.2 copy.58
  195.2 0.2 copy.59
  195.3 1.1 collective-permute-done.1
  196.4 2.1 convolution_convert_fusion.4.refs_0_
  198.5 32.2 %shard_map.93 = bf16[128,4096]{1,0:T(8,128)(2,1)} custom-call(bf16[128,4096]{1,0:T(8,128)(2,1)} %convolution_convert_fusion.4.refs_0_), custom_call_target="tpu_custom_call" | custom-call | bytes 2097152 | tf_op jit(solution)/shard_map/pallas_call | solution.py:84
  230.8 1.8 convolution_convert_fusion.1
  232.6 0.8 slice_bitcast_fusion.3
  233.4 1.7 copy-done
  235.1 1.1 multiply_reduce_fusion.1
  236.2 11.1 %all-gather.8.cloned.1.call-done = bf16[256,4096]{1,0:T(8,128)(2,1)} async-done(((bf16[128,4096]{1,0:T(8,128)(2,1)}), bf16[256,4096]{1,0:T(8,128)(2,1)}) %all-gather.8.cloned.1.call-update) | async-done | bytes 2097168 | tf_op jit(solution)/shard_map/all_gather | solution.py:212
  247.3 5.4 %fusion = f32[256,2,384]{2,0,1:T(8,128)S(1)} fusion(bf16[4096,2,384]{0,2,1:T(8,128)(2,1)} %copy.56, bf16[256,4096]{1,0:T(8,128)(2,1)} %all-gather.8.cloned.1.call-done), kind=kOutput, calls=%fused_computation.7 | convolution fusion | flops 1610612736 | bytes 9175040 | tf_op jit(solution)/shard_map/dot_general | solution.py:142
  252.7 2.2 convolution_convert_fusion.2
  254.9 0.1 constant_dynamic-slice_fusion.1
  255.0 0.4 collective-permute-start.2
  255.4 2.4 collective-permute-done.2
  257.7 1.2 add_convert_fusion.refs_0_
  259.0 34.3 %shard_map.94 = bf16[128,4096]{1,0:T(8,128)(2,1)} custom-call(bf16[128,4096]{1,0:T(8,128)(2,1)} %add_convert_fusion.refs_0_), custom_call_target="tpu_custom_call" | custom-call | bytes 2097152 | tf_op jit(solution)/shard_map/pallas_call | solution.py:84
  293.2 1.7 add_convert_fusion.2
  295.0 1.3 collective-permute-start.3
  296.3 7.2 %collective-permute-done.3 = bf16[16,4096]{1,0:T(8,128)(2,1)S(1)} collective-permute-done((bf16[16,4096]{1,0:T(8,128)(2,1)S(1)}, bf16[16,4096]{1,0:T(8,128)(2,1)S(1)}, u32[]{:S(2)}, u32[]{:S(2)}) %collective-permute-start.3) | collective-permute-done | bytes 131104 | tf_op jit(solution)/shard_map/ppermute | solution.py:105
  303.5 0.7 select_bitcast_fusion
  (53 shorter events, 0.9 us)
Async XLA Ops:
  6.5 88.1 %all-gather.6.cloned.1.call-start = ((), (), s32[]{:S(2)}) async-start(), calls=%async_computation.1 | async-start | bytes 3145728 | tf_op jit(solution)/shard_map/all_gather | solution.py:212
  12.6 72.3 %copy-start.11 = (f32[16]{0:T(128)}, f32[16]{0:T(128)S(1)}, u32[]{:S(2)}) copy-start(f32[16]{0:T(128)S(1)} %add_divide_fusion) | copy-start | bytes 196
  77.5 36.2 %all-gather.4.cloned.1.call-start = ((), (), s32[]{:S(2)}) async-start(), calls=%async_computation | async-start | bytes 3145728 | tf_op jit(solution)/shard_map/all_gather | solution.py:212
  78.3 169.0 %all-gather.8.cloned.1.call-start = ((), (), s32[]{:S(2)}) async-start(), calls=%async_computation.2 | async-start | bytes 3145728 | tf_op jit(solution)/shard_map/all_gather | solution.py:212
  84.9 8.9 %copy-start.10 = (f32[2,16,8]{1,2,0:T(8,128)S(1)}, f32[2,16,8]{1,2,0:T(8,128)}, u32[]{:S(2)}) copy-start(f32[2,16,8]{1,2,0:T(8,128)} %param.15) | copy-start | bytes 3076
  99.9 17.6 %copy-start.6 = (f32[256,2,384]{2,0,1:T(8,128)}, f32[256,2,384]{2,0,1:T(8,128)S(1)}, u32[]{:S(2)}) copy-start(f32[256,2,384]{2,0,1:T(8,128)S(1)} %fusion.17) | copy-start | bytes 2359300
  99.9 17.6 %copy-start.2 = (bf16[256,4096]{1,0:T(8,128)(2,1)S(1)}, bf16[256,4096]{1,0:T(8,128)(2,1)}, u32[]{:S(2)}) copy-start(bf16[256,4096]{1,0:T(8,128)(2,1)} %all-gather.6.cloned.1.call-done) | copy-start | bytes 6291460
  117.6 14.7 %slice-start = ((s8[6291456]{0:T(1024)(128)(4,1)}), s8[4194304]{0:T(1024)(128)(4,1)S(1)}, s32[]{:S(2)}) async-start(s8[6291456]{0:T(1024)(128)(4,1)} %bitcast.138), calls=%async_computation.3 | async-start | bytes 8388608
  124.0 8.3 %slice-start.1 = ((s8[6291456]{0:T(1024)(128)(4,1)}), s8[2097152]{0:T(1024)(128)(4,1)S(1)}, s32[]{:S(2)}) async-start(s8[6291456]{0:T(1024)(128)(4,1)} %bitcast.138), calls=%async_computation.4 | async-start | bytes 4194304
  132.3 1.9 copy-start.7
  132.3 2.1 copy-start.13
  135.7 1.3 copy-start.3
  138.1 14.3 %collective-permute-start = (bf16[128,4096]{1,0:T(8,128)(2,1)}, bf16[128,4096]{1,0:T(8,128)(2,1)}, u32[]{:S(2)}, u32[]{:S(2)}) collective-permute-start(bf16[128,4096]{1,0:T(8,128)(2,1)} %constant_dynamic-slice_fusion), channel_id=1, source_target_pairs={{0,1},{1,0},{2,3},{3,2},{4,5},{5,4},{6,7},{7,6},{8,9},{9,8},{10,11... | collective-permute-start | bytes 3145736 | tf_op jit(solution)/shard_map/ppermute | solution.py:219
  143.5 8.9 %copy-start.4 = (bf16[256,4096]{1,0:T(8,128)(2,1)S(1)}, bf16[256,4096]{1,0:T(8,128)(2,1)}, u32[]{:S(2)}) copy-start(bf16[256,4096]{1,0:T(8,128)(2,1)} %copy-done.3) | copy-start | bytes 6291460
  152.4 36.7 %copy-start.8 = (bf16[1,16,4096]{2,1,0:T(8,128)(2,1)S(1)}, bf16[1,16,4096]{2,1,0:T(8,128)(2,1)}, u32[]{:S(2)}) copy-start(bf16[1,16,4096]{2,1,0:T(8,128)(2,1)} %param.9) | copy-start | bytes 393220
  152.4 36.7 %copy-start.9 = (bf16[16,4096]{1,0:T(8,128)(2,1)S(1)}, bf16[16,4096]{1,0:T(8,128)(2,1)}, u32[]{:S(2)}) copy-start(bf16[16,4096]{1,0:T(8,128)(2,1)} %param.10) | copy-start | bytes 393220
  152.4 36.7 %copy-start.12 = (f32[16]{0:T(128)S(1)}, f32[16]{0:T(128)}, u32[]{:S(2)}) copy-start(f32[16]{0:T(128)} %copy-done.11) | copy-start | bytes 196
  189.2 41.6 %copy-start.5 = (bf16[256,4096]{1,0:T(8,128)(2,1)S(1)}, bf16[256,4096]{1,0:T(8,128)(2,1)}, u32[]{:S(2)}) copy-start(bf16[256,4096]{1,0:T(8,128)(2,1)} %all-gather.4.cloned.1.call-done) | copy-start | bytes 6291460
  191.1 5.3 %collective-permute-start.1 = (bf16[16,4096]{1,0:T(8,128)(2,1)S(1)}, bf16[16,4096]{1,0:T(8,128)(2,1)S(1)}, u32[]{:S(2)}, u32[]{:S(2)}) collective-permute-start(bf16[16,4096]{1,0:T(8,128)(2,1)S(1)} %fusion.12), channel_id=1, source_target_pairs={{128,0},{129,1},{130,2},{131,3},{132,4},{133,5},{134,6},{135,7},{1... | collective-permute-start | bytes 393224 | tf_op jit(solution)/shard_map/ppermute | solution.py:105
  233.4 1.7 copy-start
  247.3 5.4 %copy-start.1 = (bf16[384,4096]{1,0:T(8,128)(2,1)S(1)}, bf16[384,4096]{1,0:T(8,128)(2,1)}, u32[]{:S(2)}) copy-start(bf16[384,4096]{1,0:T(8,128)(2,1)} %copy-done) | copy-start | bytes 9437188
  247.3 5.4 %copy-start.14 = (bf16[1,1,384,4096]{3,2,1,0:T(8,128)(2,1)S(1)}, bf16[1,1,384,4096]{3,2,1,0:T(8,128)(2,1)}, u32[]{:S(2)}) copy-start(bf16[1,1,384,4096]{3,2,1,0:T(8,128)(2,1)} %param.17) | copy-start | bytes 9437188
  255.0 2.7 collective-permute-start.2
  295.0 8.5 %collective-permute-start.3 = (bf16[16,4096]{1,0:T(8,128)(2,1)S(1)}, bf16[16,4096]{1,0:T(8,128)(2,1)S(1)}, u32[]{:S(2)}, u32[]{:S(2)}) collective-permute-start(bf16[16,4096]{1,0:T(8,128)(2,1)S(1)} %add_convert_fusion.2), channel_id=1, source_target_pairs={{0,128},{1,129},{2,130},{3,131},{4,132},{5,133},{6,134},{7,135},{8... | collective-permute-start | bytes 393224 | tf_op jit(solution)/shard_map/ppermute | solution.py:105
Sparse Core Ops, SparseCore 0:
  77.6 16.9 all-gather.5
  96.5 17.1 all-gather.3
  230.9 16.3 all-gather.7

commit v3 on v2

--- a/solution.py
+++ b/solution.py
@@ -9,11 +9,14 @@
 MESH = pl.DeviceIdType.MESH
 
 
-def exchange_kernel(count, width, *refs):
+def exchange_kernel(count, width, share, *refs):
     parts = len(refs) // 2 - 1
     sources, targets = refs[:parts], refs[parts:2 * parts]
     send_sem, recv_sem, own_sem = refs[2 * parts:]
     me = lax.axis_index("ep")
+    rows = count * width
+    side = lax.axis_index("dp")
+    base = side * rows if share else 0
     barrier = pltpu.get_barrier_semaphore()
 
     def greet(k, carry):
@@ -22,19 +25,26 @@
         return carry
 
     lax.fori_loop(1, count, greet, 0)
-    pl.semaphore_wait(barrier, count - 1)
+    if share:
+        pl.semaphore_signal(barrier, inc=1, device_id={"dp": 1 - side}, device_id_type=MESH)
+    pl.semaphore_wait(barrier, count - 1 + (1 if share else 0))
+
+    def spot(index, start=0):
+        return pl.ds(pl.multiple_of(start + index * width, width), width)
+
     owns = []
     for part in range(parts):
-        here = pl.ds(pl.multiple_of(me * width, width), width)
-        own = pltpu.make_async_copy(sources[part].at[here], targets[part].at[here], own_sem.at[part])
+        own = pltpu.make_async_copy(
+            sources[part].at[spot(me)], targets[part].at[spot(me, base)], own_sem.at[part, 0]
+        )
         own.start()
         owns.append(own)
 
     def outgoing(part, k):
         other = lax.rem(me + k, count)
         return pltpu.make_async_remote_copy(
-            src_ref=sources[part].at[pl.ds(pl.multiple_of(other * width, width), width)],
-            dst_ref=targets[part].at[pl.ds(pl.multiple_of(me * width, width), width)],
+            src_ref=sources[part].at[spot(other)],
+            dst_ref=targets[part].at[spot(me, base)],
             send_sem=send_sem.at[part, other],
             recv_sem=recv_sem.at[part, me],
             device_id={"ep": other},
@@ -43,10 +53,9 @@
 
     def incoming(part, k):
         other = lax.rem(me + count - k, count)
-        there = pl.ds(pl.multiple_of(other * width, width), width)
         return pltpu.make_async_remote_copy(
-            src_ref=sources[part].at[there],
-            dst_ref=targets[part].at[there],
+            src_ref=sources[part].at[spot(other)],
+            dst_ref=targets[part].at[spot(other, base)],
             send_sem=send_sem.at[part, other],
             recv_sem=recv_sem.at[part, other],
             device_id={"ep": other},
@@ -75,24 +84,55 @@
     lax.fori_loop(1, count, land, 0)
     for own in owns:
         own.wait()
-
-
-def exchange(blocks, count, tag):
+    if share:
+        half = pl.ds(pl.multiple_of(base, rows), rows)
+        yonder = pl.ds(pl.multiple_of((1 - side) * rows, rows), rows)
+        passes = []
+        for part in range(parts):
+            onward = pltpu.make_async_remote_copy(
+                src_ref=targets[part].at[half],
+                dst_ref=targets[part].at[half],
+                send_sem=own_sem.at[part, 1],
+                recv_sem=own_sem.at[part, 2],
+                device_id={"dp": 1 - side},
+                device_id_type=MESH,
+            )
+            onward.start()
+            passes.append(onward)
+        for part in range(parts):
+            passes[part].wait_send()
+            pltpu.make_async_remote_copy(
+                src_ref=targets[part].at[yonder],
+                dst_ref=targets[part].at[yonder],
+                send_sem=own_sem.at[part, 1],
+                recv_sem=own_sem.at[part, 2],
+                device_id={"dp": 1 - side},
+                device_id_type=MESH,
+            ).wait_recv()
+
+
+def exchange(blocks, count, tag, share=False):
     parts = len(blocks)
     width = blocks[0].shape[0] // count
+    grow = 2 if share else 1
     size = sum(block.size * block.dtype.itemsize for block in blocks)
     return pl.pallas_call(
-        functools.partial(exchange_kernel, count, width),
-        out_shape=[jax.ShapeDtypeStruct(block.shape, block.dtype) for block in blocks],
+        functools.partial(exchange_kernel, count, width, share),
+        out_shape=[
+            jax.ShapeDtypeStruct((grow * block.shape[0],) + block.shape[1:], block.dtype)
+            for block in blocks
+        ],
         in_specs=[pl.BlockSpec(memory_space=pl.ANY)] * parts,
         out_specs=[pl.BlockSpec(memory_space=pl.ANY)] * parts,
         scratch_shapes=[
             pltpu.SemaphoreType.DMA((parts, count)),
             pltpu.SemaphoreType.DMA((parts, count)),
-            pltpu.SemaphoreType.DMA((parts,)),
+            pltpu.SemaphoreType.DMA((parts, 3)),
         ],
         compiler_params=pltpu.CompilerParams(collective_id=tag, has_side_effects=True),
-        cost_estimate=pl.CostEstimate(flops=0, transcendentals=0, bytes_accessed=2 * size),
+        cost_estimate=pl.CostEstimate(
+            flops=0, transcendentals=0, bytes_accessed=(2 + 2 * grow) * size
+        ),
     )(*blocks)
 
 
@@ -208,8 +248,7 @@
     hidden_all = own_gu.shape[2] * dp_count
 
     def spread(buffers, tag):
-        arrived = exchange(buffers, ep_count, tag)
-        return [lax.all_gather(block, "dp", axis=0, tiled=True) for block in arrived]
+        return exchange(buffers, ep_count, tag, share=True)
 
     def bring_back(pieces, tag):
         half = pieces.shape[0] // dp_count

time: 312 us -> 280 us (0.90)
  waiting for transfers between devices: 36.3 us -> 9.38 us
  between operations: 13.5 us -> 0.45 us
  Pallas kernels: 160 us -> 166 us
    all_gather x3 -> x0, waiting for transfers between devices: 24.9 us -> none  [spread(): lax.all_gather(block, 'dp', axis=0, tiled=True)]
    pallas_call x4, Pallas kernels: 160 us -> 166 us  [exchange(): pl.pallas_call(functools.partial(exchange_kernel, count, width, share), o...]
    unnamed x35 -> x37, local copies, waits for them, and re-layouts: 9.76 us -> 7.4 us
  transfers between devices with their start and end apart: 7 -> 4, of which waited for: 6 -> 2; matrix products, arithmetic and copies ran while one was open for 13% -> 14% of each run, Pallas kernels for 0% -> 0%
where the time goes in v3:
time: 280 us; the launch traced here: 279 us
  Pallas kernels  166 us (59%)
  local copies, waits for them, and re-layouts  39.3 us (14%)
  matrix products  38.8 us (14%)
  other arithmetic  19.3 us (7%)
  waiting for transfers between devices  9.38 us (3%)
  starting transfers between devices  5.08 us (2%)
    pallas_call x4, Pallas kernels, exchange(): pl.pallas_call(functools.partial(exchange_kernel, count, width, share), o...  166 us
    dot_general x1, local copies, waits for them, and re-layouts, learn_core(): jnp.dot(slot_rows, weights_gu.reshape(model_width, 2 * hidden_count), pre...  8.8 us
    convert_element_type x1, local copies, waits for them, and re-layouts, renew(): (weights.astype(jnp.float32) - rate * grads / scale).astype(jnp.bfloat16)  8.62 us
    convert_element_type x2, local copies, waits for them, and re-layouts, replica_sum(): per_replica[replica].astype(jnp.bfloat16)  8.32 us
    dot_general x1, matrix products, learn_core(): jnp.einsum('pcd,pcgh->pdgh', slot_rows.reshape(rep_count, -1, model_width...  7.47 us
    unnamed x37, local copies, waits for them, and re-layouts  7.4 us
    ppermute x2, waiting for transfers between devices, passed_along(): return lax.ppermute(block, axis, route)  7.09 us
  transfers between devices with their start and end apart: 4, of which 2 were waited for; matrix products, arithmetic and copies ran while one was open for 14% of the time, Pallas kernels for 0%

profile of v3, /device:TPU:4, one launch (start us, length us, event | category | flops | bytes accessed | tf_op | source)
XLA Modules:
  0.0 278.7 jit_solution(2991166830191188584)
XLA Ops:
  0.0 0.7 slice.44
  0.7 0.1 copy.49
  0.8 0.1 eq.69
  0.9 0.1 fusion.41
  1.0 0.2 reduce_window_sum.25
  1.1 0.2 select_reduce_fusion.1
  1.3 0.1 reduce_sum.91
  1.4 0.1 copy.50
  1.5 0.7 bitcast_add_fusion
  2.3 0.1 eq.62
  2.4 0.1 fusion.42
  2.4 0.2 reduce_window_sum.24
  2.6 0.2 select_reduce_fusion.3
  2.8 0.1 reduce_sum.87
  2.9 0.1 copy.44
  3.0 0.1 copy.45
  3.0 0.7 bitcast_select_fusion
  3.7 0.1 copy.46
  3.8 0.8 reduce-window.8
  4.6 0.7 bitcast_subtract_fusion
  5.3 0.7 select_reduce_fusion.4
  6.1 6.5 %copy.63 = bf16[512,8,2,384]{3,1,2,0:T(8,128)(2,1)} copy(bf16[512,8,2,384]{3,2,1,0:T(2,128)(2,1)} %bitcast.137) | data formatting | bytes 12582912
  12.6 8.8 %copy.47 = bf16[768,4096]{1,0:T(8,128)(2,1)} copy(bf16[768,4096]{0,1:T(8,128)(2,1)} %bitcast.136) | data formatting | bytes 12582912 | tf_op jit(solution)/shard_map/dot_general | solution.py:196
  21.4 0.1 select_reduce_fusion.2
  21.5 1.5 convolution_convert_fusion.6.refs_0_
  23.1 2.1 convolution_convert_fusion.5.refs_1_
  25.1 63.6 %shard_map.91 = (bf16[256,4096]{1,0:T(8,128)(2,1)}, bf16[256,4096]{1,0:T(8,128)(2,1)}) custom-call(bf16[128,4096]{1,0:T(8,128)(2,1)} %convolution_convert_fusion.6.refs_0_, bf16[128,4096]{1,0:T(8,128)(2,1)} %convolution_convert_fusion.5.refs_1_), custom_call_target="tpu_custom_call" | custom-call | bytes 12582912 | tf_op jit(solution)/shard_map/pallas_call | solution.py:119
  88.8 5.4 %fusion.17 = f32[256,2,384]{2,0,1:T(8,128)S(1)} fusion(bf16[2,384,4096]{2,1,0:T(8,128)(2,1)} %bitcast.142, bf16[256,4096]{1,0:T(8,128)(2,1)} %get-tuple-element.8), kind=kOutput, calls=%fused_computation.31 | convolution fusion | flops 1610612736 | bytes 9175040 | tf_op jit(solution)/shard_map/dot_general | solution.py:196
  94.2 1.3 fusion.32
  95.6 1.8 fusion.8
  97.5 2.6 fusion.11
  100.1 2.3 constant_dynamic-slice_fusion
  102.4 0.4 collective-permute-start
  102.8 0.8 fusion.57
  103.6 7.5 %convolution_convert_fusion = bf16[2,4096,2,384]{3,1,2,0:T(8,128)(2,1)} fusion(bf16[2,128,4096,1]{2,1,3,0:T(8,128)(2,1)S(1)} %bitcast.143, bf16[2,128,1,384]{3,1,2,0:T(8,128)(2,1)} %bitcast.150, bf16[2,128,1,384]{3,1,2,0:T(8,128)(2,1)} %bitcast.148), kind=kOutput, calls=%fused_computation.3 | convolution fusion | flops 1617690624 | bytes 15073280 | tf_op jit(solution)/shard_map/pcd,pcgh->pdgh/dot_general | solution.py:218
  111.1 6.0 %slice_bitcast_fusion.1 = (bf16[4096,2,384]{2,0,1:T(8,128)(2,1)S(1)}, bf16[4096,2,384]{2,0,1:T(8,128)(2,1)S(1)}) fusion(bf16[2,4096,2,384]{3,1,2,0:T(8,128)(2,1)} %convolution_convert_fusion), kind=kLoop, calls=%fused_computation.6 | loop fusion | bytes 25165824 | tf_op jit(solution)/shard_map/convert_element_type | solution.py:169
  117.1 2.0 multiply_reduce_fusion
  119.2 0.1 slice-done.2
  119.3 0.7 slice-done.3
  120.0 5.0 %subtract_convert_fusion = bf16[4096,2,384]{2,0,1:T(8,128)(2,1)} fusion(bf16[4096,2,384]{2,0,1:T(8,128)(2,1)S(1)} %get-tuple-element.14, bf16[4096,2,384]{2,0,1:T(8,128)(2,1)S(1)} %get-tuple-element.13, f32[2,384]{1,0:T(2,128)S(1)} %add_sqrt_fusion, bf16[1,1,4096,2,384]{4,3,2,1,0:T(2,128)(2,1)S(1)} %bitcast.141), kind=kLoop, calls=%fused_computation | loop fusion | flops 25165824 | bytes 25168896 | tf_op jit(solution)/shard_map/convert_element_type | solution.py:177
  124.9 1.1 copy.58
  126.1 0.2 copy.59
  126.3 3.4 %convolution_convert_fusion.1 = bf16[2,384,4096]{2,1,0:T(8,128)(2,1)S(1)} fusion(bf16[2,128,4096]{2,1,0:T(8,128)(2,1)} %bitcast.144, f32[2,128,384]{1,2,0:T(8,128)S(1)} %copy.59, f32[2,128,384]{1,2,0:T(8,128)S(1)} %copy.58), kind=kOutput, calls=%fused_computation.4 | convolution fusion | flops 809041920 | bytes 9175040 | tf_op jit(solution)/shard_map/pch,pcd->phd/dot_general | solution.py:212
  129.7 2.3 slice_bitcast_fusion.3
  132.0 3.1 %multiply_reduce_fusion.1 = f32[384]{0:T(512)S(1)} fusion(bf16[384,4096]{1,0:T(8,128)(2,1)} %get-tuple-element.16, bf16[384,4096]{1,0:T(8,128)(2,1)S(1)} %get-tuple-element.15), kind=kLoop, calls=%fused_computation.12 | loop fusion | flops 7863936 | bytes 6292992 | tf_op jit(solution)/shard_map/reduce_sum | solution.py:176
  135.2 2.5 add_convert_fusion.1.refs_0_
  137.7 33.7 %shard_map.92 = bf16[128,4096]{1,0:T(8,128)(2,1)} custom-call(bf16[128,4096]{1,0:T(8,128)(2,1)} %add_convert_fusion.1.refs_0_), custom_call_target="tpu_custom_call" | custom-call | bytes 4194304 | tf_op jit(solution)/shard_map/pallas_call | solution.py:119
  171.4 2.4 fusion.12
  173.8 3.0 %collective-permute-start.1 = (bf16[16,4096]{1,0:T(8,128)(2,1)}, bf16[16,4096]{1,0:T(8,128)(2,1)S(1)}, u32[]{:S(2)}, u32[]{:S(2)}) collective-permute-start(bf16[16,4096]{1,0:T(8,128)(2,1)} %fusion.12), channel_id=1, source_target_pairs={{128,0},{129,1},{130,2},{131,3},{132,4},{133,5},{134,6},{135,7},{1... | collective-permute-start | bytes 393224 | tf_op jit(solution)/shard_map/ppermute | solution.py:145
  176.8 8.6 %copy.56 = bf16[4096,2,384]{0,2,1:T(8,128)(2,1)} copy(bf16[4096,2,384]{2,0,1:T(8,128)(2,1)} %subtract_convert_fusion) | data formatting | bytes 12582912 | tf_op jit(solution)/shard_map/convert_element_type | solution.py:177
  185.5 0.1 convert_reduce_fusion
  185.7 1.4 convolution_convert_fusion.4.refs_0_
  187.1 35.5 %shard_map.93 = bf16[256,4096]{1,0:T(8,128)(2,1)} custom-call(bf16[128,4096]{1,0:T(8,128)(2,1)} %convolution_convert_fusion.4.refs_0_), custom_call_target="tpu_custom_call" | custom-call | bytes 6291456 | tf_op jit(solution)/shard_map/pallas_call | solution.py:119
  222.6 5.4 %fusion = f32[256,2,384]{2,0,1:T(8,128)S(1)} fusion(bf16[4096,2,384]{0,2,1:T(8,128)(2,1)} %copy.56, bf16[256,4096]{1,0:T(8,128)(2,1)} %shard_map.93), kind=kOutput, calls=%fused_computation.7 | convolution fusion | flops 1610612736 | bytes 9175040 | tf_op jit(solution)/shard_map/dot_general | solution.py:182
  228.0 2.2 convolution_convert_fusion.2
  230.2 0.1 constant_dynamic-slice_fusion.1
  230.3 0.5 collective-permute-start.2
  230.7 2.3 collective-permute-done.2
  233.0 1.2 add_convert_fusion.refs_0_
  234.3 33.6 %shard_map.94 = bf16[128,4096]{1,0:T(8,128)(2,1)} custom-call(bf16[128,4096]{1,0:T(8,128)(2,1)} %add_convert_fusion.refs_0_), custom_call_target="tpu_custom_call" | custom-call | bytes 4194304 | tf_op jit(solution)/shard_map/pallas_call | solution.py:119
  267.9 1.7 add_convert_fusion.2
  269.6 1.3 collective-permute-start.3
  270.9 7.1 %collective-permute-done.3 = bf16[16,4096]{1,0:T(8,128)(2,1)S(1)} collective-permute-done((bf16[16,4096]{1,0:T(8,128)(2,1)S(1)}, bf16[16,4096]{1,0:T(8,128)(2,1)S(1)}, u32[]{:S(2)}, u32[]{:S(2)}) %collective-permute-start.3) | collective-permute-done | bytes 131104 | tf_op jit(solution)/shard_map/ppermute | solution.py:145
  278.0 0.7 select_bitcast_fusion
  (47 shorter events, 0.3 us)
Async XLA Ops:
  6.1 17.0 %copy-start.10 = (f32[16]{0:T(128)}, f32[16]{0:T(128)S(1)}, u32[]{:S(2)}) copy-start(f32[16]{0:T(128)S(1)} %add_divide_fusion) | copy-start | bytes 196
  12.6 8.9 %copy-start.4 = (bf16[1,16,4096]{2,1,0:T(8,128)(2,1)S(1)}, bf16[1,16,4096]{2,1,0:T(8,128)(2,1)}, u32[]{:S(2)}) copy-start(bf16[1,16,4096]{2,1,0:T(8,128)(2,1)} %param.9) | copy-start | bytes 393220
  12.6 10.5 %copy-start.5 = (bf16[16,4096]{1,0:T(8,128)(2,1)S(1)}, bf16[16,4096]{1,0:T(8,128)(2,1)}, u32[]{:S(2)}) copy-start(bf16[16,4096]{1,0:T(8,128)(2,1)} %param.10) | copy-start | bytes 393220
  25.1 70.5 %slice-start = ((s8[6291456]{0:T(1024)(128)(4,1)}), s8[2097152]{0:T(1024)(128)(4,1)S(1)}, s32[]{:S(2)}) async-start(s8[6291456]{0:T(1024)(128)(4,1)} %bitcast.138), calls=%async_computation | async-start | bytes 4194304
  88.8 5.4 %copy-start.3 = (bf16[256,4096]{1,0:T(8,128)(2,1)S(1)}, bf16[256,4096]{1,0:T(8,128)(2,1)}, u32[]{:S(2)}) copy-start(bf16[256,4096]{1,0:T(8,128)(2,1)} %get-tuple-element.7) | copy-start | bytes 6291460
  88.8 5.4 %copy-start.12 = (bf16[1,1,384,4096]{3,2,1,0:T(8,128)(2,1)S(1)}, bf16[1,1,384,4096]{3,2,1,0:T(8,128)(2,1)}, u32[]{:S(2)}) copy-start(bf16[1,1,384,4096]{3,2,1,0:T(8,128)(2,1)} %param.17) | copy-start | bytes 9437188
  88.8 6.8 %slice-start.1 = ((s8[6291456]{0:T(1024)(128)(4,1)}), s8[4194304]{0:T(1024)(128)(4,1)S(1)}, s32[]{:S(2)}) async-start(s8[6291456]{0:T(1024)(128)(4,1)} %bitcast.138), calls=%async_computation.1 | async-start | bytes 8388608
  95.5 1.9 copy-start.7
  95.6 1.9 copy-start.8
  97.5 6.1 %copy-start.1 = (bf16[256,4096]{1,0:T(8,128)(2,1)S(1)}, bf16[256,4096]{1,0:T(8,128)(2,1)}, u32[]{:S(2)}) copy-start(bf16[256,4096]{1,0:T(8,128)(2,1)} %get-tuple-element.8) | copy-start | bytes 6291460
  102.4 32.7 %collective-permute-start = (bf16[128,4096]{1,0:T(8,128)(2,1)}, bf16[128,4096]{1,0:T(8,128)(2,1)}, u32[]{:S(2)}, u32[]{:S(2)}) collective-permute-start(bf16[128,4096]{1,0:T(8,128)(2,1)} %constant_dynamic-slice_fusion), channel_id=1, source_target_pairs={{0,1},{1,0},{2,3},{3,2},{4,5},{5,4},{6,7},{7,6},{8,9},{9,8},{10,11... | collective-permute-start | bytes 3145736 | tf_op jit(solution)/shard_map/ppermute | solution.py:258
  117.1 2.2 slice-start.2
  117.1 2.9 %slice-start.3 = ((s8[6291456]{0:T(1024)(128)(4,1)}), s8[2097152]{0:T(1024)(128)(4,1)S(1)}, s32[]{:S(2)}) async-start(s8[6291456]{0:T(1024)(128)(4,1)} %bitcast.140), calls=%async_computation.3 | async-start | bytes 4194304
  129.7 2.3 copy-start.9
  132.0 3.2 %copy-start.2 = (bf16[256,4096]{1,0:T(8,128)(2,1)S(1)}, bf16[256,4096]{1,0:T(8,128)(2,1)}, u32[]{:S(2)}) copy-start(bf16[256,4096]{1,0:T(8,128)(2,1)} %fusion.11) | copy-start | bytes 6291460
  135.1 36.2 %copy-start.6 = (bf16[16,4096]{1,0:T(8,128)(2,1)S(1)}, bf16[16,4096]{1,0:T(8,128)(2,1)}, u32[]{:S(2)}) copy-start(bf16[16,4096]{1,0:T(8,128)(2,1)} %param.10) | copy-start | bytes 393220
  135.1 36.2 %copy-start.11 = (f32[16]{0:T(128)S(1)}, f32[16]{0:T(128)}, u32[]{:S(2)}) copy-start(f32[16]{0:T(128)} %copy-done.10) | copy-start | bytes 196
  173.8 11.9 %collective-permute-start.1 = (bf16[16,4096]{1,0:T(8,128)(2,1)}, bf16[16,4096]{1,0:T(8,128)(2,1)S(1)}, u32[]{:S(2)}, u32[]{:S(2)}) collective-permute-start(bf16[16,4096]{1,0:T(8,128)(2,1)} %fusion.12), channel_id=1, source_target_pairs={{128,0},{129,1},{130,2},{131,3},{132,4},{133,5},{134,6},{135,7},{1... | collective-permute-start | bytes 393224 | tf_op jit(solution)/shard_map/ppermute | solution.py:145
  222.6 5.4 %copy-start = (bf16[384,4096]{1,0:T(8,128)(2,1)S(1)}, bf16[384,4096]{1,0:T(8,128)(2,1)}, u32[]{:S(2)}) copy-start(bf16[384,4096]{1,0:T(8,128)(2,1)} %get-tuple-element.16) | copy-start | bytes 9437188
  222.6 5.4 %copy-start.13 = (bf16[1,1,384,4096]{3,2,1,0:T(8,128)(2,1)S(1)}, bf16[1,1,384,4096]{3,2,1,0:T(8,128)(2,1)}, u32[]{:S(2)}) copy-start(bf16[1,1,384,4096]{3,2,1,0:T(8,128)(2,1)} %param.17) | copy-start | bytes 9437188
  230.3 2.7 collective-permute-start.2
  269.6 8.4 %collective-permute-start.3 = (bf16[16,4096]{1,0:T(8,128)(2,1)S(1)}, bf16[16,4096]{1,0:T(8,128)(2,1)S(1)}, u32[]{:S(2)}, u32[]{:S(2)}) collective-permute-start(bf16[16,4096]{1,0:T(8,128)(2,1)S(1)} %add_convert_fusion.2), channel_id=1, source_target_pairs={{0,128},{1,129},{2,130},{3,131},{4,132},{5,133},{6,134},{7,135},{8... | collective-permute-start | bytes 393224 | tf_op jit(solution)/shard_map/ppermute | solution.py:145

commit v4 on v3

--- a/solution.py
+++ b/solution.py
@@ -178,11 +178,9 @@
 
 
 def forward_core(slot_rows, weights_gu, weights_dn):
-    hidden_count = weights_gu.shape[2]
-    both = jnp.dot(
-        slot_rows,
-        weights_gu.reshape(slot_rows.shape[1], 2 * hidden_count),
-        preferred_element_type=jnp.float32,
+    hidden_count = weights_gu.shape[0] // 2
+    both = lax.dot_general(
+        slot_rows, weights_gu, (((1,), (1,)), ((), ())), preferred_element_type=jnp.float32
     ).reshape(-1, 2, hidden_count)
     active = both[:, 0]
     upward = both[:, 1]
@@ -192,11 +190,9 @@
 
 def learn_core(slot_rows, slot_grads, weights_gu, weights_dn, rep_count):
     slot_count, model_width = slot_rows.shape
-    hidden_count = weights_gu.shape[2]
-    both = jnp.dot(
-        slot_rows,
-        weights_gu.reshape(model_width, 2 * hidden_count),
-        preferred_element_type=jnp.float32,
+    hidden_count = weights_gu.shape[0] // 2
+    both = lax.dot_general(
+        slot_rows, weights_gu, (((1,), (1,)), ((), ())), preferred_element_type=jnp.float32
     ).reshape(slot_count, 2, hidden_count)
     active = both[:, 0]
     upward = both[:, 1]
@@ -216,12 +212,14 @@
         preferred_element_type=jnp.float32,
     )
     grad_gu = jnp.einsum(
-        "pcd,pcgh->pdgh",
+        "pcj,pcd->pjd",
+        d_both.reshape(rep_count, -1, 2 * hidden_count),
         slot_rows.reshape(rep_count, -1, model_width),
-        d_both.reshape(rep_count, -1, 2, hidden_count),
         preferred_element_type=jnp.float32,
     )
-    slot_dx = jnp.einsum("mgh,dgh->md", d_both, weights_gu, preferred_element_type=jnp.float32)
+    slot_dx = jnp.dot(
+        d_both.reshape(slot_count, 2 * hidden_count), weights_gu, preferred_element_type=jnp.float32
+    )
     slot_fw = jnp.dot(hidden, weights_dn, preferred_element_type=jnp.float32)
     return (grad_gu, grad_dn, slot_dx.astype(jnp.bfloat16), slot_fw.astype(jnp.bfloat16))
 
@@ -243,9 +241,9 @@
     top_count = train_experts.shape[1]
     capacity = min(row_count, max(2, 4 * row_count * top_count // (3 * ep_count)))
     is_learner = lax.axis_index("grp") == 0
-    own_gu = gate_up[0, 0]
+    own_gu = gate_up[0, 0].reshape(gate_up.shape[2], -1).T
     own_dn = down[0, 0]
-    hidden_all = own_gu.shape[2] * dp_count
+    hidden_all = own_dn.shape[0] * dp_count
 
     def spread(buffers, tag):
         return exchange(buffers, ep_count, tag, share=True)
@@ -295,7 +293,7 @@
     mixing = jnp.where(is_learner, picker, weigher)
     base = jnp.where(is_learner, weight[:, None] * cot_wide, tokens.astype(jnp.float32))
     carried = (base + combine(mixing, returned)).astype(jnp.bfloat16)
-    fresh_gu = renew(own_gu, grad_gu, 0, 0.5 / model_width**0.5)
+    fresh_gu = renew(own_gu, grad_gu, 1, 0.5 / model_width**0.5)
     fresh_dn = renew(own_dn, grad_dn, 1, 0.5 / hidden_all**0.5)
     current = passed_along(carried, "grp", -1)
     picker, weigher = routing_tables(decode_experts[1], decode_gates[1], capacity, ep_count)

time: 280 us -> 290 us (1.036)
  other arithmetic: 19.3 us -> 27.3 us
  matrix products: 38.8 us -> 42 us
    unnamed x37 -> x39, local copies, waits for them, and re-layouts: 7.4 us -> 19.1 us
    dot_general x1 -> x0, local copies, waits for them, and re-layouts: 8.8 us -> none  [learn_core(): jnp.dot(slot_rows, weights_gu.reshape(model_width, 2 * hidden_count), pre...]
    convert_element_type x1 -> x3, local copies, waits for them, and re-layouts: 8.62 us -> 0.83 us  [learn_core(): d_both = jnp.stack([d_active, d_upward], axis=1).astype(jnp.bfloat16)]
    reduce_sum x2, other arithmetic: 5.17 us -> 8.62 us  [renew(): jnp.mean(grads * grads, axis=axis_number, keepdims=True) + EPSILON]
    convert_element_type x1, other arithmetic: 4.96 us -> 8.16 us  [renew(): (weights.astype(jnp.float32) - rate * grads / scale).astype(jnp.bfloat16)]
    dot_general x1, matrix products: 2.16 us -> 5.22 us  [forward_core(): jnp.dot(hidden, weights_dn, preferred_element_type=jnp.float32)]
  transfers between devices with their start and end apart: 4 -> 4, of which waited for: 2 -> 3; matrix products, arithmetic and copies ran while one was open for 14% -> 14% of each run, Pallas kernels for 0% -> 0%
where the time goes in v4:
time: 290 us; the launch traced here: 289 us
  Pallas kernels  166 us (57%)
  matrix products  42 us (14%)
  local copies, waits for them, and re-layouts  38.7 us (13%)
  other arithmetic  27.3 us (9%)
  waiting for transfers between devices  9.7 us (3%)
  starting transfers between devices  5.07 us (2%)
    pallas_call x4, Pallas kernels, exchange(): pl.pallas_call(functools.partial(exchange_kernel, count, width, share), o...  166 us
    unnamed x39, local copies, waits for them, and re-layouts  19.1 us
    convert_element_type x2, local copies, waits for them, and re-layouts, replica_sum(): per_replica[replica].astype(jnp.bfloat16)  10.7 us
    reduce_sum x2, other arithmetic, renew(): jnp.mean(grads * grads, axis=axis_number, keepdims=True) + EPSILON  8.62 us
    convert_element_type x1, other arithmetic, renew(): (weights.astype(jnp.float32) - rate * grads / scale).astype(jnp.bfloat16)  8.16 us
    ppermute x2, waiting for transfers between devices, passed_along(): return lax.ppermute(block, axis, route)  7.41 us
    dot_general x1, matrix products, learn_core(): jnp.einsum('pcj,pcd->pjd', d_both.reshape(rep_count, -1, 2 * hidden_count...  6.43 us
  transfers between devices with their start and end apart: 4, of which 3 were waited for; matrix products, arithmetic and copies ran while one was open for 14% of the time, Pallas kernels for 0%

profile of v4, /device:TPU:4, one launch (start us, length us, event | category | flops | bytes accessed | tf_op | source)
XLA Modules:
  0.0 289.2 jit_solution(16062850510653622844)
XLA Ops:
  0.0 0.7 slice.44
  0.8 0.1 eq.69
  0.9 0.1 fusion.26
  1.0 0.2 reduce_window_sum.25
  1.1 0.2 select_reduce_fusion.1
  1.5 1.3 bitcast_add_fusion
  2.8 0.1 eq.62
  2.9 0.1 fusion.27
  3.0 0.2 reduce_window_sum.24
  3.2 0.2 select_reduce_fusion.3
  3.6 0.7 bitcast_select_fusion
  4.4 0.8 reduce-window.8
  5.2 0.7 bitcast_subtract_fusion
  5.9 0.7 select_reduce_fusion.4
  6.7 16.3 %copy.44 = bf16[1,1,4096,2,384]{2,4,3,1,0:T(8,128)(2,1)} copy(bf16[1,1,4096,2,384]{4,3,2,1,0:T(2,128)(2,1)} %param.16) | data formatting | bytes 12582912 | tf_op args[7]
  22.9 0.1 select_reduce_fusion.2
  23.1 1.4 convolution_convert_fusion.7.refs_0_
  24.5 2.1 convolution_convert_fusion.6.refs_1_
  26.6 63.6 %shard_map.91 = (bf16[256,4096]{1,0:T(8,128)(2,1)}, bf16[256,4096]{1,0:T(8,128)(2,1)}) custom-call(bf16[128,4096]{1,0:T(8,128)(2,1)} %convolution_convert_fusion.7.refs_0_, bf16[128,4096]{1,0:T(8,128)(2,1)} %convolution_convert_fusion.6.refs_1_), custom_call_target="tpu_custom_call" | custom-call | bytes 12582912 | tf_op jit(solution)/shard_map/pallas_call | solution.py:119
  90.2 5.4 %fusion = f32[256,2,384]{2,0,1:T(8,128)S(1)} fusion(bf16[1,1,4096,2,384]{2,4,3,1,0:T(8,128)(2,1)} %copy.44, bf16[256,4096]{1,0:T(8,128)(2,1)} %get-tuple-element.8), kind=kOutput, calls=%fused_computation.7 | convolution fusion | flops 1610612736 | bytes 9175040 | tf_op jit(solution)/shard_map/dot_general | solution.py:194
  95.7 1.3 fusion.17
  97.0 0.2 copy.45
  97.2 4.8 %convolution_convert_fusion.4 = bf16[256,4096]{1,0:T(8,128)(2,1)S(1)} fusion(bf16[256,768]{0,1:T(8,128)(2,1)S(1)} %bitcast.124, bf16[4096,768]{0,1:T(8,128)(2,1)} %bitcast.121), kind=kOutput, calls=%fused_computation.14 | convolution fusion | flops 1611661312 | bytes 8781824 | tf_op jit(solution)/shard_map/dot_general | solution.py:220
  102.0 2.7 fusion.2
  104.7 2.4 constant_dynamic-slice_fusion
  107.2 0.4 collective-permute-start
  107.5 0.4 copy.50
  108.0 0.8 fusion.41
  108.8 0.2 convert_element_type.173
  109.1 6.4 %convolution_convert_fusion = bf16[2,768,4096]{2,1,0:T(8,128)(2,1)} fusion(bf16[2,128,768]{2,1,0:T(8,128)(2,1)S(1)} %convert_element_type.173, bf16[2,128,4096]{2,1,0:T(8,128)(2,1)S(1)} %bitcast.125), kind=kOutput, calls=%fused_computation.3 | convolution fusion | flops 1616904192 | bytes 15073280 | tf_op jit(solution)/shard_map/pcj,pcd->pjd/dot_general | solution.py:214
  115.5 8.4 %slice_bitcast_fusion.1 = (bf16[768,4096]{1,0:T(8,128)(2,1)S(1)}, bf16[768,4096]{1,0:T(8,128)(2,1)}) fusion(bf16[2,768,4096]{2,1,0:T(8,128)(2,1)} %convolution_convert_fusion), kind=kLoop, calls=%fused_computation.6 | loop fusion | bytes 25165824 | tf_op jit(solution)/shard_map/convert_element_type | solution.py:169
  123.9 4.9 %multiply_reduce_fusion = f32[768]{0:T(1024)S(1)} fusion(bf16[768,4096]{1,0:T(8,128)(2,1)} %get-tuple-element.14, bf16[768,4096]{1,0:T(8,128)(2,1)S(1)} %get-tuple-element.13), kind=kLoop, calls=%fused_computation.1 | loop fusion | flops 15727872 | bytes 12585984 | tf_op jit(solution)/shard_map/reduce_sum | solution.py:176
  128.8 8.2 %subtract_convert_fusion = bf16[768,4096]{1,0:T(8,128)(2,1)} fusion(bf16[768,4096]{1,0:T(8,128)(2,1)} %get-tuple-element.14, bf16[768,4096]{1,0:T(8,128)(2,1)S(1)} %get-tuple-element.13, bf16[1,1,4096,2,384]{2,4,3,1,0:T(8,128)(2,1)S(1)} %bitcast.123, f32[768]{0:T(1024)S(1)} %add_sqrt_fusion), kind=kLoop, calls=%fused_computation | loop fusion | flops 25165824 | bytes 25168896 | tf_op jit(solution)/shard_map/convert_element_type | solution.py:177
  137.0 0.2 copy.56
  137.1 0.2 copy.57
  137.3 1.8 convolution_convert_fusion.1
  139.2 2.3 slice_bitcast_fusion.3
  141.5 0.6 slice_bitcast_fusion.4
  142.1 3.7 %multiply_reduce_fusion.1 = f32[384]{0:T(512)} fusion(bf16[384,4096]{1,0:T(8,128)(2,1)} %get-tuple-element.16, bf16[384,4096]{1,0:T(8,128)(2,1)S(1)} %get-tuple-element.15), kind=kLoop, calls=%fused_computation.10 | loop fusion | flops 7863936 | bytes 6292992 | tf_op jit(solution)/shard_map/reduce_sum | solution.py:176
  145.8 2.5 add_convert_fusion.1.refs_0_
  148.3 33.6 %shard_map.92 = bf16[128,4096]{1,0:T(8,128)(2,1)} custom-call(bf16[128,4096]{1,0:T(8,128)(2,1)} %add_convert_fusion.1.refs_0_), custom_call_target="tpu_custom_call" | custom-call | bytes 4194304 | tf_op jit(solution)/shard_map/pallas_call | solution.py:119
  181.9 2.4 fusion.3
  184.3 2.9 %collective-permute-start.1 = (bf16[16,4096]{1,0:T(8,128)(2,1)}, bf16[16,4096]{1,0:T(8,128)(2,1)S(1)}, u32[]{:S(2)}, u32[]{:S(2)}) collective-permute-start(bf16[16,4096]{1,0:T(8,128)(2,1)} %fusion.3), channel_id=1, source_target_pairs={{128,0},{129,1},{130,2},{131,3},{132,4},{133,5},{134,6},{135,7},{1... | collective-permute-start | bytes 393224 | tf_op jit(solution)/shard_map/ppermute | solution.py:145
  187.3 0.7 add_sqrt_fusion.1
  187.9 0.7 copy.48
  188.7 0.8 copy.49
  189.4 0.1 convert_reduce_fusion
  189.6 0.3 collective-permute-done.1
  189.9 1.4 convolution_convert_fusion.5.refs_0_
  191.3 35.1 %shard_map.93 = bf16[256,4096]{1,0:T(8,128)(2,1)} custom-call(bf16[128,4096]{1,0:T(8,128)(2,1)} %convolution_convert_fusion.5.refs_0_), custom_call_target="tpu_custom_call" | custom-call | bytes 6291456 | tf_op jit(solution)/shard_map/pallas_call | solution.py:119
  226.5 5.2 %fusion.44 = f32[256,768]{0,1:T(8,128)S(1)} fusion(bf16[256,4096]{1,0:T(8,128)(2,1)} %shard_map.93, bf16[768,4096]{1,0:T(8,128)(2,1)} %subtract_convert_fusion), kind=kOutput, calls=%fused_computation.97 | convolution fusion | flops 1610612736 | bytes 9175040 | tf_op jit(solution)/shard_map/dot_general | solution.py:182
  231.7 0.8 fusion.40
  232.5 1.9 copy.60
  234.4 0.9 copy.61
  235.4 5.2 %convolution_convert_fusion.2 = bf16[256,4096]{1,0:T(8,128)(2,1)S(1)} fusion(bf16[384,4096]{1,0:T(8,128)(2,1)} %get-tuple-element.16, bf16[384,4096]{1,0:T(8,128)(2,1)S(1)} %get-tuple-element.15, bf16[1,1,384,4096]{3,2,1,0:T(8,128)(2,1)} %param.17, f32[384]{0:T(512)S(1)} %add_sqrt_fusion.1, f32[256,1,384]{2,0,1:T(8,128)} %copy.61, f32[256,1,384]{2,0,1:T(8,128)} %copy.60), kind=kOutput, calls=%fused_computation.12 | convolution fusion | flops 819527680 | bytes 12322304 | tf_op jit(solution)/shard_map/dot_general | solution.py:188
  240.6 0.1 constant_dynamic-slice_fusion.1
  240.7 0.5 collective-permute-start.2
  241.2 2.3 collective-permute-done.2
  243.5 1.3 add_convert_fusion.refs_0_
  244.7 33.6 %shard_map.94 = bf16[128,4096]{1,0:T(8,128)(2,1)} custom-call(bf16[128,4096]{1,0:T(8,128)(2,1)} %add_convert_fusion.refs_0_), custom_call_target="tpu_custom_call" | custom-call | bytes 4194304 | tf_op jit(solution)/shard_map/pallas_call | solution.py:119
  278.4 1.7 add_convert_fusion.2
  280.1 1.3 collective-permute-start.3
  281.4 7.1 %collective-permute-done.3 = bf16[16,4096]{1,0:T(8,128)(2,1)S(1)} collective-permute-done((bf16[16,4096]{1,0:T(8,128)(2,1)S(1)}, bf16[16,4096]{1,0:T(8,128)(2,1)S(1)}, u32[]{:S(2)}, u32[]{:S(2)}) %collective-permute-start.3) | collective-permute-done | bytes 131104 | tf_op jit(solution)/shard_map/ppermute | solution.py:145
  288.5 0.7 select_bitcast_fusion
  (51 shorter events, 0.8 us)
Async XLA Ops:
  6.6 17.8 %copy-start.12 = (f32[16]{0:T(128)}, f32[16]{0:T(128)S(1)}, u32[]{:S(2)}) copy-start(f32[16]{0:T(128)S(1)} %add_divide_fusion) | copy-start | bytes 196
  6.7 16.4 %copy-start.7 = (bf16[1,16,4096]{2,1,0:T(8,128)(2,1)S(1)}, bf16[1,16,4096]{2,1,0:T(8,128)(2,1)}, u32[]{:S(2)}) copy-start(bf16[1,16,4096]{2,1,0:T(8,128)(2,1)} %param.9) | copy-start | bytes 393220
  6.7 17.8 %copy-start.8 = (bf16[16,4096]{1,0:T(8,128)(2,1)S(1)}, bf16[16,4096]{1,0:T(8,128)(2,1)}, u32[]{:S(2)}) copy-start(bf16[16,4096]{1,0:T(8,128)(2,1)} %param.10) | copy-start | bytes 393220
  90.2 5.4 %copy-start.2 = (bf16[256,4096]{1,0:T(8,128)(2,1)S(1)}, bf16[256,4096]{1,0:T(8,128)(2,1)}, u32[]{:S(2)}) copy-start(bf16[256,4096]{1,0:T(8,128)(2,1)} %get-tuple-element.7) | copy-start | bytes 6291460
  90.2 5.4 %copy-start.14 = (bf16[1,1,384,4096]{3,2,1,0:T(8,128)(2,1)S(1)}, bf16[1,1,384,4096]{3,2,1,0:T(8,128)(2,1)}, u32[]{:S(2)}) copy-start(bf16[1,1,384,4096]{3,2,1,0:T(8,128)(2,1)} %param.17) | copy-start | bytes 9437188
  95.6 6.4 %copy-start.5 = (f32[256,2,384]{2,0,1:T(8,128)}, f32[256,2,384]{2,0,1:T(8,128)S(1)}, u32[]{:S(2)}) copy-start(f32[256,2,384]{2,0,1:T(8,128)S(1)} %fusion) | copy-start | bytes 2359300
  97.2 4.8 %copy-start.15 = (bf16[1,1,384,4096]{3,2,1,0:T(8,128)(2,1)S(1)}, bf16[1,1,384,4096]{3,2,1,0:T(8,128)(2,1)}, u32[]{:S(2)}) copy-start(bf16[1,1,384,4096]{3,2,1,0:T(8,128)(2,1)} %param.17) | copy-start | bytes 9437188
  104.7 4.3 %copy-start = (bf16[256,4096]{1,0:T(8,128)(2,1)S(1)}, bf16[256,4096]{1,0:T(8,128)(2,1)}, u32[]{:S(2)}) copy-start(bf16[256,4096]{1,0:T(8,128)(2,1)} %get-tuple-element.8) | copy-start | bytes 6291460
  104.7 3.2 %copy-start.6 = (f32[256,2,384]{2,0,1:T(8,128)S(1)}, f32[256,2,384]{2,0,1:T(8,128)}, u32[]{:S(2)}) copy-start(f32[256,2,384]{2,0,1:T(8,128)} %copy-done.5) | copy-start | bytes 2359300
  107.2 38.6 %collective-permute-start = (bf16[128,4096]{1,0:T(8,128)(2,1)}, bf16[128,4096]{1,0:T(8,128)(2,1)}, u32[]{:S(2)}, u32[]{:S(2)}) collective-permute-start(bf16[128,4096]{1,0:T(8,128)(2,1)} %constant_dynamic-slice_fusion), channel_id=1, source_target_pairs={{0,1},{1,0},{2,3},{3,2},{4,5},{5,4},{6,7},{7,6},{8,9},{9,8},{10,11... | collective-permute-start | bytes 3145736 | tf_op jit(solution)/shard_map/ppermute | solution.py:256
  109.0 19.7 %slice-start = ((s8[6291456]{0:T(1024)(128)(4,1)}), s8[2097152]{0:T(1024)(128)(4,1)S(1)}, s32[]{:S(2)}) async-start(s8[6291456]{0:T(1024)(128)(4,1)} %bitcast.122), calls=%async_computation | async-start | bytes 4194304
  115.5 13.3 %slice-start.1 = ((s8[6291456]{0:T(1024)(128)(4,1)}), s8[4194304]{0:T(1024)(128)(4,1)S(1)}, s32[]{:S(2)}) async-start(s8[6291456]{0:T(1024)(128)(4,1)} %bitcast.122), calls=%async_computation.1 | async-start | bytes 8388608
  128.8 8.2 %copy-start.4 = (f32[256,1,384]{2,0,1:T(8,128)S(1)}, f32[256,1,384]{2,0,1:T(8,128)}, u32[]{:S(2)}) copy-start(f32[256,1,384]{2,0,1:T(8,128)} %get-tuple-element.21) | copy-start | bytes 1179652
  128.8 8.5 %copy-start.3 = (bf16[256,4096]{1,0:T(8,128)(2,1)S(1)}, bf16[256,4096]{1,0:T(8,128)(2,1)}, u32[]{:S(2)}) copy-start(bf16[256,4096]{1,0:T(8,128)(2,1)} %get-tuple-element.7) | copy-start | bytes 6291460
  139.1 2.3 copy-start.11
  142.1 3.7 %copy-start.1 = (bf16[256,4096]{1,0:T(8,128)(2,1)S(1)}, bf16[256,4096]{1,0:T(8,128)(2,1)}, u32[]{:S(2)}) copy-start(bf16[256,4096]{1,0:T(8,128)(2,1)} %fusion.2) | copy-start | bytes 6291460
  145.8 36.1 %copy-start.13 = (f32[16]{0:T(128)S(1)}, f32[16]{0:T(128)}, u32[]{:S(2)}) copy-start(f32[16]{0:T(128)} %copy-done.12) | copy-start | bytes 196
  184.3 5.6 %collective-permute-start.1 = (bf16[16,4096]{1,0:T(8,128)(2,1)}, bf16[16,4096]{1,0:T(8,128)(2,1)S(1)}, u32[]{:S(2)}, u32[]{:S(2)}) collective-permute-start(bf16[16,4096]{1,0:T(8,128)(2,1)} %fusion.3), channel_id=1, source_target_pairs={{128,0},{129,1},{130,2},{131,3},{132,4},{133,5},{134,6},{135,7},{1... | collective-permute-start | bytes 393224 | tf_op jit(solution)/shard_map/ppermute | solution.py:145
  189.9 41.8 %copy-start.9 = (bf16[16,4096]{1,0:T(8,128)(2,1)}, bf16[16,4096]{1,0:T(8,128)(2,1)S(1)}, u32[]{:S(2)}) copy-start(bf16[16,4096]{1,0:T(8,128)(2,1)S(1)} %collective-permute-done.1) | copy-start | bytes 393220
  240.7 37.7 %copy-start.10 = (bf16[16,4096]{1,0:T(8,128)(2,1)S(1)}, bf16[16,4096]{1,0:T(8,128)(2,1)}, u32[]{:S(2)}) copy-start(bf16[16,4096]{1,0:T(8,128)(2,1)} %copy-done.9) | copy-start | bytes 393220
  240.7 2.8 collective-permute-start.2
  280.1 8.4 %collective-permute-start.3 = (bf16[16,4096]{1,0:T(8,128)(2,1)S(1)}, bf16[16,4096]{1,0:T(8,128)(2,1)S(1)}, u32[]{:S(2)}, u32[]{:S(2)}) collective-permute-start(bf16[16,4096]{1,0:T(8,128)(2,1)S(1)} %add_convert_fusion.2), channel_id=1, source_target_pairs={{0,128},{1,129},{2,130},{3,131},{4,132},{5,133},{6,134},{7,135},{8... | collective-permute-start | bytes 393224 | tf_op jit(solution)/shard_map/ppermute | solution.py:145

commit v5 on v3

--- a/solution.py
+++ b/solution.py
@@ -41,7 +41,8 @@
         owns.append(own)
 
     def outgoing(part, k):
-        other = lax.rem(me + k, count)
+        step = jnp.where(k % 2 == 1, (k + 1) // 2, count - k // 2)
+        other = lax.rem(me + step, count)
         return pltpu.make_async_remote_copy(
             src_ref=sources[part].at[spot(other)],
             dst_ref=targets[part].at[spot(me, base)],

time: 280 us -> 279 us (level)
  transfers between devices with their start and end apart: 4 -> 4, of which waited for: 2 -> 2; matrix products, arithmetic and copies ran while one was open for 14% -> 15% of each run, Pallas kernels for 0% -> 0%
where the time goes in v5:
time: 279 us; the launch traced here: 278 us
  Pallas kernels  165 us (59%)
  local copies, waits for them, and re-layouts  39.3 us (14%)
  matrix products  38.8 us (14%)
  other arithmetic  19.3 us (7%)
  waiting for transfers between devices  9.36 us (3%)
  starting transfers between devices  5.06 us (2%)
    pallas_call x4, Pallas kernels, exchange(): pl.pallas_call(functools.partial(exchange_kernel, count, width, share), o...  165 us
    dot_general x1, local copies, waits for them, and re-layouts, learn_core(): jnp.dot(slot_rows, weights_gu.reshape(model_width, 2 * hidden_count), pre...  8.8 us
    convert_element_type x1, local copies, waits for them, and re-layouts, renew(): (weights.astype(jnp.float32) - rate * grads / scale).astype(jnp.bfloat16)  8.62 us
    convert_element_type x2, local copies, waits for them, and re-layouts, replica_sum(): per_replica[replica].astype(jnp.bfloat16)  8.32 us
    dot_general x1, matrix products, learn_core(): jnp.einsum('pcd,pcgh->pdgh', slot_rows.reshape(rep_count, -1, model_width...  7.47 us
    unnamed x37, local copies, waits for them, and re-layouts  7.4 us
    ppermute x2, waiting for transfers between devices, passed_along(): return lax.ppermute(block, axis, route)  7.07 us
  transfers between devices with their start and end apart: 4, of which 2 were waited for; matrix products, arithmetic and copies ran while one was open for 15% of the time, Pallas kernels for 0%

profile of v5, /device:TPU:4, one launch (start us, length us, event | category | flops | bytes accessed | tf_op | source)
XLA Modules:
  0.0 277.8 jit_solution(9872998523994609475)
XLA Ops:
  0.0 0.7 slice.44
  0.7 0.1 copy.49
  0.8 0.1 eq.69
  0.9 0.1 fusion.41
  1.0 0.2 reduce_window_sum.25
  1.1 0.2 select_reduce_fusion.1
  1.3 0.1 reduce_sum.91
  1.4 0.1 copy.50
  1.5 0.7 bitcast_add_fusion
  2.3 0.1 eq.62
  2.4 0.1 fusion.42
  2.4 0.2 reduce_window_sum.24
  2.6 0.2 select_reduce_fusion.3
  2.8 0.1 reduce_sum.87
  2.9 0.1 copy.44
  3.0 0.1 copy.45
  3.0 0.7 bitcast_select_fusion
  3.7 0.1 copy.46
  3.8 0.8 reduce-window.8
  4.6 0.7 bitcast_subtract_fusion
  5.3 0.7 select_reduce_fusion.4
  6.1 6.5 %copy.63 = bf16[512,8,2,384]{3,1,2,0:T(8,128)(2,1)} copy(bf16[512,8,2,384]{3,2,1,0:T(2,128)(2,1)} %bitcast.137) | data formatting | bytes 12582912
  12.6 8.8 %copy.47 = bf16[768,4096]{1,0:T(8,128)(2,1)} copy(bf16[768,4096]{0,1:T(8,128)(2,1)} %bitcast.136) | data formatting | bytes 12582912 | tf_op jit(solution)/shard_map/dot_general | solution.py:197
  21.4 0.1 select_reduce_fusion.2
  21.5 1.5 convolution_convert_fusion.6.refs_0_
  23.1 2.1 convolution_convert_fusion.5.refs_1_
  25.1 65.1 %shard_map.91 = (bf16[256,4096]{1,0:T(8,128)(2,1)}, bf16[256,4096]{1,0:T(8,128)(2,1)}) custom-call(bf16[128,4096]{1,0:T(8,128)(2,1)} %convolution_convert_fusion.6.refs_0_, bf16[128,4096]{1,0:T(8,128)(2,1)} %convolution_convert_fusion.5.refs_1_), custom_call_target="tpu_custom_call" | custom-call | bytes 12582912 | tf_op jit(solution)/shard_map/pallas_call | solution.py:120
  90.2 5.4 %fusion.17 = f32[256,2,384]{2,0,1:T(8,128)S(1)} fusion(bf16[2,384,4096]{2,1,0:T(8,128)(2,1)} %bitcast.142, bf16[256,4096]{1,0:T(8,128)(2,1)} %get-tuple-element.8), kind=kOutput, calls=%fused_computation.31 | convolution fusion | flops 1610612736 | bytes 9175040 | tf_op jit(solution)/shard_map/dot_general | solution.py:197
  95.6 1.3 fusion.32
  97.0 1.8 fusion.8
  98.9 2.6 fusion.11
  101.5 2.3 constant_dynamic-slice_fusion
  103.8 0.4 collective-permute-start
  104.2 0.8 fusion.57
  105.0 7.5 %convolution_convert_fusion = bf16[2,4096,2,384]{3,1,2,0:T(8,128)(2,1)} fusion(bf16[2,128,4096,1]{2,1,3,0:T(8,128)(2,1)S(1)} %bitcast.143, bf16[2,128,1,384]{3,1,2,0:T(8,128)(2,1)} %bitcast.150, bf16[2,128,1,384]{3,1,2,0:T(8,128)(2,1)} %bitcast.148), kind=kOutput, calls=%fused_computation.3 | convolution fusion | flops 1617690624 | bytes 15073280 | tf_op jit(solution)/shard_map/pcd,pcgh->pdgh/dot_general | solution.py:219
  112.5 6.0 %slice_bitcast_fusion.1 = (bf16[4096,2,384]{2,0,1:T(8,128)(2,1)S(1)}, bf16[4096,2,384]{2,0,1:T(8,128)(2,1)S(1)}) fusion(bf16[2,4096,2,384]{3,1,2,0:T(8,128)(2,1)} %convolution_convert_fusion), kind=kLoop, calls=%fused_computation.6 | loop fusion | bytes 25165824 | tf_op jit(solution)/shard_map/convert_element_type | solution.py:170
  118.6 2.0 multiply_reduce_fusion
  120.6 0.1 slice-done.2
  120.7 0.7 slice-done.3
  121.4 5.0 %subtract_convert_fusion = bf16[4096,2,384]{2,0,1:T(8,128)(2,1)} fusion(bf16[4096,2,384]{2,0,1:T(8,128)(2,1)S(1)} %get-tuple-element.14, bf16[4096,2,384]{2,0,1:T(8,128)(2,1)S(1)} %get-tuple-element.13, f32[2,384]{1,0:T(2,128)S(1)} %add_sqrt_fusion, bf16[1,1,4096,2,384]{4,3,2,1,0:T(2,128)(2,1)S(1)} %bitcast.141), kind=kLoop, calls=%fused_computation | loop fusion | flops 25165824 | bytes 25168896 | tf_op jit(solution)/shard_map/convert_element_type | solution.py:178
  126.4 1.1 copy.58
  127.5 0.2 copy.59
  127.7 3.4 %convolution_convert_fusion.1 = bf16[2,384,4096]{2,1,0:T(8,128)(2,1)S(1)} fusion(bf16[2,128,4096]{2,1,0:T(8,128)(2,1)} %bitcast.144, f32[2,128,384]{1,2,0:T(8,128)S(1)} %copy.59, f32[2,128,384]{1,2,0:T(8,128)S(1)} %copy.58), kind=kOutput, calls=%fused_computation.4 | convolution fusion | flops 809041920 | bytes 9175040 | tf_op jit(solution)/shard_map/pch,pcd->phd/dot_general | solution.py:213
  131.1 2.3 slice_bitcast_fusion.3
  133.4 3.1 %multiply_reduce_fusion.1 = f32[384]{0:T(512)S(1)} fusion(bf16[384,4096]{1,0:T(8,128)(2,1)} %get-tuple-element.16, bf16[384,4096]{1,0:T(8,128)(2,1)S(1)} %get-tuple-element.15), kind=kLoop, calls=%fused_computation.12 | loop fusion | flops 7863936 | bytes 6292992 | tf_op jit(solution)/shard_map/reduce_sum | solution.py:177
  136.6 2.5 add_convert_fusion.1.refs_0_
  139.1 33.0 %shard_map.92 = bf16[128,4096]{1,0:T(8,128)(2,1)} custom-call(bf16[128,4096]{1,0:T(8,128)(2,1)} %add_convert_fusion.1.refs_0_), custom_call_target="tpu_custom_call" | custom-call | bytes 4194304 | tf_op jit(solution)/shard_map/pallas_call | solution.py:120
  172.1 2.4 fusion.12
  174.5 2.9 %collective-permute-start.1 = (bf16[16,4096]{1,0:T(8,128)(2,1)}, bf16[16,4096]{1,0:T(8,128)(2,1)S(1)}, u32[]{:S(2)}, u32[]{:S(2)}) collective-permute-start(bf16[16,4096]{1,0:T(8,128)(2,1)} %fusion.12), channel_id=1, source_target_pairs={{128,0},{129,1},{130,2},{131,3},{132,4},{133,5},{134,6},{135,7},{1... | collective-permute-start | bytes 393224 | tf_op jit(solution)/shard_map/ppermute | solution.py:146
  177.5 8.6 %copy.56 = bf16[4096,2,384]{0,2,1:T(8,128)(2,1)} copy(bf16[4096,2,384]{2,0,1:T(8,128)(2,1)} %subtract_convert_fusion) | data formatting | bytes 12582912 | tf_op jit(solution)/shard_map/convert_element_type | solution.py:178
  186.2 0.1 convert_reduce_fusion
  186.4 1.4 convolution_convert_fusion.4.refs_0_
  187.8 34.2 %shard_map.93 = bf16[256,4096]{1,0:T(8,128)(2,1)} custom-call(bf16[128,4096]{1,0:T(8,128)(2,1)} %convolution_convert_fusion.4.refs_0_), custom_call_target="tpu_custom_call" | custom-call | bytes 6291456 | tf_op jit(solution)/shard_map/pallas_call | solution.py:120
  222.0 5.4 %fusion = f32[256,2,384]{2,0,1:T(8,128)S(1)} fusion(bf16[4096,2,384]{0,2,1:T(8,128)(2,1)} %copy.56, bf16[256,4096]{1,0:T(8,128)(2,1)} %shard_map.93), kind=kOutput, calls=%fused_computation.7 | convolution fusion | flops 1610612736 | bytes 9175040 | tf_op jit(solution)/shard_map/dot_general | solution.py:183
  227.4 2.2 convolution_convert_fusion.2
  229.6 0.1 constant_dynamic-slice_fusion.1
  229.7 0.5 collective-permute-start.2
  230.2 2.3 collective-permute-done.2
  232.5 1.2 add_convert_fusion.refs_0_
  233.7 33.3 %shard_map.94 = bf16[128,4096]{1,0:T(8,128)(2,1)} custom-call(bf16[128,4096]{1,0:T(8,128)(2,1)} %add_convert_fusion.refs_0_), custom_call_target="tpu_custom_call" | custom-call | bytes 4194304 | tf_op jit(solution)/shard_map/pallas_call | solution.py:120
  267.0 1.7 add_convert_fusion.2
  268.7 1.3 collective-permute-start.3
  270.0 7.1 %collective-permute-done.3 = bf16[16,4096]{1,0:T(8,128)(2,1)S(1)} collective-permute-done((bf16[16,4096]{1,0:T(8,128)(2,1)S(1)}, bf16[16,4096]{1,0:T(8,128)(2,1)S(1)}, u32[]{:S(2)}, u32[]{:S(2)}) %collective-permute-start.3) | collective-permute-done | bytes 131104 | tf_op jit(solution)/shard_map/ppermute | solution.py:146
  277.1 0.7 select_bitcast_fusion
  (47 shorter events, 0.3 us)
Async XLA Ops:
  6.1 17.0 %copy-start.10 = (f32[16]{0:T(128)}, f32[16]{0:T(128)S(1)}, u32[]{:S(2)}) copy-start(f32[16]{0:T(128)S(1)} %add_divide_fusion) | copy-start | bytes 196
  12.6 8.9 %copy-start.4 = (bf16[1,16,4096]{2,1,0:T(8,128)(2,1)S(1)}, bf16[1,16,4096]{2,1,0:T(8,128)(2,1)}, u32[]{:S(2)}) copy-start(bf16[1,16,4096]{2,1,0:T(8,128)(2,1)} %param.9) | copy-start | bytes 393220
  12.6 10.5 %copy-start.5 = (bf16[16,4096]{1,0:T(8,128)(2,1)S(1)}, bf16[16,4096]{1,0:T(8,128)(2,1)}, u32[]{:S(2)}) copy-start(bf16[16,4096]{1,0:T(8,128)(2,1)} %param.10) | copy-start | bytes 393220
  25.1 71.9 %slice-start = ((s8[6291456]{0:T(1024)(128)(4,1)}), s8[2097152]{0:T(1024)(128)(4,1)S(1)}, s32[]{:S(2)}) async-start(s8[6291456]{0:T(1024)(128)(4,1)} %bitcast.138), calls=%async_computation | async-start | bytes 4194304
  90.2 5.4 %copy-start.3 = (bf16[256,4096]{1,0:T(8,128)(2,1)S(1)}, bf16[256,4096]{1,0:T(8,128)(2,1)}, u32[]{:S(2)}) copy-start(bf16[256,4096]{1,0:T(8,128)(2,1)} %get-tuple-element.7) | copy-start | bytes 6291460
  90.2 5.4 %copy-start.12 = (bf16[1,1,384,4096]{3,2,1,0:T(8,128)(2,1)S(1)}, bf16[1,1,384,4096]{3,2,1,0:T(8,128)(2,1)}, u32[]{:S(2)}) copy-start(bf16[1,1,384,4096]{3,2,1,0:T(8,128)(2,1)} %param.17) | copy-start | bytes 9437188
  90.2 6.8 %slice-start.1 = ((s8[6291456]{0:T(1024)(128)(4,1)}), s8[4194304]{0:T(1024)(128)(4,1)S(1)}, s32[]{:S(2)}) async-start(s8[6291456]{0:T(1024)(128)(4,1)} %bitcast.138), calls=%async_computation.1 | async-start | bytes 8388608
  97.0 1.9 copy-start.7
  97.0 1.9 copy-start.8
  98.9 6.1 %copy-start.1 = (bf16[256,4096]{1,0:T(8,128)(2,1)S(1)}, bf16[256,4096]{1,0:T(8,128)(2,1)}, u32[]{:S(2)}) copy-start(bf16[256,4096]{1,0:T(8,128)(2,1)} %get-tuple-element.8) | copy-start | bytes 6291460
  103.8 32.8 %collective-permute-start = (bf16[128,4096]{1,0:T(8,128)(2,1)}, bf16[128,4096]{1,0:T(8,128)(2,1)}, u32[]{:S(2)}, u32[]{:S(2)}) collective-permute-start(bf16[128,4096]{1,0:T(8,128)(2,1)} %constant_dynamic-slice_fusion), channel_id=1, source_target_pairs={{0,1},{1,0},{2,3},{3,2},{4,5},{5,4},{6,7},{7,6},{8,9},{9,8},{10,11... | collective-permute-start | bytes 3145736 | tf_op jit(solution)/shard_map/ppermute | solution.py:259
  118.5 2.2 slice-start.2
  118.5 2.9 %slice-start.3 = ((s8[6291456]{0:T(1024)(128)(4,1)}), s8[2097152]{0:T(1024)(128)(4,1)S(1)}, s32[]{:S(2)}) async-start(s8[6291456]{0:T(1024)(128)(4,1)} %bitcast.140), calls=%async_computation.3 | async-start | bytes 4194304
  131.1 2.3 copy-start.9
  133.4 3.2 %copy-start.2 = (bf16[256,4096]{1,0:T(8,128)(2,1)S(1)}, bf16[256,4096]{1,0:T(8,128)(2,1)}, u32[]{:S(2)}) copy-start(bf16[256,4096]{1,0:T(8,128)(2,1)} %fusion.11) | copy-start | bytes 6291460
  136.5 35.6 %copy-start.6 = (bf16[16,4096]{1,0:T(8,128)(2,1)S(1)}, bf16[16,4096]{1,0:T(8,128)(2,1)}, u32[]{:S(2)}) copy-start(bf16[16,4096]{1,0:T(8,128)(2,1)} %param.10) | copy-start | bytes 393220
  136.5 35.6 %copy-start.11 = (f32[16]{0:T(128)S(1)}, f32[16]{0:T(128)}, u32[]{:S(2)}) copy-start(f32[16]{0:T(128)} %copy-done.10) | copy-start | bytes 196
  174.5 11.8 %collective-permute-start.1 = (bf16[16,4096]{1,0:T(8,128)(2,1)}, bf16[16,4096]{1,0:T(8,128)(2,1)S(1)}, u32[]{:S(2)}, u32[]{:S(2)}) collective-permute-start(bf16[16,4096]{1,0:T(8,128)(2,1)} %fusion.12), channel_id=1, source_target_pairs={{128,0},{129,1},{130,2},{131,3},{132,4},{133,5},{134,6},{135,7},{1... | collective-permute-start | bytes 393224 | tf_op jit(solution)/shard_map/ppermute | solution.py:146
  222.0 5.4 %copy-start = (bf16[384,4096]{1,0:T(8,128)(2,1)S(1)}, bf16[384,4096]{1,0:T(8,128)(2,1)}, u32[]{:S(2)}) copy-start(bf16[384,4096]{1,0:T(8,128)(2,1)} %get-tuple-element.16) | copy-start | bytes 9437188
  222.0 5.4 %copy-start.13 = (bf16[1,1,384,4096]{3,2,1,0:T(8,128)(2,1)S(1)}, bf16[1,1,384,4096]{3,2,1,0:T(8,128)(2,1)}, u32[]{:S(2)}) copy-start(bf16[1,1,384,4096]{3,2,1,0:T(8,128)(2,1)} %param.17) | copy-start | bytes 9437188
  229.7 2.7 collective-permute-start.2
  268.7 8.4 %collective-permute-start.3 = (bf16[16,4096]{1,0:T(8,128)(2,1)S(1)}, bf16[16,4096]{1,0:T(8,128)(2,1)S(1)}, u32[]{:S(2)}, u32[]{:S(2)}) collective-permute-start(bf16[16,4096]{1,0:T(8,128)(2,1)S(1)} %add_convert_fusion.2), channel_id=1, source_target_pairs={{0,128},{1,129},{2,130},{3,131},{4,132},{5,133},{6,134},{7,135},{8... | collective-permute-start | bytes 393224 | tf_op jit(solution)/shard_map/ppermute | solution.py:146

commit v6 on v5

--- a/solution.py
+++ b/solution.py
@@ -9,10 +9,7 @@
 MESH = pl.DeviceIdType.MESH
 
 
-def exchange_kernel(count, width, share, *refs):
-    parts = len(refs) // 2 - 1
-    sources, targets = refs[:parts], refs[parts:2 * parts]
-    send_sem, recv_sem, own_sem = refs[2 * parts:]
+def exchange_kernel(count, width, share, source, target, send_sem, recv_sem, own_sem):
     me = lax.axis_index("ep")
     rows = count * width
     side = lax.axis_index("dp")
@@ -32,109 +29,97 @@
     def spot(index, start=0):
         return pl.ds(pl.multiple_of(start + index * width, width), width)
 
-    owns = []
-    for part in range(parts):
-        own = pltpu.make_async_copy(
-            sources[part].at[spot(me)], targets[part].at[spot(me, base)], own_sem.at[part, 0]
-        )
-        own.start()
-        owns.append(own)
-
-    def outgoing(part, k):
+    own = pltpu.make_async_copy(
+        source.at[:, spot(me)], target.at[:, spot(me, base)], own_sem.at[0]
+    )
+    own.start()
+
+    def outgoing(k):
         step = jnp.where(k % 2 == 1, (k + 1) // 2, count - k // 2)
         other = lax.rem(me + step, count)
         return pltpu.make_async_remote_copy(
-            src_ref=sources[part].at[spot(other)],
-            dst_ref=targets[part].at[spot(me, base)],
-            send_sem=send_sem.at[part, other],
-            recv_sem=recv_sem.at[part, me],
+            src_ref=source.at[:, spot(other)],
+            dst_ref=target.at[:, spot(me, base)],
+            send_sem=send_sem.at[other],
+            recv_sem=recv_sem.at[me],
             device_id={"ep": other},
             device_id_type=MESH,
         )
 
-    def incoming(part, k):
+    def incoming(k):
         other = lax.rem(me + count - k, count)
         return pltpu.make_async_remote_copy(
-            src_ref=sources[part].at[spot(other)],
-            dst_ref=targets[part].at[spot(other, base)],
-            send_sem=send_sem.at[part, other],
-            recv_sem=recv_sem.at[part, other],
+            src_ref=source.at[:, spot(other)],
+            dst_ref=target.at[:, spot(other, base)],
+            send_sem=send_sem.at[other],
+            recv_sem=recv_sem.at[other],
             device_id={"ep": other},
             device_id_type=MESH,
         )
 
     def launch(k, carry):
-        for part in range(parts):
-            outgoing(part, k).start()
+        outgoing(k).start()
         return carry
 
     lax.fori_loop(1, count, launch, 0)
 
     def settle(k, carry):
-        for part in range(parts):
-            outgoing(part, k).wait_send()
+        outgoing(k).wait_send()
         return carry
 
     lax.fori_loop(1, count, settle, 0)
 
     def land(k, carry):
-        for part in range(parts):
-            incoming(part, k).wait_recv()
+        incoming(k).wait_recv()
         return carry
 
     lax.fori_loop(1, count, land, 0)
-    for own in owns:
-        own.wait()
+    own.wait()
     if share:
         half = pl.ds(pl.multiple_of(base, rows), rows)
         yonder = pl.ds(pl.multiple_of((1 - side) * rows, rows), rows)
-        passes = []
-        for part in range(parts):
-            onward = pltpu.make_async_remote_copy(
-                src_ref=targets[part].at[half],
-                dst_ref=targets[part].at[half],
-                send_sem=own_sem.at[part, 1],
-                recv_sem=own_sem.at[part, 2],
-                device_id={"dp": 1 - side},
-                device_id_type=MESH,
-            )
-            onward.start()
-            passes.append(onward)
-        for part in range(parts):
-            passes[part].wait_send()
-            pltpu.make_async_remote_copy(
-                src_ref=targets[part].at[yonder],
-                dst_ref=targets[part].at[yonder],
-                send_sem=own_sem.at[part, 1],
-                recv_sem=own_sem.at[part, 2],
-                device_id={"dp": 1 - side},
-                device_id_type=MESH,
-            ).wait_recv()
+        onward = pltpu.make_async_remote_copy(
+            src_ref=target.at[:, half],
+            dst_ref=target.at[:, half],
+            send_sem=own_sem.at[1],
+            recv_sem=own_sem.at[2],
+            device_id={"dp": 1 - side},
+            device_id_type=MESH,
+        )
+        onward.start()
+        onward.wait_send()
+        pltpu.make_async_remote_copy(
+            src_ref=target.at[:, yonder],
+            dst_ref=target.at[:, yonder],
+            send_sem=own_sem.at[1],
+            recv_sem=own_sem.at[2],
+            device_id={"dp": 1 - side},
+            device_id_type=MESH,
+        ).wait_recv()
 
 
 def exchange(blocks, count, tag, share=False):
-    parts = len(blocks)
-    width = blocks[0].shape[0] // count
+    block = jnp.stack(blocks)
+    width = block.shape[1] // count
     grow = 2 if share else 1
-    size = sum(block.size * block.dtype.itemsize for block in blocks)
-    return pl.pallas_call(
+    size = block.size * block.dtype.itemsize
+    shape = (block.shape[0], grow * block.shape[1]) + block.shape[2:]
+    merged = pl.pallas_call(
         functools.partial(exchange_kernel, count, width, share),
-        out_shape=[
-            jax.ShapeDtypeStruct((grow * block.shape[0],) + block.shape[1:], block.dtype)
-            for block in blocks
-        ],
-        in_specs=[pl.BlockSpec(memory_space=pl.ANY)] * parts,
-        out_specs=[pl.BlockSpec(memory_space=pl.ANY)] * parts,
+        out_shape=jax.ShapeDtypeStruct(shape, block.dtype),
+        in_specs=[pl.BlockSpec(memory_space=pl.ANY)],
+        out_specs=pl.BlockSpec(memory_space=pl.ANY),
         scratch_shapes=[
-            pltpu.SemaphoreType.DMA((parts, count)),
-            pltpu.SemaphoreType.DMA((parts, count)),
-            pltpu.SemaphoreType.DMA((parts, 3)),
+            pltpu.SemaphoreType.DMA((count,)),
+            pltpu.SemaphoreType.DMA((count,)),
+            pltpu.SemaphoreType.DMA((3,)),
         ],
         compiler_params=pltpu.CompilerParams(collective_id=tag, has_side_effects=True),
         cost_estimate=pl.CostEstimate(
             flops=0, transcendentals=0, bytes_accessed=(2 + 2 * grow) * size
         ),
-    )(*blocks)
+    )(block)
+    return [merged[index] for index in range(len(blocks))]
 
 
 EPSILON = 1e-06

time: 279 us -> 282 us (1.011)
  local copies, waits for them, and re-layouts: 39.3 us -> 43.1 us
  other arithmetic: 19.3 us -> 22.6 us
  matrix products: 38.8 us -> 35.5 us
    another operation x1 -> x4, other arithmetic: 0.83 us -> 6.1 us  [the longest x3 5.28 us: exchange(): block = jnp.stack(blocks)]
    slice x0 -> x1, local copies, waits for them, and re-layouts: none -> 4.02 us  [exchange(): return [merged[index] for index in range(len(blocks))]]
    convert_element_type x2 -> x0, other arithmetic: 3.75 us -> none  [bring_back(): (keep.astype(jnp.float32) + got.astype(jnp.float32)).astype(jnp.bfloat16)]
    unnamed x37 -> x41, local copies, waits for them, and re-layouts: 7.4 us -> 7.57 us
  transfers between devices with their start and end apart: 4 -> 4, of which waited for: 2 -> 2; matrix products, arithmetic and copies ran while one was open for 15% -> 16% of each run, Pallas kernels for 0% -> 0%
where the time goes in v6:
time: 282 us; the launch traced here: 280 us
  Pallas kernels  164 us (58%)
  local copies, waits for them, and re-layouts  43.1 us (15%)
  matrix products  35.5 us (13%)
  other arithmetic  22.6 us (8%)
  waiting for transfers between devices  9.36 us (3%)
  starting transfers between devices  5.1 us (2%)
    pallas_call x4, Pallas kernels, exchange(): pl.pallas_call(functools.partial(exchange_kernel, count, width, share), o...  164 us
    dot_general x1, local copies, waits for them, and re-layouts, learn_core(): jnp.dot(slot_rows, weights_gu.reshape(model_width, 2 * hidden_count), pre...  8.87 us
    convert_element_type x1, local copies, waits for them, and re-layouts, renew(): (weights.astype(jnp.float32) - rate * grads / scale).astype(jnp.bfloat16)  8.74 us
    convert_element_type x2, local copies, waits for them, and re-layouts, replica_sum(): per_replica[replica].astype(jnp.bfloat16)  8.33 us
    unnamed x41, local copies, waits for them, and re-layouts  7.57 us
    ppermute x2, waiting for transfers between devices, passed_along(): return lax.ppermute(block, axis, route)  7.07 us
    dot_general x1, matrix products, learn_core(): jnp.einsum('pcd,pcgh->pdgh', slot_rows.reshape(rep_count, -1, model_width...  6.41 us
    reduce_sum x2, other arithmetic, renew(): jnp.mean(grads * grads, axis=axis_number, keepdims=True) + EPSILON  5.64 us
  transfers between devices with their start and end apart: 4, of which 2 were waited for; matrix products, arithmetic and copies ran while one was open for 16% of the time, Pallas kernels for 0%

profile of v6, /device:TPU:4, one launch (start us, length us, event | category | flops | bytes accessed | tf_op | source)
XLA Modules:
  0.0 280.4 jit_solution(1012110039506440543)
XLA Ops:
  0.0 0.7 slice.52
  0.8 0.1 eq.69
  0.9 0.1 fusion.50
  1.0 0.2 reduce_window_sum.25
  1.1 0.2 select_reduce_fusion.1
  1.4 0.1 copy.50
  1.5 1.3 bitcast_add_fusion
  2.9 0.1 eq.62
  2.9 0.1 fusion.51
  3.0 0.2 reduce_window_sum.24
  3.2 0.2 select_reduce_fusion.3
  3.5 0.1 copy.44
  3.6 0.7 bitcast_select_fusion
  4.4 0.8 reduce-window.8
  5.2 0.7 bitcast_subtract_fusion
  5.9 0.7 select_reduce_fusion.4
  6.7 0.1 convert_reduce_fusion.1
  6.8 1.4 fusion.13
  8.1 2.0 fusion.12
  10.1 1.5 pad_maximum_fusion.source
  11.7 63.7 %shard_map.91 = bf16[2,256,4096]{2,1,0:T(8,128)(2,1)} custom-call(bf16[2,128,4096]{2,1,0:T(8,128)(2,1)} %pad_maximum_fusion.source), custom_call_target="tpu_custom_call" | custom-call | bytes 12582912 | tf_op jit(solution)/shard_map/pallas_call | solution.py:107
  75.4 6.5 %copy.63 = bf16[512,8,2,384]{3,1,2,0:T(8,128)(2,1)} copy(bf16[512,8,2,384]{3,2,1,0:T(2,128)(2,1)} %bitcast.159) | data formatting | bytes 12582912
  81.9 8.9 %copy.47 = bf16[768,4096]{1,0:T(8,128)(2,1)} copy(bf16[768,4096]{0,1:T(8,128)(2,1)} %bitcast.158) | data formatting | bytes 12582912 | tf_op jit(solution)/shard_map/dot_general | solution.py:182
  90.8 5.4 %fusion.20 = f32[256,2,384]{2,0,1:T(8,128)S(1)} fusion(bf16[2,384,4096]{2,1,0:T(8,128)(2,1)} %bitcast.166, bf16[2,256,4096]{2,1,0:T(8,128)(2,1)} %shard_map.91), kind=kOutput, calls=%fused_computation.35 | convolution fusion | flops 1610612736 | bytes 9175040 | tf_op jit(solution)/shard_map/dot_general | solution.py:182
  96.2 0.2 copy-done.14
  96.4 1.3 fusion.41
  97.7 1.8 fusion.8
  99.6 1.3 fusion.11
  101.0 1.2 constant_dynamic-slice_fusion
  102.1 0.4 collective-permute-start
  102.5 4.0 %fusion.68 = (bf16[1,256,4096]{2,1,0:T(8,128)(2,1)S(1)}, bf16[1,256,4096]{2,1,0:T(8,128)(2,1)}) fusion(bf16[2,256,4096]{2,1,0:T(8,128)(2,1)} %shard_map.91), kind=kLoop, calls=%fused_computation.117 | loop fusion | bytes 8388608 | tf_op jit(solution)/shard_map/slice | solution.py:122
  106.5 0.8 fusion.69
  107.4 6.4 %convolution_convert_fusion = bf16[2,4096,2,384]{3,1,2,0:T(8,128)(2,1)} fusion(bf16[2,128,4096,1]{2,1,3,0:T(8,128)(2,1)S(1)} %bitcast.164, bf16[2,128,1,384]{3,1,2,0:T(8,128)(2,1)S(1)} %bitcast.172, bf16[2,128,1,384]{3,1,2,0:T(8,128)(2,1)S(1)} %bitcast.170), kind=kOutput, calls=%fused_computation.3 | convolution fusion | flops 1617690624 | bytes 15073280 | tf_op jit(solution)/shard_map/pcd,pcgh->pdgh/dot_general | solution.py:204
  113.8 6.0 %slice_bitcast_fusion.1 = (bf16[4096,2,384]{2,0,1:T(8,128)(2,1)S(1)}, bf16[4096,2,384]{2,0,1:T(8,128)(2,1)S(1)}) fusion(bf16[2,4096,2,384]{3,1,2,0:T(8,128)(2,1)} %convolution_convert_fusion), kind=kLoop, calls=%fused_computation.6 | loop fusion | bytes 25165824 | tf_op jit(solution)/shard_map/convert_element_type | solution.py:155
  119.8 2.0 multiply_reduce_fusion
  121.9 0.1 slice-done.2
  122.0 0.7 slice-done.3
  122.7 5.0 %subtract_convert_fusion = bf16[4096,2,384]{2,0,1:T(8,128)(2,1)} fusion(bf16[4096,2,384]{2,0,1:T(8,128)(2,1)S(1)} %get-tuple-element.10, bf16[4096,2,384]{2,0,1:T(8,128)(2,1)S(1)} %get-tuple-element.9, f32[2,384]{1,0:T(2,128)S(1)} %add_sqrt_fusion, bf16[1,1,4096,2,384]{4,3,2,1,0:T(2,128)(2,1)S(1)} %bitcast.163), kind=kLoop, calls=%fused_computation | loop fusion | flops 25165824 | bytes 25168896 | tf_op jit(solution)/shard_map/convert_element_type | solution.py:163
  127.6 1.1 copy.58
  128.8 0.2 copy.59
  129.0 3.4 %convolution_convert_fusion.1 = bf16[2,384,4096]{2,1,0:T(8,128)(2,1)S(1)} fusion(bf16[2,128,4096]{2,1,0:T(8,128)(2,1)} %bitcast.165, f32[2,128,384]{1,2,0:T(8,128)S(1)} %copy.59, f32[2,128,384]{1,2,0:T(8,128)S(1)} %copy.58), kind=kOutput, calls=%fused_computation.4 | convolution fusion | flops 809041920 | bytes 9175040 | tf_op jit(solution)/shard_map/pch,pcd->phd/dot_general | solution.py:198
  132.4 2.3 slice_bitcast_fusion.3
  134.7 0.6 slice_bitcast_fusion.6
  135.3 3.6 %multiply_reduce_fusion.1 = f32[384]{0:T(512)} fusion(bf16[384,4096]{1,0:T(8,128)(2,1)} %get-tuple-element.12, bf16[384,4096]{1,0:T(8,128)(2,1)S(1)} %get-tuple-element.11), kind=kLoop, calls=%fused_computation.12 | loop fusion | flops 7863936 | bytes 6292992 | tf_op jit(solution)/shard_map/reduce_sum | solution.py:162
  138.9 2.5 fusion.23.source
  141.4 33.1 %shard_map.92 = bf16[1,128,4096]{2,1,0:T(8,128)(2,1)} custom-call(bf16[1,128,4096]{2,1,0:T(8,128)(2,1)} %fusion.23.source), custom_call_target="tpu_custom_call" | custom-call | bytes 4194304 | tf_op jit(solution)/shard_map/pallas_call | solution.py:107
  174.6 1.8 fusion.15
  176.3 3.0 %collective-permute-start.1 = (bf16[16,4096]{1,0:T(8,128)(2,1)S(1)}, bf16[16,4096]{1,0:T(8,128)(2,1)S(1)}, u32[]{:S(2)}, u32[]{:S(2)}) collective-permute-start(bf16[16,4096]{1,0:T(8,128)(2,1)S(1)} %fusion.15), channel_id=1, source_target_pairs={{128,0},{129,1},{130,2},{131,3},{132,4},{133,5},{134,6},{135,7},{1... | collective-permute-start | bytes 393224 | tf_op jit(solution)/shard_map/ppermute | solution.py:131
  179.3 0.7 add_sqrt_fusion.1
  180.0 8.7 %copy.56 = bf16[4096,2,384]{0,2,1:T(8,128)(2,1)} copy(bf16[4096,2,384]{2,0,1:T(8,128)(2,1)} %subtract_convert_fusion) | data formatting | bytes 12582912 | tf_op jit(solution)/shard_map/convert_element_type | solution.py:163
  188.9 0.1 convert_reduce_fusion
  189.0 1.5 fusion.14.source
  190.5 34.3 %shard_map.93 = bf16[1,256,4096]{2,1,0:T(8,128)(2,1)} custom-call(bf16[1,128,4096]{2,1,0:T(8,128)(2,1)} %fusion.14.source), custom_call_target="tpu_custom_call" | custom-call | bytes 6291456 | tf_op jit(solution)/shard_map/pallas_call | solution.py:107
  224.8 5.4 %fusion = f32[256,2,384]{2,0,1:T(8,128)S(1)} fusion(bf16[4096,2,384]{0,2,1:T(8,128)(2,1)} %copy.56, bf16[1,256,4096]{2,1,0:T(8,128)(2,1)} %shard_map.93), kind=kOutput, calls=%fused_computation.7 | convolution fusion | flops 1610612736 | bytes 9175040 | tf_op jit(solution)/shard_map/dot_general | solution.py:168
  230.2 2.2 convolution_convert_fusion.2
  232.4 0.1 constant_dynamic-slice_fusion.1
  232.5 0.5 collective-permute-start.2
  233.0 2.3 collective-permute-done.2
  235.3 1.2 fusion.24.source
  236.5 33.0 %shard_map.94 = bf16[1,128,4096]{2,1,0:T(8,128)(2,1)} custom-call(bf16[1,128,4096]{2,1,0:T(8,128)(2,1)} %fusion.24.source), custom_call_target="tpu_custom_call" | custom-call | bytes 4194304 | tf_op jit(solution)/shard_map/pallas_call | solution.py:107
  269.6 1.7 add_convert_fusion.2
  271.3 1.3 collective-permute-start.3
  272.6 7.1 %collective-permute-done.3 = bf16[16,4096]{1,0:T(8,128)(2,1)S(1)} collective-permute-done((bf16[16,4096]{1,0:T(8,128)(2,1)S(1)}, bf16[16,4096]{1,0:T(8,128)(2,1)S(1)}, u32[]{:S(2)}, u32[]{:S(2)}) %collective-permute-start.3) | collective-permute-done | bytes 131104 | tf_op jit(solution)/shard_map/ppermute | solution.py:131
  279.7 0.7 select_bitcast_fusion
  (53 shorter events, 0.7 us)
Async XLA Ops:
  6.6 68.7 %copy-start.13 = (f32[16]{0:T(128)}, f32[16]{0:T(128)S(1)}, u32[]{:S(2)}) copy-start(f32[16]{0:T(128)S(1)} %add_divide_fusion) | copy-start | bytes 196
  81.9 15.8 %slice-start = ((s8[6291456]{0:T(1024)(128)(4,1)}), s8[2097152]{0:T(1024)(128)(4,1)S(1)}, s32[]{:S(2)}) async-start(s8[6291456]{0:T(1024)(128)(4,1)} %bitcast.160), calls=%async_computation | async-start | bytes 4194304
  90.8 5.4 %copy-start = (bf16[2,256,4096]{2,1,0:T(8,128)(2,1)S(1)}, bf16[2,256,4096]{2,1,0:T(8,128)(2,1)}, u32[]{:S(2)}) copy-start(bf16[2,256,4096]{2,1,0:T(8,128)(2,1)} %shard_map.91) | copy-start | bytes 12582916
  90.8 5.6 %copy-start.14 = (bf16[1,1,384,4096]{3,2,1,0:T(8,128)(2,1)S(1)}, bf16[1,1,384,4096]{3,2,1,0:T(8,128)(2,1)}, u32[]{:S(2)}) copy-start(bf16[1,1,384,4096]{3,2,1,0:T(8,128)(2,1)} %param.17) | copy-start | bytes 9437188
  90.8 6.9 %slice-start.1 = ((s8[6291456]{0:T(1024)(128)(4,1)}), s8[4194304]{0:T(1024)(128)(4,1)S(1)}, s32[]{:S(2)}) async-start(s8[6291456]{0:T(1024)(128)(4,1)} %bitcast.160), calls=%async_computation.1 | async-start | bytes 8388608
  97.7 1.9 copy-start.6
  97.7 1.9 copy-start.8
  101.0 5.6 %copy-start.2 = (bf16[256,4096]{1,0:T(8,128)(2,1)}, bf16[256,4096]{1,0:T(8,128)(2,1)S(1)}, u32[]{:S(2)}) copy-start(bf16[256,4096]{1,0:T(8,128)(2,1)S(1)} %fusion.11) | copy-start | bytes 6291460
  102.1 5.2 %copy-start.7 = (bf16[256,384]{1,0:T(8,128)(2,1)S(1)}, bf16[256,384]{1,0:T(8,128)(2,1)}, u32[]{:S(2)}) copy-start(bf16[256,384]{1,0:T(8,128)(2,1)} %copy-done.6) | copy-start | bytes 589828
  102.1 5.2 %copy-start.9 = (bf16[256,384]{1,0:T(8,128)(2,1)S(1)}, bf16[256,384]{1,0:T(8,128)(2,1)}, u32[]{:S(2)}) copy-start(bf16[256,384]{1,0:T(8,128)(2,1)} %copy-done.8) | copy-start | bytes 589828
  102.1 36.8 %collective-permute-start = (bf16[128,4096]{1,0:T(8,128)(2,1)}, bf16[128,4096]{1,0:T(8,128)(2,1)}, u32[]{:S(2)}, u32[]{:S(2)}) collective-permute-start(bf16[128,4096]{1,0:T(8,128)(2,1)} %constant_dynamic-slice_fusion), channel_id=1, source_target_pairs={{0,1},{1,0},{2,3},{3,2},{4,5},{5,4},{6,7},{7,6},{8,9},{9,8},{10,11... | collective-permute-start | bytes 3145736 | tf_op jit(solution)/shard_map/ppermute | solution.py:244
  119.8 2.2 slice-start.2
  119.8 2.9 %slice-start.3 = ((s8[6291456]{0:T(1024)(128)(4,1)}), s8[2097152]{0:T(1024)(128)(4,1)S(1)}, s32[]{:S(2)}) async-start(s8[6291456]{0:T(1024)(128)(4,1)} %bitcast.162), calls=%async_computation.3 | async-start | bytes 4194304
  132.4 2.3 copy-start.12
  134.7 4.2 %copy-start.3 = (bf16[256,4096]{1,0:T(8,128)(2,1)S(1)}, bf16[256,4096]{1,0:T(8,128)(2,1)}, u32[]{:S(2)}) copy-start(bf16[256,4096]{1,0:T(8,128)(2,1)} %copy-done.2) | copy-start | bytes 6291460
  138.9 35.7 %copy-start.4 = (bf16[16,4096]{1,0:T(8,128)(2,1)S(1)}, bf16[16,4096]{1,0:T(8,128)(2,1)}, u32[]{:S(2)}) copy-start(bf16[16,4096]{1,0:T(8,128)(2,1)} %param.10) | copy-start | bytes 393220
  138.9 35.7 %copy-start.5 = (bf16[1,16,4096]{2,1,0:T(8,128)(2,1)S(1)}, bf16[1,16,4096]{2,1,0:T(8,128)(2,1)}, u32[]{:S(2)}) copy-start(bf16[1,16,4096]{2,1,0:T(8,128)(2,1)} %param.9) | copy-start | bytes 393220
  176.3 12.7 %collective-permute-start.1 = (bf16[16,4096]{1,0:T(8,128)(2,1)S(1)}, bf16[16,4096]{1,0:T(8,128)(2,1)S(1)}, u32[]{:S(2)}, u32[]{:S(2)}) collective-permute-start(bf16[16,4096]{1,0:T(8,128)(2,1)S(1)} %fusion.15), channel_id=1, source_target_pairs={{128,0},{129,1},{130,2},{131,3},{132,4},{133,5},{134,6},{135,7},{1... | collective-permute-start | bytes 393224 | tf_op jit(solution)/shard_map/ppermute | solution.py:131
  180.0 8.7 %copy-start.10 = (s32[16,8]{0,1:T(8,128)S(1)}, s32[16,8]{0,1:T(8,128)}, u32[]{:S(2)}) copy-start(s32[16,8]{0,1:T(8,128)} %get-tuple-element.19) | copy-start | bytes 1540
  180.0 8.8 %copy-start.11 = (f32[16,8]{0,1:T(8,128)S(1)}, f32[16,8]{0,1:T(8,128)}, u32[]{:S(2)}) copy-start(f32[16,8]{0,1:T(8,128)} %slice_bitcast_fusion.6) | copy-start | bytes 1540
  224.8 5.4 %copy-start.1 = (bf16[384,4096]{1,0:T(8,128)(2,1)S(1)}, bf16[384,4096]{1,0:T(8,128)(2,1)}, u32[]{:S(2)}) copy-start(bf16[384,4096]{1,0:T(8,128)(2,1)} %get-tuple-element.12) | copy-start | bytes 9437188
  224.8 5.4 %copy-start.15 = (bf16[1,1,384,4096]{3,2,1,0:T(8,128)(2,1)S(1)}, bf16[1,1,384,4096]{3,2,1,0:T(8,128)(2,1)}, u32[]{:S(2)}) copy-start(bf16[1,1,384,4096]{3,2,1,0:T(8,128)(2,1)} %param.17) | copy-start | bytes 9437188
  232.5 2.7 collective-permute-start.2
  271.3 8.4 %collective-permute-start.3 = (bf16[16,4096]{1,0:T(8,128)(2,1)S(1)}, bf16[16,4096]{1,0:T(8,128)(2,1)S(1)}, u32[]{:S(2)}, u32[]{:S(2)}) collective-permute-start(bf16[16,4096]{1,0:T(8,128)(2,1)S(1)} %add_convert_fusion.2), channel_id=1, source_target_pairs={{0,128},{1,129},{2,130},{3,131},{4,132},{5,133},{6,134},{7,135},{8... | collective-permute-start | bytes 393224 | tf_op jit(solution)/shard_map/ppermute | solution.py:131

commit v7 on v5

--- a/solution.py
+++ b/solution.py
@@ -135,6 +135,34 @@
             flops=0, transcendentals=0, bytes_accessed=(2 + 2 * grow) * size
         ),
     )(*blocks)
+
+
+def swap_kernel(source, target, send_sem, recv_sem):
+    side = lax.axis_index("grp")
+    barrier = pltpu.get_barrier_semaphore()
+    pl.semaphore_signal(barrier, inc=1, device_id={"grp": 1 - side}, device_id_type=MESH)
+    pl.semaphore_wait(barrier, 1)
+    copy = pltpu.make_async_remote_copy(
+        src_ref=source,
+        dst_ref=target,
+        send_sem=send_sem,
+        recv_sem=recv_sem,
+        device_id={"grp": 1 - side},
+        device_id_type=MESH,
+    )
+    copy.start()
+    copy.wait()
+
+
+def swapped(block, tag):
+    return pl.pallas_call(
+        swap_kernel,
+        out_shape=jax.ShapeDtypeStruct(block.shape, block.dtype),
+        in_specs=[pl.BlockSpec(memory_space=pl.ANY)],
+        out_specs=pl.BlockSpec(memory_space=pl.ANY),
+        scratch_shapes=[pltpu.SemaphoreType.DMA(()), pltpu.SemaphoreType.DMA(())],
+        compiler_params=pltpu.CompilerParams(collective_id=tag, has_side_effects=True),
+    )(block)
 
 
 EPSILON = 1e-06
@@ -298,13 +326,13 @@
     carried = (base + combine(mixing, returned)).astype(jnp.bfloat16)
     fresh_gu = renew(own_gu, grad_gu, 0, 0.5 / model_width**0.5)
     fresh_dn = renew(own_dn, grad_dn, 1, 0.5 / hidden_all**0.5)
-    current = passed_along(carried, "grp", -1)
+    current = swapped(carried, 4)
     picker, weigher = routing_tables(decode_experts[1], decode_gates[1], capacity, ep_count)
     (rows_got,) = spread([dispatch(picker, current)], 2)
     slot_out = forward_core(rows_got, fresh_gu, fresh_dn)
     returned = bring_back(slot_out, 3)
     current = (current.astype(jnp.float32) + combine(weigher, returned)).astype(jnp.bfloat16)
-    final_rows = jnp.where(is_learner, carried, passed_along(current, "grp", 1))
+    final_rows = jnp.where(is_learner, carried, swapped(current, 5))
     return final_rows[None]
 
 

time: 279 us -> 283 us (1.014)
  Pallas kernels: 165 us -> 178 us
  waiting for transfers between devices: 9.36 us -> 2.3 us
  starting transfers between devices: 5.06 us -> 0.82 us
    pallas_call x0 -> x2, Pallas kernels: none -> 13.6 us  [swapped(): pl.pallas_call(swap_kernel, out_shape=jax.ShapeDtypeStruct(block.shape, b...]
    ppermute x2 -> x0, waiting for transfers between devices: 7.07 us -> none  [passed_along(): return lax.ppermute(block, axis, route)]
    ppermute x2 -> x0, starting transfers between devices: 4.22 us -> none  [passed_along(): return lax.ppermute(block, axis, route)]
    unnamed x37 -> x41, local copies, waits for them, and re-layouts: 7.4 us -> 7.41 us
  transfers between devices with their start and end apart: 4 -> 2, of which waited for: 2 -> 1; matrix products, arithmetic and copies ran while one was open for 15% -> 14% of each run, Pallas kernels for 0% -> 0%
where the time goes in v7:
time: 283 us; the launch traced here: 282 us
  Pallas kernels  178 us (63%)
  matrix products  40.4 us (14%)
  local copies, waits for them, and re-layouts  39.5 us (14%)
  other arithmetic  20.4 us (7%)
    pallas_call x4, Pallas kernels, exchange(): pl.pallas_call(functools.partial(exchange_kernel, count, width, share), o...  165 us
    pallas_call x2, Pallas kernels, swapped(): pl.pallas_call(swap_kernel, out_shape=jax.ShapeDtypeStruct(block.shape, b...  13.6 us
    dot_general x1, local copies, waits for them, and re-layouts, learn_core(): jnp.dot(slot_rows, weights_gu.reshape(model_width, 2 * hidden_count), pre...  8.8 us
    convert_element_type x1, local copies, waits for them, and re-layouts, renew(): (weights.astype(jnp.float32) - rate * grads / scale).astype(jnp.bfloat16)  8.77 us
    convert_element_type x2, local copies, waits for them, and re-layouts, replica_sum(): per_replica[replica].astype(jnp.bfloat16)  8.32 us
    dot_general x1, matrix products, learn_core(): jnp.einsum('pcd,pcgh->pdgh', slot_rows.reshape(rep_count, -1, model_width...  7.47 us
    unnamed x41, local copies, waits for them, and re-layouts  7.41 us
  transfers between devices with their start and end apart: 2, of which 1 were waited for; matrix products, arithmetic and copies ran while one was open for 14% of the time, Pallas kernels for 0%

profile of v7, /device:TPU:4, one launch (start us, length us, event | category | flops | bytes accessed | tf_op | source)
XLA Modules:
  0.0 282.3 jit_solution(15161491306062915816)
XLA Ops:
  0.0 0.7 slice.44
  0.7 0.1 copy.49
  0.8 0.1 eq.69
  0.9 0.1 fusion.42
  1.0 0.2 reduce_window_sum.25
  1.1 0.2 select_reduce_fusion.1
  1.3 0.1 reduce_sum.91
  1.4 0.1 copy.50
  1.5 0.7 bitcast_add_fusion
  2.3 0.1 eq.62
  2.4 0.1 fusion.43
  2.4 0.2 reduce_window_sum.24
  2.6 0.2 select_reduce_fusion.3
  2.8 0.1 reduce_sum.87
  2.9 0.1 copy.44
  3.0 0.1 copy.45
  3.0 0.7 bitcast_select_fusion
  3.7 0.1 copy.46
  3.8 0.8 reduce-window.8
  4.6 0.7 bitcast_subtract_fusion
  5.3 0.7 select_reduce_fusion.4
  6.1 6.5 %copy.63 = bf16[512,8,2,384]{3,1,2,0:T(8,128)(2,1)} copy(bf16[512,8,2,384]{3,2,1,0:T(2,128)(2,1)} %bitcast.137) | data formatting | bytes 12582912
  12.6 8.8 %copy.47 = bf16[768,4096]{1,0:T(8,128)(2,1)} copy(bf16[768,4096]{0,1:T(8,128)(2,1)} %bitcast.136) | data formatting | bytes 12582912 | tf_op jit(solution)/shard_map/dot_general | solution.py:225
  21.4 0.1 select_reduce_fusion.2
  21.5 1.5 convolution_convert_fusion.6.refs_0_
  23.1 2.1 convolution_convert_fusion.5.refs_1_
  25.1 65.1 %shard_map.91 = (bf16[256,4096]{1,0:T(8,128)(2,1)}, bf16[256,4096]{1,0:T(8,128)(2,1)}) custom-call(bf16[128,4096]{1,0:T(8,128)(2,1)} %convolution_convert_fusion.6.refs_0_, bf16[128,4096]{1,0:T(8,128)(2,1)} %convolution_convert_fusion.5.refs_1_), custom_call_target="tpu_custom_call" | custom-call | bytes 12582912 | tf_op jit(solution)/shard_map/pallas_call | solution.py:120
  90.2 5.4 %fusion.18 = f32[256,2,384]{2,0,1:T(8,128)S(1)} fusion(bf16[2,384,4096]{2,1,0:T(8,128)(2,1)} %bitcast.142, bf16[256,4096]{1,0:T(8,128)(2,1)} %get-tuple-element.8), kind=kOutput, calls=%fused_computation.33 | convolution fusion | flops 1610612736 | bytes 9175040 | tf_op jit(solution)/shard_map/dot_general | solution.py:225
  95.6 1.3 fusion.33
  97.0 1.8 fusion.8
  98.9 2.6 fusion.11
  101.5 2.3 constant_dynamic-slice_fusion
  103.8 0.4 collective-permute-start
  104.2 0.8 fusion.58
  105.0 7.5 %convolution_convert_fusion = bf16[2,4096,2,384]{3,1,2,0:T(8,128)(2,1)} fusion(bf16[2,128,4096,1]{2,1,3,0:T(8,128)(2,1)S(1)} %bitcast.143, bf16[2,128,1,384]{3,1,2,0:T(8,128)(2,1)} %bitcast.150, bf16[2,128,1,384]{3,1,2,0:T(8,128)(2,1)} %bitcast.148), kind=kOutput, calls=%fused_computation.3 | convolution fusion | flops 1617690624 | bytes 15073280 | tf_op jit(solution)/shard_map/pcd,pcgh->pdgh/dot_general | solution.py:247
  112.5 6.0 %slice_bitcast_fusion.1 = (bf16[4096,2,384]{2,0,1:T(8,128)(2,1)S(1)}, bf16[4096,2,384]{2,0,1:T(8,128)(2,1)S(1)}) fusion(bf16[2,4096,2,384]{3,1,2,0:T(8,128)(2,1)} %convolution_convert_fusion), kind=kLoop, calls=%fused_computation.6 | loop fusion | bytes 25165824 | tf_op jit(solution)/shard_map/convert_element_type | solution.py:198
  118.6 2.0 multiply_reduce_fusion
  120.6 0.1 slice-done.2
  120.7 0.7 slice-done.3
  121.4 5.1 %subtract_convert_fusion = bf16[4096,2,384]{2,0,1:T(8,128)(2,1)} fusion(bf16[4096,2,384]{2,0,1:T(8,128)(2,1)S(1)} %get-tuple-element.14, bf16[4096,2,384]{2,0,1:T(8,128)(2,1)S(1)} %get-tuple-element.13, f32[2,384]{1,0:T(2,128)S(1)} %add_sqrt_fusion, bf16[1,1,4096,2,384]{4,3,2,1,0:T(2,128)(2,1)S(1)} %bitcast.141), kind=kLoop, calls=%fused_computation | loop fusion | flops 25165824 | bytes 25168896 | tf_op jit(solution)/shard_map/convert_element_type | solution.py:206
  126.5 1.1 copy.58
  127.6 0.2 copy.59
  127.8 3.4 %convolution_convert_fusion.1 = bf16[2,384,4096]{2,1,0:T(8,128)(2,1)S(1)} fusion(bf16[2,128,4096]{2,1,0:T(8,128)(2,1)} %bitcast.144, f32[2,128,384]{1,2,0:T(8,128)S(1)} %copy.59, f32[2,128,384]{1,2,0:T(8,128)S(1)} %copy.58), kind=kOutput, calls=%fused_computation.4 | convolution fusion | flops 809041920 | bytes 9175040 | tf_op jit(solution)/shard_map/pch,pcd->phd/dot_general | solution.py:241
  131.2 2.3 slice_bitcast_fusion.3
  133.5 8.8 %copy.56 = bf16[4096,2,384]{0,2,1:T(8,128)(2,1)} copy(bf16[4096,2,384]{2,0,1:T(8,128)(2,1)} %subtract_convert_fusion) | data formatting | bytes 12582912 | tf_op jit(solution)/shard_map/convert_element_type | solution.py:206
  142.3 0.1 copy.52
  142.4 0.1 convert_reduce_fusion
  142.5 3.1 %multiply_reduce_fusion.1 = f32[384]{0:T(512)S(1)} fusion(bf16[384,4096]{1,0:T(8,128)(2,1)} %get-tuple-element.16, bf16[384,4096]{1,0:T(8,128)(2,1)S(1)} %get-tuple-element.15), kind=kLoop, calls=%fused_computation.12 | loop fusion | flops 7863936 | bytes 6292992 | tf_op jit(solution)/shard_map/reduce_sum | solution.py:205
  145.7 2.5 add_convert_fusion.1.refs_0_
  148.2 33.0 %shard_map.92 = bf16[128,4096]{1,0:T(8,128)(2,1)} custom-call(bf16[128,4096]{1,0:T(8,128)(2,1)} %add_convert_fusion.1.refs_0_), custom_call_target="tpu_custom_call" | custom-call | bytes 4194304 | tf_op jit(solution)/shard_map/pallas_call | solution.py:120
  181.2 2.4 fusion.12.source
  183.6 6.8 %shard_map.93 = bf16[16,4096]{1,0:T(8,128)(2,1)} custom-call(bf16[16,4096]{1,0:T(8,128)(2,1)} %fusion.12.source), custom_call_target="tpu_custom_call" | custom-call | tf_op jit(solution)/shard_map/pallas_call | solution.py:158
  190.4 2.4 convolution_convert_fusion.4.refs_0_
  192.9 32.9 %shard_map.94 = bf16[256,4096]{1,0:T(8,128)(2,1)} custom-call(bf16[128,4096]{1,0:T(8,128)(2,1)} %convolution_convert_fusion.4.refs_0_), custom_call_target="tpu_custom_call" | custom-call | bytes 6291456 | tf_op jit(solution)/shard_map/pallas_call | solution.py:120
  225.8 5.4 %fusion = f32[256,2,384]{2,0,1:T(8,128)S(1)} fusion(bf16[4096,2,384]{0,2,1:T(8,128)(2,1)} %copy.56, bf16[256,4096]{1,0:T(8,128)(2,1)} %shard_map.94), kind=kOutput, calls=%fused_computation.7 | convolution fusion | flops 1610612736 | bytes 9175040 | tf_op jit(solution)/shard_map/dot_general | solution.py:211
  231.2 2.2 convolution_convert_fusion.2
  233.4 0.1 constant_dynamic-slice_fusion.1
  233.5 0.4 collective-permute-start.1
  234.0 2.3 collective-permute-done.1
  236.3 1.3 add_convert_fusion.refs_0_
  237.5 33.9 %shard_map.95 = bf16[128,4096]{1,0:T(8,128)(2,1)} custom-call(bf16[128,4096]{1,0:T(8,128)(2,1)} %add_convert_fusion.refs_0_), custom_call_target="tpu_custom_call" | custom-call | bytes 4194304 | tf_op jit(solution)/shard_map/pallas_call | solution.py:120
  271.5 2.4 fusion.13.source
  273.9 6.8 %shard_map.96 = bf16[16,4096]{1,0:T(8,128)(2,1)} custom-call(bf16[16,4096]{1,0:T(8,128)(2,1)} %fusion.13.source), custom_call_target="tpu_custom_call" | custom-call | tf_op jit(solution)/shard_map/pallas_call | solution.py:158
  280.7 1.6 select_bitcast_fusion
  (49 shorter events, 0.3 us)
Async XLA Ops:
  6.1 17.0 %copy-start.12 = (f32[16]{0:T(128)}, f32[16]{0:T(128)S(1)}, u32[]{:S(2)}) copy-start(f32[16]{0:T(128)S(1)} %add_divide_fusion) | copy-start | bytes 196
  12.6 8.9 %copy-start.6 = (bf16[1,16,4096]{2,1,0:T(8,128)(2,1)S(1)}, bf16[1,16,4096]{2,1,0:T(8,128)(2,1)}, u32[]{:S(2)}) copy-start(bf16[1,16,4096]{2,1,0:T(8,128)(2,1)} %param.9) | copy-start | bytes 393220
  12.6 10.5 %copy-start.7 = (bf16[16,4096]{1,0:T(8,128)(2,1)S(1)}, bf16[16,4096]{1,0:T(8,128)(2,1)}, u32[]{:S(2)}) copy-start(bf16[16,4096]{1,0:T(8,128)(2,1)} %param.10) | copy-start | bytes 393220
  25.1 71.9 %slice-start = ((s8[6291456]{0:T(1024)(128)(4,1)}), s8[2097152]{0:T(1024)(128)(4,1)S(1)}, s32[]{:S(2)}) async-start(s8[6291456]{0:T(1024)(128)(4,1)} %bitcast.138), calls=%async_computation | async-start | bytes 4194304
  90.2 5.4 %copy-start.3 = (bf16[256,4096]{1,0:T(8,128)(2,1)S(1)}, bf16[256,4096]{1,0:T(8,128)(2,1)}, u32[]{:S(2)}) copy-start(bf16[256,4096]{1,0:T(8,128)(2,1)} %get-tuple-element.7) | copy-start | bytes 6291460
  90.2 5.4 %copy-start.14 = (bf16[1,1,384,4096]{3,2,1,0:T(8,128)(2,1)S(1)}, bf16[1,1,384,4096]{3,2,1,0:T(8,128)(2,1)}, u32[]{:S(2)}) copy-start(bf16[1,1,384,4096]{3,2,1,0:T(8,128)(2,1)} %param.17) | copy-start | bytes 9437188
  90.2 6.8 %slice-start.1 = ((s8[6291456]{0:T(1024)(128)(4,1)}), s8[4194304]{0:T(1024)(128)(4,1)S(1)}, s32[]{:S(2)}) async-start(s8[6291456]{0:T(1024)(128)(4,1)} %bitcast.138), calls=%async_computation.1 | async-start | bytes 8388608
  97.0 1.9 copy-start.9
  97.0 1.9 copy-start.10
  98.9 6.1 %copy-start.1 = (bf16[256,4096]{1,0:T(8,128)(2,1)S(1)}, bf16[256,4096]{1,0:T(8,128)(2,1)}, u32[]{:S(2)}) copy-start(bf16[256,4096]{1,0:T(8,128)(2,1)} %get-tuple-element.8) | copy-start | bytes 6291460
  103.8 41.9 %collective-permute-start = (bf16[128,4096]{1,0:T(8,128)(2,1)}, bf16[128,4096]{1,0:T(8,128)(2,1)}, u32[]{:S(2)}, u32[]{:S(2)}) collective-permute-start(bf16[128,4096]{1,0:T(8,128)(2,1)} %constant_dynamic-slice_fusion), channel_id=1, source_target_pairs={{0,1},{1,0},{2,3},{3,2},{4,5},{5,4},{6,7},{7,6},{8,9},{9,8},{10,11... | collective-permute-start | bytes 3145736 | tf_op jit(solution)/shard_map/ppermute | solution.py:287
  118.5 2.2 slice-start.2
  118.5 2.9 %slice-start.3 = ((s8[6291456]{0:T(1024)(128)(4,1)}), s8[2097152]{0:T(1024)(128)(4,1)S(1)}, s32[]{:S(2)}) async-start(s8[6291456]{0:T(1024)(128)(4,1)} %bitcast.140), calls=%async_computation.3 | async-start | bytes 4194304
  133.5 8.8 %copy-start.11 = (f32[2,16,8]{1,2,0:T(8,128)S(1)}, f32[2,16,8]{1,2,0:T(8,128)}, u32[]{:S(2)}) copy-start(f32[2,16,8]{1,2,0:T(8,128)} %param.15) | copy-start | bytes 3076
  142.4 3.3 %copy-start.2 = (bf16[256,4096]{1,0:T(8,128)(2,1)S(1)}, bf16[256,4096]{1,0:T(8,128)(2,1)}, u32[]{:S(2)}) copy-start(bf16[256,4096]{1,0:T(8,128)(2,1)} %fusion.11) | copy-start | bytes 6291460
  145.6 35.6 %copy-start.8 = (bf16[16,4096]{1,0:T(8,128)(2,1)S(1)}, bf16[16,4096]{1,0:T(8,128)(2,1)}, u32[]{:S(2)}) copy-start(bf16[16,4096]{1,0:T(8,128)(2,1)} %param.10) | copy-start | bytes 393220
  145.6 35.6 %copy-start.13 = (f32[16]{0:T(128)S(1)}, f32[16]{0:T(128)}, u32[]{:S(2)}) copy-start(f32[16]{0:T(128)} %copy-done.12) | copy-start | bytes 196
  225.8 5.4 %copy-start = (bf16[384,4096]{1,0:T(8,128)(2,1)S(1)}, bf16[384,4096]{1,0:T(8,128)(2,1)}, u32[]{:S(2)}) copy-start(bf16[384,4096]{1,0:T(8,128)(2,1)} %get-tuple-element.16) | copy-start | bytes 9437188
  225.8 5.4 %copy-start.15 = (bf16[1,1,384,4096]{3,2,1,0:T(8,128)(2,1)S(1)}, bf16[1,1,384,4096]{3,2,1,0:T(8,128)(2,1)}, u32[]{:S(2)}) copy-start(bf16[1,1,384,4096]{3,2,1,0:T(8,128)(2,1)} %param.17) | copy-start | bytes 9437188
  233.4 38.1 %copy-start.4 = (bf16[16,4096]{1,0:T(8,128)(2,1)S(1)}, bf16[16,4096]{1,0:T(8,128)(2,1)}, u32[]{:S(2)}) copy-start(bf16[16,4096]{1,0:T(8,128)(2,1)} %shard_map.93) | copy-start | bytes 393220
  233.4 47.3 %copy-start.5 = (bf16[16,4096]{1,0:T(8,128)(2,1)S(1)}, bf16[16,4096]{1,0:T(8,128)(2,1)}, u32[]{:S(2)}) copy-start(bf16[16,4096]{1,0:T(8,128)(2,1)} %fusion.12.source) | copy-start | bytes 393220
  233.5 2.7 collective-permute-start.1

commit v8 on v5

--- a/solution.py
+++ b/solution.py
@@ -289,18 +289,42 @@
         "rs,rd->sd", weigher * weight[:, None], cot_wide, precision=lax.Precision.HIGHEST
     ).astype(jnp.bfloat16)
     rows_got, grads_got = spread([row_buffer, grad_buffer], 0)
-    per_gu, per_dn, slot_dx, slot_fw = learn_core(rows_got, grads_got, own_gu, own_dn, dp_count)
-    grad_gu = replica_sum(per_gu)
-    grad_dn = replica_sum(per_dn)
-    returned = bring_back(jnp.where(is_learner, slot_dx, slot_fw), 1)
+
+    def learner_side(rows_got, grads_got):
+        per_gu, per_dn, slot_dx, _ = learn_core(rows_got, grads_got, own_gu, own_dn, dp_count)
+        grad_gu = replica_sum(per_gu)
+        grad_dn = replica_sum(per_dn)
+        fresh_gu = renew(own_gu, grad_gu, 0, 0.5 / model_width**0.5)
+        fresh_dn = renew(own_dn, grad_dn, 1, 0.5 / hidden_all**0.5)
+        return (slot_dx, fresh_gu, fresh_dn)
+
+    def rollout_side(rows_got, grads_got):
+        return (forward_core(rows_got, own_gu, own_dn), own_gu, own_dn)
+
+    pieces, fresh_gu, fresh_dn = lax.cond(
+        is_learner, learner_side, rollout_side, rows_got, grads_got
+    )
+    returned = bring_back(pieces, 1)
     mixing = jnp.where(is_learner, picker, weigher)
     base = jnp.where(is_learner, weight[:, None] * cot_wide, tokens.astype(jnp.float32))
     carried = (base + combine(mixing, returned)).astype(jnp.bfloat16)
-    fresh_gu = renew(own_gu, grad_gu, 0, 0.5 / model_width**0.5)
-    fresh_dn = renew(own_dn, grad_dn, 1, 0.5 / hidden_all**0.5)
+    picker, weigher = routing_tables(decode_experts[1], decode_gates[1], capacity, ep_count)
+
+    def learner_wait(carried):
+        return jnp.zeros((ep_count * capacity, model_width), jnp.bfloat16)
+
+    def rollout_send(carried):
+        return exchange([dispatch(picker, carried)], ep_count, 2)[0]
+
+    half_rows = lax.cond(is_learner, learner_wait, rollout_send, carried)
     current = passed_along(carried, "grp", -1)
-    picker, weigher = routing_tables(decode_experts[1], decode_gates[1], capacity, ep_count)
-    (rows_got,) = spread([dispatch(picker, current)], 2)
+    half_rows = passed_along(half_rows, "grp", -1)
+    other_rows = lax.ppermute(half_rows, "dp", [(0, 1), (1, 0)])
+    rows_got = jnp.where(
+        lax.axis_index("dp") == 0,
+        jnp.concatenate([half_rows, other_rows], axis=0),
+        jnp.concatenate([other_rows, half_rows], axis=0),
+    )
     slot_out = forward_core(rows_got, fresh_gu, fresh_dn)
     returned = bring_back(slot_out, 3)
     current = (current.astype(jnp.float32) + combine(weigher, returned)).astype(jnp.bfloat16)

time: 279 us -> 289 us (1.036)
  waiting for transfers between devices: 9.36 us -> 31.3 us
  starting transfers between devices: 5.06 us -> 20.7 us
  matrix products: 38.8 us -> 23.7 us
  other arithmetic: 19.3 us -> 9.5 us
    dot_general x6 -> x0, matrix products: 22 us -> none  [the longest x1 7.47 us: learn_core(): jnp.einsum('pcd,pcgh->pdgh', slot_rows.reshape(rep_count, -1, model_width...]
    ppermute x2 -> x3, waiting for transfers between devices: 7.07 us -> 27.2 us  [passed_along(): return lax.ppermute(block, axis, route)]
    convert_element_type x3 -> x0, local copies, waits for them, and re-layouts: 16.9 us -> none  [the longest x1 8.62 us: renew(): (weights.astype(jnp.float32) - rate * grads / scale).astype(jnp.bfloat16)]
    another operation x0 -> x1, local copies, waits for them, and re-layouts: none -> 16.2 us
    ppermute x2 -> x3, starting transfers between devices: 4.22 us -> 20.1 us  [passed_along(): return lax.ppermute(block, axis, route)]
    unnamed x37 -> x31, local copies, waits for them, and re-layouts: 7.4 us -> 17.6 us
    dot_general x1 -> x0, local copies, waits for them, and re-layouts: 8.8 us -> none  [learn_core(): jnp.dot(slot_rows, weights_gu.reshape(model_width, 2 * hidden_count), pre...]
    dot_general x1 -> x2, matrix products: 5.39 us -> 11.3 us  [forward_core(): jnp.dot(slot_rows, weights_gu.reshape(slot_rows.shape[1], 2 * hidden_coun...]
  transfers between devices with their start and end apart: 4 -> 6, of which waited for: 2 -> 4; matrix products, arithmetic and copies ran while one was open for 15% -> 1% of each run, Pallas kernels for 0% -> 12%
where the time goes in v8:
time: 289 us; the launch traced here: 288 us
  Pallas kernels  164 us (57%)
  local copies, waits for them, and re-layouts  38.6 us (13%)
  waiting for transfers between devices  31.3 us (11%)
  matrix products  23.7 us (8%)
  starting transfers between devices  20.7 us (7%)
  other arithmetic  9.5 us (3%)
    pallas_call x4, Pallas kernels, exchange(): pl.pallas_call(functools.partial(exchange_kernel, count, width, share), o...  164 us
    ppermute x3, waiting for transfers between devices, passed_along(): return lax.ppermute(block, axis, route)  27.2 us
    ppermute x3, starting transfers between devices, passed_along(): return lax.ppermute(block, axis, route)  20.1 us
    unnamed x31, local copies, waits for them, and re-layouts  17.6 us
    another operation x1, local copies, waits for them, and re-layouts  16.2 us
    dot_general x2, matrix products, forward_core(): jnp.dot(slot_rows, weights_gu.reshape(slot_rows.shape[1], 2 * hidden_coun...  11.3 us
  transfers between devices with their start and end apart: 6, of which 4 were waited for; matrix products, arithmetic and copies ran while one was open for 1% of the time, Pallas kernels for 12%

profile of v8, /device:TPU:4, one launch (start us, length us, event | category | flops | bytes accessed | tf_op | source)
XLA Modules:
  0.0 288.1 jit_solution(16089656006531524401)
XLA Ops:
  0.0 0.0 slice-start.2
  0.0 0.0 copy-start.16
  0.0 0.7 slice-done.2
  0.8 0.1 copy.57
  0.8 0.1 eq.72
  0.9 0.1 fusion.49
  1.0 0.2 reduce_window_sum.25
  1.2 0.2 select_reduce_fusion.1
  1.4 0.1 reduce_sum.92
  1.4 0.1 copy.58
  1.5 0.6 bitcast_add_fusion
  2.1 0.1 copy.50
  2.2 0.1 eq.65
  2.3 0.1 fusion.50
  2.4 0.2 reduce_window_sum.24
  2.6 0.2 select_reduce_fusion.3
  2.7 0.1 reduce_sum.88
  2.8 0.1 copy.51
  2.9 0.1 copy.52
  3.0 0.1 copy.53
  3.1 0.2 reduce-window.8
  3.3 0.1 select_reduce_fusion.4
  3.4 0.0 copy-start.6
  3.4 0.0 copy-start.8
  3.4 16.2 %copy.54 = bf16[1,1,4096,2,384]{2,4,3,1,0:T(8,128)(2,1)} copy(bf16[1,1,4096,2,384]{4,3,2,1,0:T(2,128)(2,1)} %param.20) | data formatting | bytes 12582912 | tf_op args[7]
  19.6 0.1 select_reduce_fusion.2
  19.7 1.4 convolution_convert_fusion.4.refs_0_
  21.2 2.1 convolution_convert_fusion.3.refs_1_
  23.3 65.0 %shard_map.91 = (bf16[256,4096]{1,0:T(8,128)(2,1)}, bf16[256,4096]{1,0:T(8,128)(2,1)}) custom-call(bf16[128,4096]{1,0:T(8,128)(2,1)} %convolution_convert_fusion.4.refs_0_, bf16[128,4096]{1,0:T(8,128)(2,1)} %convolution_convert_fusion.3.refs_1_), custom_call_target="tpu_custom_call" | custom-call | bytes 12582912 | tf_op jit(solution)/shard_map/pallas_call | solution.py:120
  88.3 24.1 %conditional.3 = (bf16[256,4096]{1,0:T(8,128)(2,1)}, bf16[4096,2,384]{0,2,1:T(8,128)(2,1)}, bf16[384,4096]{1,0:T(8,128)(2,1)S(1)}) conditional(s32[]{:T(128)} %convert_element_type.140, (bf16[1,1,4096,2,384]{4,3,2,1,0:T(2,128)(2,1)}, bf16[256,4096]{1,0:T(8,128)(2,1)}, bf16[384,4096]{1,0:T(8,128)(2,1)S(1)}, ...), branch_computations={%region_6.7_spmd, %region_7.10_spmd} | conditional | flops 6515491840 | bytes 220612896
  88.3 16.2 %copy.55 = bf16[1,1,4096,2,384]{2,4,3,1,0:T(8,128)(2,1)} copy(bf16[1,1,4096,2,384]{4,3,2,1,0:T(2,128)(2,1)} %get-tuple-element.75) | data formatting | bytes 12582912 | tf_op jit(solution)/shard_map
  104.6 5.2 %fusion = f32[256,2,384]{2,0,1:T(8,128)S(1)} fusion(bf16[1,1,4096,2,384]{2,4,3,1,0:T(8,128)(2,1)} %copy.55, bf16[256,4096]{1,0:T(8,128)(2,1)} %get-tuple-element.36), kind=kOutput, calls=%fused_computation | convolution fusion | flops 1610612736 | bytes 9175040 | tf_op jit(solution)/shard_map/cond/branch_0_fun/dot_general | solution.py:183
  109.8 2.6 fusion.5
  112.4 2.3 constant_dynamic-slice_fusion
  114.8 0.4 collective-permute-start
  115.2 0.8 copy.59
  115.9 0.7 fusion.48
  116.6 1.2 collective-permute-done
  117.8 2.8 add_convert_fusion.1.refs_0_
  120.6 33.5 %shard_map.92 = bf16[128,4096]{1,0:T(8,128)(2,1)} custom-call(bf16[128,4096]{1,0:T(8,128)(2,1)} %add_convert_fusion.1.refs_0_), custom_call_target="tpu_custom_call" | custom-call | bytes 4194304 | tf_op jit(solution)/shard_map/pallas_call | solution.py:120
  154.1 1.8 fusion.34
  155.9 34.0 %conditional.4 = (bf16[128,4096]{1,0:T(8,128)(2,1)}) conditional(s32[]{:T(128)} %convert_element_type.140, (f32[16,8,128]{2,1,0:T(8,128)}, bf16[16,4096]{1,0:T(8,128)(2,1)S(1)}) %tuple.24, () %tuple.25), branch_computations={%region_13.15_spmd, %region_15.16_spmd} | conditional | flops 17315840 | bytes 5447692 | solution.py:319
  155.9 0.9 reduce_sum.77
  156.7 1.4 convolution_convert_fusion.1.refs_0_
  158.2 31.7 %branch_0_fun.1 = bf16[128,4096]{1,0:T(8,128)(2,1)} custom-call(bf16[128,4096]{1,0:T(8,128)(2,1)} %convolution_convert_fusion.1.refs_0_), custom_call_target="tpu_custom_call" | custom-call | bytes 4194304 | tf_op jit(solution)/shard_map/cond/branch_0_fun/pallas_call | solution.py:120
  189.9 12.9 %collective-permute-start.2 = (bf16[128,4096]{1,0:T(8,128)(2,1)}, bf16[128,4096]{1,0:T(8,128)(2,1)}, u32[]{:S(2)}, u32[]{:S(2)}) collective-permute-start(bf16[128,4096]{1,0:T(8,128)(2,1)} %get-tuple-element.102), channel_id=1, source_target_pairs={{128,0},{129,1},{130,2},{131,3},{132,4},{133,5},{134,6},{135,7},{1... | collective-permute-start | bytes 3145736 | tf_op jit(solution)/shard_map/ppermute | solution.py:146
  202.8 20.1 %collective-permute-done.2 = bf16[128,4096]{1,0:T(8,128)(2,1)} collective-permute-done((bf16[128,4096]{1,0:T(8,128)(2,1)}, bf16[128,4096]{1,0:T(8,128)(2,1)}, u32[]{:S(2)}, u32[]{:S(2)}) %collective-permute-start.2) | collective-permute-done | bytes 1048608 | tf_op jit(solution)/shard_map/ppermute | solution.py:146
  222.9 3.0 %collective-permute-done.3 = bf16[128,4096]{1,0:T(8,128)(2,1)} collective-permute-done((bf16[128,4096]{1,0:T(8,128)(2,1)}, bf16[128,4096]{1,0:T(8,128)(2,1)}, u32[]{:S(2)}, u32[]{:S(2)}) %collective-permute-start.3) | collective-permute-done | bytes 1048608 | tf_op jit(solution)/shard_map/ppermute | solution.py:322
  225.9 6.1 %fusion.32 = f32[256,2,384]{2,0,1:T(8,128)S(1)} fusion(bf16[4096,2,384]{0,2,1:T(8,128)(2,1)} %get-tuple-element.55, bf16[128,4096]{1,0:T(8,128)(2,1)} %collective-permute-done.3, bf16[128,4096]{1,0:T(8,128)(2,1)} %collective-permute-done.2, pred[]{:T(512)S(6)} %eq.79), kind=kOutput, calls=%fused_computation.54 | convolution fusion | flops 1620049920 | bytes 9175041 | tf_op jit(solution)/shard_map/dot_general | solution.py:183
  232.0 0.0 copy-start.17
  232.0 1.3 convolution_convert_fusion.2
  233.3 1.3 copy-done.2
  234.6 0.1 constant_dynamic-slice_fusion.1
  234.7 0.2 collective-permute-start.4
  235.0 0.1 copy.60
  235.0 0.1 select_reduce_fusion
  235.1 5.9 %collective-permute-start.1 = (bf16[16,4096]{1,0:T(8,128)(2,1)S(1)}, bf16[16,4096]{1,0:T(8,128)(2,1)S(1)}, u32[]{:S(2)}, u32[]{:S(2)}) collective-permute-start(bf16[16,4096]{1,0:T(8,128)(2,1)S(1)} %fusion.34), channel_id=1, source_target_pairs={{128,0},{129,1},{130,2},{131,3},{132,4},{133,5},{134,6},{135,7},{1... | collective-permute-start | bytes 393224 | tf_op jit(solution)/shard_map/ppermute | solution.py:146
  241.1 2.5 add_convert_fusion.refs_0_
  243.5 33.7 %shard_map.93 = bf16[128,4096]{1,0:T(8,128)(2,1)} custom-call(bf16[128,4096]{1,0:T(8,128)(2,1)} %add_convert_fusion.refs_0_), custom_call_target="tpu_custom_call" | custom-call | bytes 4194304 | tf_op jit(solution)/shard_map/pallas_call | solution.py:120
  277.3 0.0 collective-permute-done.1
  277.3 1.7 add_convert_fusion.2
  279.0 1.3 collective-permute-start.5
  280.3 7.1 %collective-permute-done.5 = bf16[16,4096]{1,0:T(8,128)(2,1)S(1)} collective-permute-done((bf16[16,4096]{1,0:T(8,128)(2,1)S(1)}, bf16[16,4096]{1,0:T(8,128)(2,1)S(1)}, u32[]{:S(2)}, u32[]{:S(2)}) %collective-permute-start.5) | collective-permute-done | bytes 131104 | tf_op jit(solution)/shard_map/ppermute | solution.py:146
  287.4 0.7 select_bitcast_fusion
  (33 shorter events, 0.1 us)
Async XLA Ops:
  0.0 3.1 %copy-start.21 = (s32[4]{0:T(128)S(1)}, s32[4]{0:T(128)}, u32[]{:S(2)}) copy-start(s32[4]{0:T(128)} %param.15) | copy-start | bytes 52
  0.0 1.5 copy-start.18
  0.0 3.0 %copy-start.19 = (f32[16,8]{0,1:T(8,128)S(1)}, f32[16,8]{0,1:T(8,128)}, u32[]{:S(2)}) copy-start(f32[16,8]{0,1:T(8,128)} %param.17) | copy-start | bytes 1540
  0.0 0.7 slice-start.2
  0.0 1.5 copy-start.15
  0.0 3.0 %copy-start.16 = (f32[2,16,8]{1,2,0:T(8,128)S(1)}, f32[2,16,8]{1,2,0:T(8,128)}, u32[]{:S(2)}) copy-start(f32[2,16,8]{1,2,0:T(8,128)} %param.19) | copy-start | bytes 3076
  3.4 17.8 %copy-start.20 = (f32[16]{0:T(128)}, f32[16]{0:T(128)S(1)}, u32[]{:S(2)}) copy-start(f32[16]{0:T(128)S(1)} %add_divide_fusion) | copy-start | bytes 196
  3.4 16.3 %copy-start.6 = (bf16[1,16,4096]{2,1,0:T(8,128)(2,1)S(1)}, bf16[1,16,4096]{2,1,0:T(8,128)(2,1)}, u32[]{:S(2)}) copy-start(bf16[1,16,4096]{2,1,0:T(8,128)(2,1)} %param.13) | copy-start | bytes 393220
  3.4 17.8 %copy-start.8 = (bf16[16,4096]{1,0:T(8,128)(2,1)S(1)}, bf16[16,4096]{1,0:T(8,128)(2,1)}, u32[]{:S(2)}) copy-start(bf16[16,4096]{1,0:T(8,128)(2,1)} %param.14) | copy-start | bytes 393220
  19.6 68.7 %copy-start.1 = (bf16[1,1,384,4096]{3,2,1,0:T(8,128)(2,1)S(1)}, bf16[1,1,384,4096]{3,2,1,0:T(8,128)(2,1)}, u32[]{:S(2)}) copy-start(bf16[1,1,384,4096]{3,2,1,0:T(8,128)(2,1)} %param.21) | copy-start | bytes 9437188
  112.4 41.7 %copy-start.7 = (bf16[1,16,4096]{2,1,0:T(8,128)(2,1)S(1)}, bf16[1,16,4096]{2,1,0:T(8,128)(2,1)}, u32[]{:S(2)}) copy-start(bf16[1,16,4096]{2,1,0:T(8,128)(2,1)} %param.13) | copy-start | bytes 393220
  112.4 41.7 %copy-start.9 = (bf16[16,4096]{1,0:T(8,128)(2,1)S(1)}, bf16[16,4096]{1,0:T(8,128)(2,1)}, u32[]{:S(2)}) copy-start(bf16[16,4096]{1,0:T(8,128)(2,1)} %param.14) | copy-start | bytes 393220
  114.8 3.0 %collective-permute-start = (bf16[128,4096]{1,0:T(8,128)(2,1)}, bf16[128,4096]{1,0:T(8,128)(2,1)}, u32[]{:S(2)}, u32[]{:S(2)}) collective-permute-start(bf16[128,4096]{1,0:T(8,128)(2,1)} %constant_dynamic-slice_fusion), channel_id=1, source_target_pairs={{0,1},{1,0},{2,3},{3,2},{4,5},{5,4},{6,7},{7,6},{8,9},{9,8},{10,11... | collective-permute-start | bytes 3145736 | tf_op jit(solution)/shard_map/ppermute | solution.py:259
  115.9 4.7 %copy-start.13 = (s32[16,8]{1,0:T(8,128)}, s32[16,8]{1,0:T(8,128)S(1)}, u32[]{:S(2)}) copy-start(s32[16,8]{1,0:T(8,128)S(1)} %copy.59) | copy-start | bytes 1540
  189.9 33.0 %collective-permute-start.2 = (bf16[128,4096]{1,0:T(8,128)(2,1)}, bf16[128,4096]{1,0:T(8,128)(2,1)}, u32[]{:S(2)}, u32[]{:S(2)}) collective-permute-start(bf16[128,4096]{1,0:T(8,128)(2,1)} %get-tuple-element.102), channel_id=1, source_target_pairs={{128,0},{129,1},{130,2},{131,3},{132,4},{133,5},{134,6},{135,7},{1... | collective-permute-start | bytes 3145736 | tf_op jit(solution)/shard_map/ppermute | solution.py:146
  222.9 3.0 %collective-permute-start.3 = (bf16[128,4096]{1,0:T(8,128)(2,1)}, bf16[128,4096]{1,0:T(8,128)(2,1)}, u32[]{:S(2)}, u32[]{:S(2)}) collective-permute-start(bf16[128,4096]{1,0:T(8,128)(2,1)} %collective-permute-done.2), channel_id=1, source_target_pairs={{0,1},{1,0},{2,3},{3,2},{4,5},{5,4},{6,7},{7,6},{8,9},{9,8},{10,11... | collective-permute-start | bytes 3145736 | tf_op jit(solution)/shard_map/ppermute | solution.py:322
  232.0 2.9 %copy-start.17 = (f32[2,16,8]{1,2,0:T(8,128)S(1)}, f32[2,16,8]{1,2,0:T(8,128)}, u32[]{:S(2)}) copy-start(f32[2,16,8]{1,2,0:T(8,128)} %param.19) | copy-start | bytes 3076
  232.0 3.0 %copy-start.14 = (s32[16,8]{1,0:T(8,128)S(1)}, s32[16,8]{1,0:T(8,128)}, u32[]{:S(2)}) copy-start(s32[16,8]{1,0:T(8,128)} %copy-done.13) | copy-start | bytes 1540
  233.3 1.3 copy-start.2
  234.7 6.3 %collective-permute-start.4 = (bf16[128,4096]{1,0:T(8,128)(2,1)S(1)}, bf16[128,4096]{1,0:T(8,128)(2,1)S(1)}, u32[]{:S(2)}, u32[]{:S(2)}) collective-permute-start(bf16[128,4096]{1,0:T(8,128)(2,1)S(1)} %constant_dynamic-slice_fusion.1), channel_id=1, source_target_pairs={{0,1},{1,0},{2,3},{3,2},{4,5},{5,4},{6,7},{7,6},{8,9},{9,8},{10,11... | collective-permute-start | bytes 3145736 | tf_op jit(solution)/shard_map/ppermute | solution.py:259
  235.1 42.1 %collective-permute-start.1 = (bf16[16,4096]{1,0:T(8,128)(2,1)S(1)}, bf16[16,4096]{1,0:T(8,128)(2,1)S(1)}, u32[]{:S(2)}, u32[]{:S(2)}) collective-permute-start(bf16[16,4096]{1,0:T(8,128)(2,1)S(1)} %fusion.34), channel_id=1, source_target_pairs={{128,0},{129,1},{130,2},{131,3},{132,4},{133,5},{134,6},{135,7},{1... | collective-permute-start | bytes 393224 | tf_op jit(solution)/shard_map/ppermute | solution.py:146
  279.0 8.4 %collective-permute-start.5 = (bf16[16,4096]{1,0:T(8,128)(2,1)S(1)}, bf16[16,4096]{1,0:T(8,128)(2,1)S(1)}, u32[]{:S(2)}, u32[]{:S(2)}) collective-permute-start(bf16[16,4096]{1,0:T(8,128)(2,1)S(1)} %add_convert_fusion.2), channel_id=1, source_target_pairs={{0,128},{1,129},{2,130},{3,131},{4,132},{5,133},{6,134},{7,135},{8... | collective-permute-start | bytes 393224 | tf_op jit(solution)/shard_map/ppermute | solution.py:146

commit v9 on v5

--- a/solution.py
+++ b/solution.py
@@ -261,8 +261,11 @@
         return exchange([summed], ep_count, tag)[0]
 
     def combine(mixing, returned):
-        total = returned.astype(jnp.float32)
-        return jnp.einsum("rs,sd->rd", mixing, total, precision=lax.Precision.HIGHEST)
+        high = mixing.astype(jnp.bfloat16)
+        low = (mixing - high.astype(jnp.float32)).astype(jnp.bfloat16)
+        return jnp.dot(high, returned, preferred_element_type=jnp.float32) + jnp.dot(
+            low, returned, preferred_element_type=jnp.float32
+        )
 
     def dispatch(picker, values):
         buffer = jnp.einsum(
@@ -285,8 +288,12 @@
     picker, weigher = routing_tables(route_ids, route_gates, capacity, ep_count)
     row_buffer = dispatch(picker, tokens)
     cot_wide = cotangent.astype(jnp.float32)
-    grad_buffer = jnp.einsum(
-        "rs,rd->sd", weigher * weight[:, None], cot_wide, precision=lax.Precision.HIGHEST
+    scaled = weigher * weight[:, None]
+    scaled_high = scaled.astype(jnp.bfloat16)
+    scaled_low = (scaled - scaled_high.astype(jnp.float32)).astype(jnp.bfloat16)
+    grad_buffer = (
+        jnp.einsum("rs,rd->sd", scaled_high, cotangent, preferred_element_type=jnp.float32)
+        + jnp.einsum("rs,rd->sd", scaled_low, cotangent, preferred_element_type=jnp.float32)
     ).astype(jnp.bfloat16)
     rows_got, grads_got = spread([row_buffer, grad_buffer], 0)
     per_gu, per_dn, slot_dx, slot_fw = learn_core(rows_got, grads_got, own_gu, own_dn, dp_count)

time: 279 us -> 283 us (1.014)
  matrix products: 38.8 us -> 42 us
    dot_general x3 -> x6, matrix products: 6.22 us -> 10.4 us  [the longest x2 3.62 us: combine(): jnp.dot(high, returned, preferred_element_type=jnp.float32)]
    unnamed x37 -> x41, local copies, waits for them, and re-layouts: 7.4 us -> 6.63 us
  transfers between devices with their start and end apart: 4 -> 4, of which waited for: 2 -> 2; matrix products, arithmetic and copies ran while one was open for 15% -> 14% of each run, Pallas kernels for 0% -> 0%
where the time goes in v9:
time: 283 us; the launch traced here: 281 us
  Pallas kernels  165 us (58%)
  matrix products  42 us (15%)
  local copies, waits for them, and re-layouts  40 us (14%)
  other arithmetic  19.4 us (7%)
  waiting for transfers between devices  9.36 us (3%)
  starting transfers between devices  5.02 us (2%)
    pallas_call x4, Pallas kernels, exchange(): pl.pallas_call(functools.partial(exchange_kernel, count, width, share), o...  165 us
    dot_general x1, local copies, waits for them, and re-layouts, learn_core(): jnp.dot(slot_rows, weights_gu.reshape(model_width, 2 * hidden_count), pre...  8.79 us
    convert_element_type x1, local copies, waits for them, and re-layouts, renew(): (weights.astype(jnp.float32) - rate * grads / scale).astype(jnp.bfloat16)  8.73 us
    convert_element_type x2, local copies, waits for them, and re-layouts, replica_sum(): per_replica[replica].astype(jnp.bfloat16)  8.48 us
    ppermute x2, waiting for transfers between devices, passed_along(): return lax.ppermute(block, axis, route)  7.07 us
    unnamed x41, local copies, waits for them, and re-layouts  6.63 us
    dot_general x1, matrix products, learn_core(): jnp.einsum('pcd,pcgh->pdgh', slot_rows.reshape(rep_count, -1, model_width...  6.43 us
  transfers between devices with their start and end apart: 4, of which 2 were waited for; matrix products, arithmetic and copies ran while one was open for 14% of the time, Pallas kernels for 0%

profile of v9, /device:TPU:4, one launch (start us, length us, event | category | flops | bytes accessed | tf_op | source)
XLA Modules:
  0.0 281.5 jit_solution(13998734105104721605)
XLA Ops:
  0.0 0.7 slice.44
  0.7 0.1 copy.49
  0.8 0.1 eq.69
  0.9 0.1 fusion.43
  1.0 0.2 reduce_window_sum.25
  1.1 0.2 select_reduce_fusion.1
  1.3 0.1 reduce_sum.91
  1.4 0.1 copy.50
  1.5 0.7 bitcast_add_fusion
  2.3 0.1 eq.62
  2.4 0.1 fusion.44
  2.4 0.2 reduce_window_sum.24
  2.6 0.2 select_reduce_fusion.3
  2.8 0.1 reduce_sum.87
  2.9 0.1 copy.44
  3.0 0.1 copy.45
  3.0 0.7 bitcast_select_fusion
  3.8 0.8 reduce-window.8
  4.6 0.7 bitcast_subtract_fusion
  5.3 0.7 select_reduce_fusion.4
  6.1 0.1 select_reduce_fusion.2
  6.2 1.4 fusion.45
  7.6 2.4 fusion.12.refs_1_
  10.0 6.5 %copy.63 = bf16[512,8,2,384]{3,1,2,0:T(8,128)(2,1)} copy(bf16[512,8,2,384]{3,2,1,0:T(2,128)(2,1)} %bitcast.139) | data formatting | bytes 12582912
  16.6 8.8 %copy.47 = bf16[768,4096]{1,0:T(8,128)(2,1)} copy(bf16[768,4096]{0,1:T(8,128)(2,1)} %bitcast.138) | data formatting | bytes 12582912 | tf_op jit(solution)/shard_map/dot_general | solution.py:197
  25.4 1.5 convolution_convert_fusion.5.refs_0_
  26.9 65.1 %shard_map.91 = (bf16[256,4096]{1,0:T(8,128)(2,1)}, bf16[256,4096]{1,0:T(8,128)(2,1)}) custom-call(bf16[128,4096]{1,0:T(8,128)(2,1)} %convolution_convert_fusion.5.refs_0_, bf16[128,4096]{1,0:T(8,128)(2,1)} %fusion.12.refs_1_), custom_call_target="tpu_custom_call" | custom-call | bytes 12582912 | tf_op jit(solution)/shard_map/pallas_call | solution.py:120
  92.0 5.4 %fusion.19 = f32[256,2,384]{2,0,1:T(8,128)S(1)} fusion(bf16[2,384,4096]{2,1,0:T(8,128)(2,1)} %bitcast.144, bf16[256,4096]{1,0:T(8,128)(2,1)} %get-tuple-element.8), kind=kOutput, calls=%fused_computation.34 | convolution fusion | flops 1610612736 | bytes 9175040 | tf_op jit(solution)/shard_map/dot_general | solution.py:197
  97.4 1.3 fusion.34
  98.8 1.8 fusion.8
  100.7 2.6 fusion.11
  103.3 2.5 constant_dynamic-slice_fusion
  105.8 0.4 collective-permute-start
  106.1 1.9 fusion.67
  108.1 6.4 %convolution_convert_fusion = bf16[2,4096,2,384]{3,1,2,0:T(8,128)(2,1)} fusion(bf16[2,128,4096,1]{2,1,3,0:T(8,128)(2,1)S(1)} %bitcast.145, bf16[2,128,1,384]{3,1,2,0:T(8,128)(2,1)S(1)} %bitcast.152, bf16[2,128,1,384]{3,1,2,0:T(8,128)(2,1)S(1)} %bitcast.150), kind=kOutput, calls=%fused_computation.3 | convolution fusion | flops 1617690624 | bytes 15073280 | tf_op jit(solution)/shard_map/pcd,pcgh->pdgh/dot_general | solution.py:219
  114.5 6.2 %slice_bitcast_fusion.1 = (bf16[4096,2,384]{2,0,1:T(8,128)(2,1)S(1)}, bf16[4096,2,384]{2,0,1:T(8,128)(2,1)S(1)}) fusion(bf16[2,4096,2,384]{3,1,2,0:T(8,128)(2,1)} %convolution_convert_fusion), kind=kLoop, calls=%fused_computation.6 | loop fusion | bytes 25165824 | tf_op jit(solution)/shard_map/convert_element_type | solution.py:170
  120.7 2.0 multiply_reduce_fusion
  122.8 5.0 %subtract_convert_fusion = bf16[4096,2,384]{2,0,1:T(8,128)(2,1)} fusion(bf16[4096,2,384]{2,0,1:T(8,128)(2,1)S(1)} %get-tuple-element.14, bf16[4096,2,384]{2,0,1:T(8,128)(2,1)S(1)} %get-tuple-element.13, f32[2,384]{1,0:T(2,128)S(1)} %add_sqrt_fusion, bf16[1,1,4096,2,384]{4,3,2,1,0:T(2,128)(2,1)S(1)} %bitcast.143), kind=kLoop, calls=%fused_computation | loop fusion | flops 25165824 | bytes 25168896 | tf_op jit(solution)/shard_map/convert_element_type | solution.py:178
  127.8 1.1 copy.58
  128.9 0.2 copy.59
  129.1 3.4 %convolution_convert_fusion.1 = bf16[2,384,4096]{2,1,0:T(8,128)(2,1)S(1)} fusion(bf16[2,128,4096]{2,1,0:T(8,128)(2,1)} %bitcast.146, f32[2,128,384]{1,2,0:T(8,128)S(1)} %copy.59, f32[2,128,384]{1,2,0:T(8,128)S(1)} %copy.58), kind=kOutput, calls=%fused_computation.4 | convolution fusion | flops 809041920 | bytes 9175040 | tf_op jit(solution)/shard_map/pch,pcd->phd/dot_general | solution.py:213
  132.5 2.3 slice_bitcast_fusion.3
  134.8 3.1 %multiply_reduce_fusion.1 = f32[384]{0:T(512)S(1)} fusion(bf16[384,4096]{1,0:T(8,128)(2,1)} %get-tuple-element.16, bf16[384,4096]{1,0:T(8,128)(2,1)S(1)} %get-tuple-element.15), kind=kLoop, calls=%fused_computation.12 | loop fusion | flops 7863936 | bytes 6292992 | tf_op jit(solution)/shard_map/reduce_sum | solution.py:177
  138.0 2.5 add_convert_fusion.1.refs_0_
  140.5 33.0 %shard_map.92 = bf16[128,4096]{1,0:T(8,128)(2,1)} custom-call(bf16[128,4096]{1,0:T(8,128)(2,1)} %add_convert_fusion.1.refs_0_), custom_call_target="tpu_custom_call" | custom-call | bytes 4194304 | tf_op jit(solution)/shard_map/pallas_call | solution.py:120
  173.5 1.5 fusion.46
  175.0 2.1 fusion.14
  177.2 2.9 %collective-permute-start.1 = (bf16[16,4096]{1,0:T(8,128)(2,1)}, bf16[16,4096]{1,0:T(8,128)(2,1)S(1)}, u32[]{:S(2)}, u32[]{:S(2)}) collective-permute-start(bf16[16,4096]{1,0:T(8,128)(2,1)} %fusion.14), channel_id=1, source_target_pairs={{128,0},{129,1},{130,2},{131,3},{132,4},{133,5},{134,6},{135,7},{1... | collective-permute-start | bytes 393224 | tf_op jit(solution)/shard_map/ppermute | solution.py:146
  180.1 8.7 %copy.56 = bf16[4096,2,384]{0,2,1:T(8,128)(2,1)} copy(bf16[4096,2,384]{2,0,1:T(8,128)(2,1)} %subtract_convert_fusion) | data formatting | bytes 12582912 | tf_op jit(solution)/shard_map/convert_element_type | solution.py:178
  189.0 0.1 select_reduce_fusion
  189.1 1.5 convolution_convert_fusion.4.refs_0_
  190.6 34.1 %shard_map.93 = bf16[256,4096]{1,0:T(8,128)(2,1)} custom-call(bf16[128,4096]{1,0:T(8,128)(2,1)} %convolution_convert_fusion.4.refs_0_), custom_call_target="tpu_custom_call" | custom-call | bytes 6291456 | tf_op jit(solution)/shard_map/pallas_call | solution.py:120
  224.7 5.4 %fusion = f32[256,2,384]{2,0,1:T(8,128)S(1)} fusion(bf16[4096,2,384]{0,2,1:T(8,128)(2,1)} %copy.56, bf16[256,4096]{1,0:T(8,128)(2,1)} %shard_map.93), kind=kOutput, calls=%fused_computation.7 | convolution fusion | flops 1610612736 | bytes 9175040 | tf_op jit(solution)/shard_map/dot_general | solution.py:183
  230.1 2.2 convolution_convert_fusion.2
  232.3 0.1 constant_dynamic-slice_fusion.1
  232.4 0.5 collective-permute-start.2
  232.8 2.3 collective-permute-done.2
  235.1 1.2 add_convert_fusion.refs_0_
  236.4 33.1 %shard_map.94 = bf16[128,4096]{1,0:T(8,128)(2,1)} custom-call(bf16[128,4096]{1,0:T(8,128)(2,1)} %add_convert_fusion.refs_0_), custom_call_target="tpu_custom_call" | custom-call | bytes 4194304 | tf_op jit(solution)/shard_map/pallas_call | solution.py:120
  269.5 1.5 fusion.47
  271.0 1.5 add_convert_fusion.2
  272.4 1.3 collective-permute-start.3
  273.7 7.1 %collective-permute-done.3 = bf16[16,4096]{1,0:T(8,128)(2,1)S(1)} collective-permute-done((bf16[16,4096]{1,0:T(8,128)(2,1)S(1)}, bf16[16,4096]{1,0:T(8,128)(2,1)S(1)}, u32[]{:S(2)}, u32[]{:S(2)}) %collective-permute-start.3) | collective-permute-done | bytes 131104 | tf_op jit(solution)/shard_map/ppermute | solution.py:146
  280.8 0.7 select_bitcast_fusion
  (54 shorter events, 0.4 us)
Async XLA Ops:
  6.1 10.5 %copy-start.12 = (f32[16]{0:T(128)}, f32[16]{0:T(128)S(1)}, u32[]{:S(2)}) copy-start(f32[16]{0:T(128)S(1)} %add_divide_fusion) | copy-start | bytes 196
  16.6 8.8 %copy-start.6 = (bf16[1,16,4096]{2,1,0:T(8,128)(2,1)S(1)}, bf16[1,16,4096]{2,1,0:T(8,128)(2,1)}, u32[]{:S(2)}) copy-start(bf16[1,16,4096]{2,1,0:T(8,128)(2,1)} %param.9) | copy-start | bytes 393220
  26.9 71.9 %slice-start = ((s8[6291456]{0:T(1024)(128)(4,1)}), s8[2097152]{0:T(1024)(128)(4,1)S(1)}, s32[]{:S(2)}) async-start(s8[6291456]{0:T(1024)(128)(4,1)} %bitcast.140), calls=%async_computation | async-start | bytes 4194304
  92.0 5.4 %copy-start.3 = (bf16[256,4096]{1,0:T(8,128)(2,1)S(1)}, bf16[256,4096]{1,0:T(8,128)(2,1)}, u32[]{:S(2)}) copy-start(bf16[256,4096]{1,0:T(8,128)(2,1)} %get-tuple-element.7) | copy-start | bytes 6291460
  92.0 5.4 %copy-start.14 = (bf16[1,1,384,4096]{3,2,1,0:T(8,128)(2,1)S(1)}, bf16[1,1,384,4096]{3,2,1,0:T(8,128)(2,1)}, u32[]{:S(2)}) copy-start(bf16[1,1,384,4096]{3,2,1,0:T(8,128)(2,1)} %param.17) | copy-start | bytes 9437188
  92.0 6.8 %slice-start.1 = ((s8[6291456]{0:T(1024)(128)(4,1)}), s8[4194304]{0:T(1024)(128)(4,1)S(1)}, s32[]{:S(2)}) async-start(s8[6291456]{0:T(1024)(128)(4,1)} %bitcast.140), calls=%async_computation.1 | async-start | bytes 8388608
  97.4 3.3 %copy-start.5 = (f32[256,2,384]{2,0,1:T(8,128)}, f32[256,2,384]{2,0,1:T(8,128)S(1)}, u32[]{:S(2)}) copy-start(f32[256,2,384]{2,0,1:T(8,128)S(1)} %fusion.19) | copy-start | bytes 2359300
  98.8 1.9 copy-start.7
  98.8 1.9 copy-start.9
  103.3 4.8 %copy-start.1 = (bf16[256,4096]{1,0:T(8,128)(2,1)S(1)}, bf16[256,4096]{1,0:T(8,128)(2,1)}, u32[]{:S(2)}) copy-start(bf16[256,4096]{1,0:T(8,128)(2,1)} %get-tuple-element.8) | copy-start | bytes 6291460
  103.3 4.8 %copy-start.8 = (bf16[256,384]{1,0:T(8,128)(2,1)S(1)}, bf16[256,384]{1,0:T(8,128)(2,1)}, u32[]{:S(2)}) copy-start(bf16[256,384]{1,0:T(8,128)(2,1)} %copy-done.7) | copy-start | bytes 589828
  103.3 4.8 %copy-start.10 = (bf16[256,384]{1,0:T(8,128)(2,1)S(1)}, bf16[256,384]{1,0:T(8,128)(2,1)}, u32[]{:S(2)}) copy-start(bf16[256,384]{1,0:T(8,128)(2,1)} %copy-done.9) | copy-start | bytes 589828
  105.8 32.2 %collective-permute-start = (bf16[128,4096]{1,0:T(8,128)(2,1)}, bf16[128,4096]{1,0:T(8,128)(2,1)}, u32[]{:S(2)}, u32[]{:S(2)}) collective-permute-start(bf16[128,4096]{1,0:T(8,128)(2,1)} %constant_dynamic-slice_fusion), channel_id=1, source_target_pairs={{0,1},{1,0},{2,3},{3,2},{4,5},{5,4},{6,7},{7,6},{8,9},{9,8},{10,11... | collective-permute-start | bytes 3145736 | tf_op jit(solution)/shard_map/ppermute | solution.py:259
  108.1 14.7 %slice-start.2 = ((s8[6291456]{0:T(1024)(128)(4,1)}), s8[4194304]{0:T(1024)(128)(4,1)S(1)}, s32[]{:S(2)}) async-start(s8[6291456]{0:T(1024)(128)(4,1)} %bitcast.142), calls=%async_computation.2 | async-start | bytes 8388608
  114.5 8.3 %slice-start.3 = ((s8[6291456]{0:T(1024)(128)(4,1)}), s8[2097152]{0:T(1024)(128)(4,1)S(1)}, s32[]{:S(2)}) async-start(s8[6291456]{0:T(1024)(128)(4,1)} %bitcast.142), calls=%async_computation.3 | async-start | bytes 4194304
  132.5 2.3 copy-start.11
  134.8 3.2 %copy-start.2 = (bf16[256,4096]{1,0:T(8,128)(2,1)S(1)}, bf16[256,4096]{1,0:T(8,128)(2,1)}, u32[]{:S(2)}) copy-start(bf16[256,4096]{1,0:T(8,128)(2,1)} %fusion.11) | copy-start | bytes 6291460
  138.0 37.1 %copy-start.4 = (bf16[16,4096]{1,0:T(8,128)(2,1)S(1)}, bf16[16,4096]{1,0:T(8,128)(2,1)}, u32[]{:S(2)}) copy-start(bf16[16,4096]{1,0:T(8,128)(2,1)} %param.10) | copy-start | bytes 393220
  138.0 37.0 %copy-start.13 = (f32[16]{0:T(128)S(1)}, f32[16]{0:T(128)}, u32[]{:S(2)}) copy-start(f32[16]{0:T(128)} %copy-done.12) | copy-start | bytes 196
  177.2 11.9 %collective-permute-start.1 = (bf16[16,4096]{1,0:T(8,128)(2,1)}, bf16[16,4096]{1,0:T(8,128)(2,1)S(1)}, u32[]{:S(2)}, u32[]{:S(2)}) collective-permute-start(bf16[16,4096]{1,0:T(8,128)(2,1)} %fusion.14), channel_id=1, source_target_pairs={{128,0},{129,1},{130,2},{131,3},{132,4},{133,5},{134,6},{135,7},{1... | collective-permute-start | bytes 393224 | tf_op jit(solution)/shard_map/ppermute | solution.py:146
  224.7 5.4 %copy-start = (bf16[384,4096]{1,0:T(8,128)(2,1)S(1)}, bf16[384,4096]{1,0:T(8,128)(2,1)}, u32[]{:S(2)}) copy-start(bf16[384,4096]{1,0:T(8,128)(2,1)} %get-tuple-element.16) | copy-start | bytes 9437188
  224.7 5.4 %copy-start.15 = (bf16[1,1,384,4096]{3,2,1,0:T(8,128)(2,1)S(1)}, bf16[1,1,384,4096]{3,2,1,0:T(8,128)(2,1)}, u32[]{:S(2)}) copy-start(bf16[1,1,384,4096]{3,2,1,0:T(8,128)(2,1)} %param.17) | copy-start | bytes 9437188
  232.4 2.7 collective-permute-start.2
  272.4 8.4 %collective-permute-start.3 = (bf16[16,4096]{1,0:T(8,128)(2,1)S(1)}, bf16[16,4096]{1,0:T(8,128)(2,1)S(1)}, u32[]{:S(2)}, u32[]{:S(2)}) collective-permute-start(bf16[16,4096]{1,0:T(8,128)(2,1)S(1)} %add_convert_fusion.2), channel_id=1, source_target_pairs={{0,128},{1,129},{2,130},{3,131},{4,132},{5,133},{6,134},{7,135},{8... | collective-permute-start | bytes 393224 | tf_op jit(solution)/shard_map/ppermute | solution.py:146

commit v10 on v5

--- a/solution.py
+++ b/solution.py
@@ -167,9 +167,7 @@
 def replica_sum(per_replica):
     total = jnp.zeros(per_replica.shape[1:], jnp.float32)
     for replica in range(per_replica.shape[0]):
-        total = total + lax.optimization_barrier(per_replica[replica].astype(jnp.bfloat16)).astype(
-            jnp.float32
-        )
+        total = total + per_replica[replica].astype(jnp.bfloat16).astype(jnp.float32)
     return total
 
 

time: 279 us -> 287 us (1.029)
  other arithmetic: 19.3 us -> 33 us
  local copies, waits for them, and re-layouts: 39.3 us -> 35.2 us
  matrix products: 38.8 us -> 35.7 us
    convert_element_type x3 -> x0, local copies, waits for them, and re-layouts: 16.9 us -> none  [the longest x1 8.62 us: renew(): (weights.astype(jnp.float32) - rate * grads / scale).astype(jnp.bfloat16)]
    another operation x0 -> x3, local copies, waits for them, and re-layouts: none -> 10.8 us  [the longest x1 8.62 us: learn_core(): weights_gu.reshape(model_width, 2 * hidden_count)]
    reduce_sum x2, other arithmetic: 5.17 us -> 12.8 us  [renew(): jnp.mean(grads * grads, axis=axis_number, keepdims=True) + EPSILON]
    convert_element_type x1, other arithmetic: 4.96 us -> 10.5 us  [renew(): (weights.astype(jnp.float32) - rate * grads / scale).astype(jnp.bfloat16)]
    unnamed x37 -> x41, local copies, waits for them, and re-layouts: 7.4 us -> 9.95 us
  transfers between devices with their start and end apart: 4 -> 4, of which waited for: 2 -> 3; matrix products, arithmetic and copies ran while one was open for 15% -> 15% of each run, Pallas kernels for 0% -> 0%
where the time goes in v10:
time: 287 us; the launch traced here: 286 us
  Pallas kernels  165 us (57%)
  matrix products  35.7 us (12%)
  local copies, waits for them, and re-layouts  35.2 us (12%)
  other arithmetic  33 us (11%)
  waiting for transfers between devices  11.4 us (4%)
  starting transfers between devices  5.07 us (2%)
    pallas_call x4, Pallas kernels, exchange(): pl.pallas_call(functools.partial(exchange_kernel, count, width, share), o...  165 us
    reduce_sum x2, other arithmetic, renew(): jnp.mean(grads * grads, axis=axis_number, keepdims=True) + EPSILON  12.8 us
    convert_element_type x1, other arithmetic, renew(): (weights.astype(jnp.float32) - rate * grads / scale).astype(jnp.bfloat16)  10.5 us
    unnamed x41, local copies, waits for them, and re-layouts  9.95 us
    ppermute x2, waiting for transfers between devices, passed_along(): return lax.ppermute(block, axis, route)  9.06 us
    dot_general x1, local copies, waits for them, and re-layouts, learn_core(): jnp.dot(slot_rows, weights_gu.reshape(model_width, 2 * hidden_count), pre...  8.8 us
    another operation x1, local copies, waits for them, and re-layouts, learn_core(): weights_gu.reshape(model_width, 2 * hidden_count)  8.62 us
    dot_general x1, matrix products, learn_core(): jnp.einsum('pcd,pcgh->pdgh', slot_rows.reshape(rep_count, -1, model_width...  6.27 us
  transfers between devices with their start and end apart: 4, of which 3 were waited for; matrix products, arithmetic and copies ran while one was open for 15% of the time, Pallas kernels for 0%

profile of v10, /device:TPU:4, one launch (start us, length us, event | category | flops | bytes accessed | tf_op | source)
XLA Modules:
  0.0 285.9 jit_solution(13735240203447427876)
XLA Ops:
  0.0 0.7 slice.40
  0.8 0.1 eq.69
  0.9 0.1 fusion.47
  1.0 0.2 reduce_window_sum.25
  1.1 0.2 select_reduce_fusion.1
  1.3 0.1 reduce_sum.91
  1.4 0.1 copy.49
  1.5 1.3 bitcast_add_fusion
  2.9 0.1 eq.62
  2.9 0.1 fusion.48
  3.0 0.2 reduce_window_sum.24
  3.2 0.2 select_reduce_fusion.3
  3.4 0.1 reduce_sum.87
  3.5 0.1 copy.43
  3.6 0.1 copy.44
  3.6 0.7 bitcast_select_fusion
  4.4 0.8 reduce-window.8
  5.2 0.7 bitcast_subtract_fusion
  5.9 0.7 select_reduce_fusion.4
  6.7 6.6 %copy.59 = bf16[512,8,2,384]{3,1,2,0:T(8,128)(2,1)} copy(bf16[512,8,2,384]{3,2,1,0:T(2,128)(2,1)} %bitcast.125) | data formatting | bytes 12582912
  13.2 8.8 %copy.46 = bf16[768,4096]{1,0:T(8,128)(2,1)} copy(bf16[768,4096]{0,1:T(8,128)(2,1)} %bitcast.121) | data formatting | bytes 12582912 | tf_op jit(solution)/shard_map/dot_general | solution.py:195
  22.0 0.1 select_reduce_fusion.2
  22.2 1.5 convolution_convert_fusion.4.refs_0_
  23.7 2.1 convolution_convert_fusion.3.refs_1_
  25.8 65.1 %shard_map.91 = (bf16[256,4096]{1,0:T(8,128)(2,1)}, bf16[256,4096]{1,0:T(8,128)(2,1)}) custom-call(bf16[128,4096]{1,0:T(8,128)(2,1)} %convolution_convert_fusion.4.refs_0_, bf16[128,4096]{1,0:T(8,128)(2,1)} %convolution_convert_fusion.3.refs_1_), custom_call_target="tpu_custom_call" | custom-call | bytes 12582912 | tf_op jit(solution)/shard_map/pallas_call | solution.py:120
  90.9 5.4 %fusion.22 = f32[256,2,384]{2,0,1:T(8,128)S(1)} fusion(bf16[2,384,4096]{2,1,0:T(8,128)(2,1)} %bitcast.129, bf16[256,4096]{1,0:T(8,128)(2,1)} %get-tuple-element.8), kind=kOutput, calls=%fused_computation.33 | convolution fusion | flops 1610612736 | bytes 9175040 | tf_op jit(solution)/shard_map/dot_general | solution.py:195
  96.3 1.3 fusion.37
  97.7 1.8 fusion.10
  99.6 2.6 fusion.13
  102.2 2.5 constant_dynamic-slice_fusion
  104.7 0.4 collective-permute-start
  105.0 1.2 fusion.63
  106.2 1.1 copy.53
  107.3 1.1 copy.54
  108.4 6.3 %fusion.28 = bf16[2,4096,2,384]{1,3,2,0:T(8,128)(2,1)} fusion(bf16[2,128,4096,1]{2,1,3,0:T(8,128)(2,1)S(1)} %bitcast.131, bf16[2,128,1,384]{1,3,2,0:T(8,128)(2,1)S(1)} %copy.54, bf16[2,128,1,384]{1,3,2,0:T(8,128)(2,1)S(1)} %copy.53), kind=kOutput, calls=%fused_computation.42 | convolution fusion | flops 1611399168 | bytes 15073280 | tf_op jit(solution)/shard_map/pcd,pcgh->pdgh/dot_general | solution.py:217
  114.7 11.7 %multiply_reduce_fusion = (f32[2,384]{1,0:T(2,128)S(1)}, f32[1,4096,2,384]{1,3,2,0:T(8,128)}) fusion(bf16[2,4096,2,384]{1,3,2,0:T(8,128)(2,1)} %fusion.28), kind=kLoop, calls=%fused_computation.5 | loop fusion | flops 18873600 | bytes 25168896 | tf_op jit(solution)/shard_map/reduce_sum | solution.py:175
  126.4 8.6 %copy.52 = bf16[4096,768]{0,1:T(8,128)(2,1)} copy(bf16[4096,768]{1,0:T(8,128)(2,1)} %bitcast.122) | data formatting | bytes 12582912 | tf_op jit(solution)/shard_map/reshape;squeeze | solution.py:197
  135.0 0.2 copy.56
  135.2 0.2 copy.57
  135.4 10.5 %fusion.1 = bf16[4096,768]{0,1:T(8,128)(2,1)} fusion(f32[1,4096,2,384]{1,3,2,0:T(8,128)} %get-tuple-element.14, bf16[4096,768]{0,1:T(8,128)(2,1)} %copy.52, f32[768]{0:T(1024)S(1)} %sqrt.20), kind=kLoop, calls=%fused_computation.4 | loop fusion | flops 12582912 | bytes 25168896 | tf_op jit(solution)/shard_map/convert_element_type | solution.py:176
  145.8 1.8 fusion.41
  147.7 2.7 copy-done
  150.3 1.1 multiply_reduce_fusion.1
  151.4 0.5 copy-done.2
  151.9 2.5 add_convert_fusion.1.refs_0_
  154.4 33.0 %shard_map.92 = bf16[128,4096]{1,0:T(8,128)(2,1)} custom-call(bf16[128,4096]{1,0:T(8,128)(2,1)} %add_convert_fusion.1.refs_0_), custom_call_target="tpu_custom_call" | custom-call | bytes 4194304 | tf_op jit(solution)/shard_map/pallas_call | solution.py:120
  187.4 1.8 fusion.14
  189.1 3.0 %collective-permute-start.1 = (bf16[16,4096]{1,0:T(8,128)(2,1)S(1)}, bf16[16,4096]{1,0:T(8,128)(2,1)S(1)}, u32[]{:S(2)}, u32[]{:S(2)}) collective-permute-start(bf16[16,4096]{1,0:T(8,128)(2,1)S(1)} %fusion.14), channel_id=1, source_target_pairs={{128,0},{129,1},{130,2},{131,3},{132,4},{133,5},{134,6},{135,7},{1... | collective-permute-start | bytes 393224 | tf_op jit(solution)/shard_map/ppermute | solution.py:146
  192.3 0.1 convert_reduce_fusion
  192.4 2.0 collective-permute-done.1
  194.4 1.5 convolution_convert_fusion.2.refs_0_
  195.9 33.7 %shard_map.93 = bf16[256,4096]{1,0:T(8,128)(2,1)} custom-call(bf16[128,4096]{1,0:T(8,128)(2,1)} %convolution_convert_fusion.2.refs_0_), custom_call_target="tpu_custom_call" | custom-call | bytes 6291456 | tf_op jit(solution)/shard_map/pallas_call | solution.py:120
  229.6 5.4 %fusion.20 = f32[256,2,384]{2,0,1:T(8,128)S(1)} fusion(bf16[2,384,4096]{2,1,0:T(8,128)(2,1)} %bitcast.130, bf16[256,4096]{1,0:T(8,128)(2,1)} %shard_map.93), kind=kOutput, calls=%fused_computation.31 | convolution fusion | flops 1610612736 | bytes 9175040 | tf_op jit(solution)/shard_map/dot_general | solution.py:181
  235.0 0.2 copy-done.15
  235.2 2.5 convolution_convert_fusion
  237.7 0.1 constant_dynamic-slice_fusion.1
  237.8 0.4 collective-permute-start.2
  238.2 2.3 collective-permute-done.2
  240.5 1.2 add_convert_fusion.refs_0_
  241.8 33.3 %shard_map.94 = bf16[128,4096]{1,0:T(8,128)(2,1)} custom-call(bf16[128,4096]{1,0:T(8,128)(2,1)} %add_convert_fusion.refs_0_), custom_call_target="tpu_custom_call" | custom-call | bytes 4194304 | tf_op jit(solution)/shard_map/pallas_call | solution.py:120
  275.1 1.7 add_convert_fusion.2
  276.9 1.3 collective-permute-start.3
  278.2 7.1 %collective-permute-done.3 = bf16[16,4096]{1,0:T(8,128)(2,1)S(1)} collective-permute-done((bf16[16,4096]{1,0:T(8,128)(2,1)S(1)}, bf16[16,4096]{1,0:T(8,128)(2,1)S(1)}, u32[]{:S(2)}, u32[]{:S(2)}) %collective-permute-start.3) | collective-permute-done | bytes 131104 | tf_op jit(solution)/shard_map/ppermute | solution.py:146
  285.2 0.7 select_bitcast_fusion
  (52 shorter events, 0.5 us)
Async XLA Ops:
  6.6 17.0 %copy-start.12 = (f32[16]{0:T(128)}, f32[16]{0:T(128)S(1)}, u32[]{:S(2)}) copy-start(f32[16]{0:T(128)S(1)} %add_divide_fusion) | copy-start | bytes 196
  13.2 8.9 %copy-start.6 = (bf16[1,16,4096]{2,1,0:T(8,128)(2,1)S(1)}, bf16[1,16,4096]{2,1,0:T(8,128)(2,1)}, u32[]{:S(2)}) copy-start(bf16[1,16,4096]{2,1,0:T(8,128)(2,1)} %param.9) | copy-start | bytes 393220
  13.2 10.5 %copy-start.7 = (bf16[16,4096]{1,0:T(8,128)(2,1)S(1)}, bf16[16,4096]{1,0:T(8,128)(2,1)}, u32[]{:S(2)}) copy-start(bf16[16,4096]{1,0:T(8,128)(2,1)} %param.10) | copy-start | bytes 393220
  25.8 71.9 %slice-start.2 = ((s8[6291456]{0:T(1024)(128)(4,1)}), s8[2097152]{0:T(1024)(128)(4,1)S(1)}, s32[]{:S(2)}) async-start(s8[6291456]{0:T(1024)(128)(4,1)} %bitcast.126), calls=%async_computation.2 | async-start | bytes 4194304
  90.8 5.5 %copy-start.3 = (bf16[256,4096]{1,0:T(8,128)(2,1)S(1)}, bf16[256,4096]{1,0:T(8,128)(2,1)}, u32[]{:S(2)}) copy-start(bf16[256,4096]{1,0:T(8,128)(2,1)} %get-tuple-element.7) | copy-start | bytes 6291460
  90.8 5.5 %copy-start.14 = (bf16[1,1,384,4096]{3,2,1,0:T(8,128)(2,1)S(1)}, bf16[1,1,384,4096]{3,2,1,0:T(8,128)(2,1)}, u32[]{:S(2)}) copy-start(bf16[1,1,384,4096]{3,2,1,0:T(8,128)(2,1)} %param.17) | copy-start | bytes 9437188
  90.9 6.8 %slice-start.3 = ((s8[6291456]{0:T(1024)(128)(4,1)}), s8[4194304]{0:T(1024)(128)(4,1)S(1)}, s32[]{:S(2)}) async-start(s8[6291456]{0:T(1024)(128)(4,1)} %bitcast.126), calls=%async_computation.3 | async-start | bytes 8388608
  96.3 3.3 %copy-start.5 = (f32[256,2,384]{2,0,1:T(8,128)}, f32[256,2,384]{2,0,1:T(8,128)S(1)}, u32[]{:S(2)}) copy-start(f32[256,2,384]{2,0,1:T(8,128)S(1)} %fusion.22) | copy-start | bytes 2359300
  97.7 1.9 copy-start.8
  97.7 1.9 copy-start.9
  102.2 6.2 %copy-start.1 = (bf16[256,4096]{1,0:T(8,128)(2,1)S(1)}, bf16[256,4096]{1,0:T(8,128)(2,1)}, u32[]{:S(2)}) copy-start(bf16[256,4096]{1,0:T(8,128)(2,1)} %get-tuple-element.8) | copy-start | bytes 6291460
  104.7 46.8 %collective-permute-start = (bf16[128,4096]{1,0:T(8,128)(2,1)}, bf16[128,4096]{1,0:T(8,128)(2,1)}, u32[]{:S(2)}, u32[]{:S(2)}) collective-permute-start(bf16[128,4096]{1,0:T(8,128)(2,1)} %constant_dynamic-slice_fusion), channel_id=1, source_target_pairs={{0,1},{1,0},{2,3},{3,2},{4,5},{5,4},{6,7},{7,6},{8,9},{9,8},{10,11... | collective-permute-start | bytes 3145736 | tf_op jit(solution)/shard_map/ppermute | solution.py:257
  135.4 10.5 %copy-start.11 = (f32[2,16,8]{1,2,0:T(8,128)S(1)}, f32[2,16,8]{1,2,0:T(8,128)}, u32[]{:S(2)}) copy-start(f32[2,16,8]{1,2,0:T(8,128)} %param.15) | copy-start | bytes 3076
  135.4 10.5 %copy-start.4 = (bf16[256,4096]{1,0:T(8,128)(2,1)S(1)}, bf16[256,4096]{1,0:T(8,128)(2,1)}, u32[]{:S(2)}) copy-start(bf16[256,4096]{1,0:T(8,128)(2,1)} %get-tuple-element.7) | copy-start | bytes 6291460
  147.7 2.7 copy-start
  150.3 1.6 copy-start.2
  151.4 36.0 %copy-start.13 = (f32[16]{0:T(128)S(1)}, f32[16]{0:T(128)}, u32[]{:S(2)}) copy-start(f32[16]{0:T(128)} %copy-done.12) | copy-start | bytes 196
  151.4 40.7 %copy-start.10 = (s32[16,8]{0,1:T(8,128)S(1)}, s32[16,8]{0,1:T(8,128)}, u32[]{:S(2)}) copy-start(s32[16,8]{0,1:T(8,128)} %get-tuple-element.19) | copy-start | bytes 1540
  189.1 5.3 %collective-permute-start.1 = (bf16[16,4096]{1,0:T(8,128)(2,1)S(1)}, bf16[16,4096]{1,0:T(8,128)(2,1)S(1)}, u32[]{:S(2)}, u32[]{:S(2)}) collective-permute-start(bf16[16,4096]{1,0:T(8,128)(2,1)S(1)} %fusion.14), channel_id=1, source_target_pairs={{128,0},{129,1},{130,2},{131,3},{132,4},{133,5},{134,6},{135,7},{1... | collective-permute-start | bytes 393224 | tf_op jit(solution)/shard_map/ppermute | solution.py:146
  195.9 39.1 %slice-start = ((s8[6291456]{0:T(1024)(128)(4,1)}), s8[2097152]{0:T(1024)(128)(4,1)S(1)}, s32[]{:S(2)}) async-start(s8[6291456]{0:T(1024)(128)(4,1)} %bitcast.123), calls=%async_computation | async-start | bytes 4194304
  229.6 5.4 %slice-start.1 = ((s8[6291456]{0:T(1024)(128)(4,1)}), s8[4194304]{0:T(1024)(128)(4,1)S(1)}, s32[]{:S(2)}) async-start(s8[6291456]{0:T(1024)(128)(4,1)} %bitcast.123), calls=%async_computation.1 | async-start | bytes 8388608
  229.6 5.6 %copy-start.15 = (bf16[1,1,384,4096]{3,2,1,0:T(8,128)(2,1)S(1)}, bf16[1,1,384,4096]{3,2,1,0:T(8,128)(2,1)}, u32[]{:S(2)}) copy-start(bf16[1,1,384,4096]{3,2,1,0:T(8,128)(2,1)} %param.17) | copy-start | bytes 9437188
  237.8 2.7 collective-permute-start.2
  276.9 8.4 %collective-permute-start.3 = (bf16[16,4096]{1,0:T(8,128)(2,1)S(1)}, bf16[16,4096]{1,0:T(8,128)(2,1)S(1)}, u32[]{:S(2)}, u32[]{:S(2)}) collective-permute-start(bf16[16,4096]{1,0:T(8,128)(2,1)S(1)} %add_convert_fusion.2), channel_id=1, source_target_pairs={{0,128},{1,129},{2,130},{3,131},{4,132},{5,133},{6,134},{7,135},{8... | collective-permute-start | bytes 393224 | tf_op jit(solution)/shard_map/ppermute | solution.py:146
